TPU v7x, 128 devices: a whole 4x4x4 slice. The times are simulated.
128 devices in a mesh: face: 8 (over x, z_hi), tile: 16 (over z_lo, y, core).
Axes of the slice: x: 4, y: 4, z: 4 (z_hi: 2, z_lo: 2; z = z_hi * 2 + z_lo), core: 2. Of those that a mesh axis runs over, the one named last changes fastest.
Arguments:
- state_field: bfloat16 [4, 512, 1024, 256], P(None, 'face', 'tile'), may hold values from -6 to 6
- cotangent: bfloat16 [4, 512, 1024, 256], P(None, 'face', 'tile'), may hold values from -6 to 6
- depth_weight: float32 [9, 256], replicated, may hold values from -2 to 2
- depth_bias: float32 [256], replicated, may hold values from -3 to 3
- point_weight: bfloat16 [256, 256], replicated, may hold values from -0.375 to 0.375
- tile_links: int32 [128, 4], P(('face', 'tile')), may hold values from 0 to 127, as said below
- link_sides: int32 [128, 4], P(('face', 'tile')), may hold values from 0 to 3
- link_flips: int32 [128, 4], P(('face', 'tile')), may hold values from 0 to 1
- corner_masks: int32 [128, 4], P(('face', 'tile')), may hold values 0 or 1
Outputs:
- field_grad: bfloat16 [4, 512, 1024, 256], P(None, 'face', 'tile')
- depth_grad: float32 [9, 256], replicated
- bias_grad: float32 [256], replicated
- point_grad: float32 [256, 256], replicated
Inputs may be any that keep to these rules, and one draw needn't show every extreme that they name: Tile ids number the grid row by row, the row being the index along face. The four neighbours of a tile are the four tiles one step away along face or along tile with wrap-around, each exactly once. Links are mutual: if tile_links[a, s] = b and link_sides[a, s] = o then tile_links[b, o] = a, link_sides[b, o] = s and link_flips[b, o] = link_flips[a, s].
All inputs are finite; a program needn't handle non-finite values. No bound on the sum of `corner_masks` on one device may be relied on, other than what follows from the above.
Results may differ from a plain program's by a relative error of at most 0.0049.
Values may be sent and summed in bfloat16 or wider, within the bound.
No kernel may reach another device: no remote copies, remote signals or barrier semaphores. Data moves between devices by JAX's collectives and lax.ppermute only.
A program may use at most 192 MiB of HBM per device.

v0:
```python
import jax
import jax.numpy as jnp
from jax import lax
from jax.sharding import PartitionSpec as P

root_two_pi = 0.7978845608028654
cubic_coef = 0.044715


def with_halo(block, sides, width):
    for axis, dim in sides:
        count = lax.axis_size(axis)
        forward = [(i, i + 1) for i in range(count - 1)]
        forward.append((count - 1, 0))
        backward = [(target, source) for source, target in forward]
        low = lax.ppermute(
            lax.slice_in_dim(block, block.shape[dim] - width, None, axis=dim), axis, forward
        )
        high = lax.ppermute(lax.slice_in_dim(block, 0, width, axis=dim), axis, backward)
        block = jnp.concatenate([low, block, high], axis=dim)
    return block


def gelu_pair(hidden):
    inside = root_two_pi * (hidden + cubic_coef * hidden * hidden * hidden)
    tanh_val = jnp.tanh(inside)
    output = 0.5 * hidden * (1.0 + tanh_val)
    slope = 0.5 * (1.0 + tanh_val) + 0.5 * hidden * (1.0 - tanh_val * tanh_val) * root_two_pi * (
        1.0 + 3.0 * cubic_coef * hidden * hidden
    )
    return (output, slope)


def edge_rows(block):
    return jnp.stack([block[:, 0], block[:, :, -1], block[:, -1], block[:, :, 0]], axis=0)


def split_dirs(per_dir):
    return (
        jnp.stack([per_dir[0], per_dir[2]], axis=0),
        jnp.stack([per_dir[3], per_dir[1]], axis=0),
    )


def join_dirs(got_face, got_tile):
    return jnp.stack([got_face[0], got_tile[3], got_face[3], got_tile[0]], axis=0)


def padded_tile(block, rim_rows, cmask):
    rim32 = rim_rows.astype(jnp.float32)
    north_west = (cmask[0] * 0.5 * (rim32[0][:, 0] + rim32[3][:, 0])).astype(jnp.bfloat16)
    north_east = (cmask[1] * 0.5 * (rim32[0][:, -1] + rim32[1][:, 0])).astype(jnp.bfloat16)
    south_east = (cmask[2] * 0.5 * (rim32[1][:, -1] + rim32[2][:, -1])).astype(jnp.bfloat16)
    south_west = (cmask[3] * 0.5 * (rim32[2][:, 0] + rim32[3][:, -1])).astype(jnp.bfloat16)
    top_row = jnp.concatenate([north_west[:, None], rim_rows[0], north_east[:, None]], axis=1)
    low_row = jnp.concatenate([south_west[:, None], rim_rows[2], south_east[:, None]], axis=1)
    middle = jnp.concatenate([rim_rows[3][:, :, None], block, rim_rows[1][:, :, None]], axis=2)
    return jnp.concatenate([top_row[:, None], middle, low_row[:, None]], axis=1)


def rim_terms(tap_rows, ext_rows):
    inner_rows = ext_rows[:, :, 1:-1].astype(jnp.float32)
    zero_rows = jnp.zeros_like(inner_rows[:, :, :1])
    padded_rows = jnp.concatenate([zero_rows, inner_rows, zero_rows], axis=2)
    tap_first = tap_rows[:, 0][:, None, None, :]
    tap_middle = tap_rows[:, 1][:, None, None, :]
    tap_last = tap_rows[:, 2][:, None, None, :]
    result = (
        tap_first * padded_rows[:, :, 2:]
        + tap_middle * padded_rows[:, :, 1:-1]
        + tap_last * padded_rows[:, :, :-2]
    )
    result = result.at[:, :, 0].add(
        0.5 * tap_first[:, :, 0] * ext_rows[:, :, 0].astype(jnp.float32)
    )
    result = result.at[:, :, -1].add(
        0.5 * tap_last[:, :, 0] * ext_rows[:, :, -1].astype(jnp.float32)
    )
    return result


def shards(
    state_field,
    cotangent,
    depth_weight,
    depth_bias,
    point_weight,
    tile_links,
    link_sides,
    link_flips,
    corner_masks,
):
    batch_size, tile_side, unused_side, channels = state_field.shape
    face_count = lax.axis_size("face")
    tile_count = lax.axis_size("tile")
    face_pos = lax.axis_index("face")
    tile_pos = lax.axis_index("tile")
    toward = jnp.stack(
        [
            (face_pos - 1) % face_count * tile_count + tile_pos,
            face_pos * tile_count + (tile_pos + 1) % tile_count,
            (face_pos + 1) % face_count * tile_count + tile_pos,
            face_pos * tile_count + (tile_pos - 1) % tile_count,
        ]
    )
    matched = tile_links[0][:, None] == toward[None, :]
    counter = jnp.arange(4, dtype=jnp.int32)
    dir_of_side = jnp.sum(jnp.where(matched, counter[None, :], 0), axis=1)
    side_of_dir = jnp.sum(jnp.where(matched, counter[:, None], 0), axis=0)
    flip_side = (link_flips[0] == 1)[:, None, None, None]
    cmask = corner_masks[0].astype(jnp.float32)
    sending = jnp.take(edge_rows(state_field), side_of_dir, axis=0)
    along_face, along_tile = split_dirs(sending)
    got_face = with_halo(along_face, (("face", 0),), 1)
    got_tile = with_halo(along_tile, (("tile", 0),), 1)
    rim_rows = jnp.take(join_dirs(got_face, got_tile), dir_of_side, axis=0)
    rim_rows = jnp.where(flip_side, rim_rows[:, :, ::-1], rim_rows)
    padded = padded_tile(state_field, rim_rows, cmask)
    tap_table = depth_weight.reshape(3, 3, channels)
    hidden = jnp.zeros(state_field.shape, jnp.float32) + depth_bias
    for row_off in range(3):
        for col_off in range(3):
            hidden = hidden + tap_table[row_off, col_off] * padded[
                :, row_off : row_off + tile_side, col_off : col_off + tile_side
            ].astype(jnp.float32)
    output, slope = gelu_pair(hidden)
    act = output.astype(jnp.bfloat16)
    row_count = batch_size * tile_side * tile_side
    cot_rows = cotangent.reshape(row_count, channels)
    grad_act = lax.dot_general(
        cot_rows, point_weight, (((1,), (1,)), ((), ())), preferred_element_type=jnp.float32
    )
    grad_hidden = (grad_act.reshape(hidden.shape) * slope).astype(jnp.bfloat16)
    point_part = lax.dot_general(
        act.reshape(row_count, channels),
        cot_rows,
        (((0,), (0,)), ((), ())),
        preferred_element_type=jnp.float32,
    )
    grad32 = grad_hidden.astype(jnp.float32)
    depth_list = []
    for row_off in range(3):
        for col_off in range(3):
            window = padded[:, row_off : row_off + tile_side, col_off : col_off + tile_side].astype(
                jnp.float32
            )
            depth_list.append(jnp.sum(grad32 * window, axis=(0, 1, 2)))
    depth_part = jnp.stack(depth_list, axis=0)
    bias_part = jnp.sum(grad32, axis=(0, 1, 2))
    point_sum, depth_sum, bias_sum = lax.psum((point_part, depth_part, bias_part), ("face", "tile"))
    norm_scale = float(batch_size * tile_side * tile_side * face_count * tile_count) ** (-0.5)
    grad_padded = jnp.pad(grad32, ((0, 0), (1, 1), (1, 1), (0, 0)))
    inner_grad = jnp.zeros(state_field.shape, jnp.float32)
    for row_off in range(3):
        for col_off in range(3):
            inner_grad = (
                inner_grad
                + tap_table[row_off, col_off]
                * grad_padded[
                    :, 2 - row_off : 2 - row_off + tile_side, 2 - col_off : 2 - col_off + tile_side
                ]
            )
    side_taps = jnp.stack([tap_table[0], tap_table[:, 2], tap_table[2], tap_table[:, 0]], axis=0)
    low_corner = jnp.array([0, 1, 3, 0], dtype=jnp.int32)
    high_corner = jnp.array([1, 2, 2, 3], dtype=jnp.int32)
    mask_low = jnp.take(corner_masks[0], low_corner).astype(jnp.bfloat16)[:, None, None, None]
    mask_high = jnp.take(corner_masks[0], high_corner).astype(jnp.bfloat16)[:, None, None, None]
    hidden_edges = edge_rows(grad_hidden)
    ext_rows = jnp.concatenate(
        [hidden_edges[:, :, :1] * mask_low, hidden_edges, hidden_edges[:, :, -1:] * mask_high],
        axis=2,
    )
    rim_parts = rim_terms(side_taps, ext_rows)
    outgoing = jnp.take(rim_parts, side_of_dir, axis=0)
    part_face, part_tile = split_dirs(outgoing)
    back_face = with_halo(part_face.astype(jnp.bfloat16), (("face", 0),), 1).astype(part_face.dtype)
    back_tile = with_halo(part_tile.astype(jnp.bfloat16), (("tile", 0),), 1).astype(part_tile.dtype)
    incoming = jnp.take(join_dirs(back_face, back_tile), dir_of_side, axis=0)
    incoming = jnp.where(flip_side, incoming[:, :, ::-1], incoming)
    inner_grad = (
        inner_grad.at[:, 0]
        .add(incoming[0])
        .at[:, :, -1]
        .add(incoming[1])
        .at[:, -1]
        .add(incoming[2])
        .at[:, :, 0]
        .add(incoming[3])
    )
    field_grad = inner_grad.astype(jnp.bfloat16)
    return (field_grad, depth_sum * norm_scale, bias_sum * norm_scale, point_sum * norm_scale)


def solution(mesh):
    in_specs = (
        P(None, "face", "tile", None),
        P(None, "face", "tile", None),
        P(),
        P(),
        P(),
        P(("face", "tile"), None),
        P(("face", "tile"), None),
        P(("face", "tile"), None),
        P(("face", "tile"), None),
    )
    out_specs = (P(None, "face", "tile", None), P(), P(), P())
    return jax.shard_map(shards, mesh=mesh, in_specs=in_specs, out_specs=out_specs, check_vma=False)
```

profile of v0, /device:TPU:1, one launch (start us, length us, event | category | flops | bytes accessed | tf_op | source)
XLA Modules:
  0.0 391.2 jit_solution(6158489630904382677)
XLA Ops:
  8.3 1.0 slice_bitcast_fusion.18
  9.3 11.6 %copy.60 = bf16[4,64,64,256]{3,1,0,2:T(8,128)(2,1)} copy(bf16[4,64,64,256]{3,2,1,0:T(8,128)(2,1)} %param.29) | data formatting | bytes 16777216 | tf_op args[0]
  20.8 1.0 slice_bitcast_fusion.16
  22.7 4.5 %collective-permute-start = (bf16[1,4,64,256]{3,2,1,0:T(8,128)(2,1)S(1)}, bf16[1,4,64,256]{3,2,1,0:T(8,128)(2,1)S(1)}, u32[]{:S(2)}, u32[]{:S(2)}) collective-permute-start(bf16[1,4,64,256]{3,2,1,0:T(8,128)(2,1)S(1)} %get-tuple-element.148), channel_id=1, source_target_pairs={{0,16},{16,32},{32,48},{48,64},{64,80},{80,96},{96,112},{112,0},{1... | collective-permute-start | bytes 393224 | tf_op jit(solution)/shard_map/ppermute | solution.py:16
  27.2 2.1 collective-permute-start.3
  29.3 2.0 collective-permute-start.2
  36.2 1.3 collective-permute-done.2
  39.6 16.4 %maximum_maximum_fusion = (bf16[4,65,66,256]{3,1,0,2:T(8,128)(2,1)S(1)}, bf16[4,65,66,256]{3,1,0,2:T(8,128)(2,1)}) fusion(bf16[4,64,1,256]{3,1,0,2:T(8,128)(2,1)S(1)} %get-tuple-element.145, bf16[4,64,64,256]{3,1,0,2:T(8,128)(2,1)} %copy.60, bf16[4,64,1,256]{3,1,0,2:T(8,128)(2,1)S(1)} %get-tuple-element.146, bf16[4,1,66,256]{3,1,0,2:T(2,128)(2,1)S(1)} %copy.64, ...), kind=kLoop, calls=%fused_computation.78 | loop fusion | flops 70287360 | bytes 26492928 | tf_op jit(solution)/shard_map/concatenate | solution.py:58
  56.0 35.1 %multiply_convert_fusion = (bf16[4,64,64,256]{3,1,0,2:T(8,128)(2,1)}, f32[4,64,64,256]{3,1,0,2:T(8,128)}) fusion(bf16[4,65,66,256]{3,1,0,2:T(8,128)(2,1)} %get-tuple-element.119, f32[256]{0:T(256)S(1)} %bitcast.133, f32[256]{0:T(256)S(1)} %bitcast.135, f32[256]{0:T(256)S(1)} %bitcast.137, bf16[4,64,1,256]{3,1,0,2:T(8,128)(2,1)S(1)} %get-tuple-element.145, ...), kind=kLoop, calls=%fused_computation.77 | loop fusion | flops 159383552 | bytes 84158464 | tf_op jit(solution)/shard_map/convert_element_type | solution.py:127
  91.1 16.0 %fusion.29 = f32[4,64,64,256]{3,1,0,2:T(8,128)} fusion(f32[4,64,64,256]{3,1,0,2:T(8,128)} %get-tuple-element.111), kind=kLoop, calls=%fused_computation.65 | loop fusion | flops 71303168 | bytes 33554432 | tf_op jit(solution)/shard_map/add | solution.py:28
  107.1 25.4 %fusion.39 = bf16[4,64,64,256]{3,2,1,0:T(8,128)(2,1)} fusion(f32[4,64,64,256]{3,1,0,2:T(8,128)} %fusion.29, bf16[4,64,64,256]{3,2,1,0:T(8,128)(2,1)} %param.30, bf16[256,256]{1,0:T(8,128)(2,1)S(1)} %copy-done), kind=kOutput, calls=%fused_computation.76 | convolution fusion | flops 2155872256 | bytes 33685504 | tf_op jit(solution)/shard_map/dot_general | solution.py:130
  132.5 35.5 %fusion.38 = (f32[256]{0:T(256)S(1)}, f32[256]{0:T(256)S(1)}, f32[256]{0:T(256)S(1)}, f32[256]{0:T(256)S(1)}, f32[256]{0:T(256)S(1)}, /*index=5*/f32[256]{0:T(25...) fusion(bf16[4,65,66,256]{3,1,0,2:T(8,128)(2,1)} %get-tuple-element.119, ...), kind=kLoop, calls=%fused_computation.74 | loop fusion | flops 130020864 | bytes 75769856 | tf_op jit(solution)/shard_map/reduce_sum | solution.py:147
  168.1 1.4 slice.591
  169.4 1.0 slice_bitcast_fusion.10
  170.4 12.5 %fusion.78 = (bf16[4,64,64,256]{3,1,0,2:T(8,128)(2,1)}, f32[4,64,64,256]{3,1,0,2:T(8,128)}) fusion(bf16[4,64,64,256]{3,2,1,0:T(8,128)(2,1)} %fusion.39), kind=kLoop, calls=%fused_computation.198 | loop fusion | flops 4194304 | bytes 33554432 | tf_op jit(solution)/shard_map/convert_element_type | solution.py:133
  182.9 15.5 %fusion.43 = f32[256,256]{1,0:T(8,128)} fusion(bf16[4,64,64,256]{3,2,1,0:T(8,128)(2,1)} %param.30, bf16[4,64,64,256]{3,1,0,2:T(8,128)(2,1)} %get-tuple-element.110), kind=kOutput, calls=%fused_computation.87 | convolution fusion | flops 2147483648 | bytes 17039360 | tf_op jit(solution)/shard_map/dot_general | solution.py:134
  198.5 65.7 %all-reduce.3 = (f32[9,256]{1,0:T(8,128)S(1)}, f32[256]{0:T(256)S(1)}) all-reduce(f32[9,256]{1,0:T(8,128)S(1)} %stack.83, f32[256]{0:T(256)S(1)} %get-tuple-element.99), channel_id=1, replica_groups=mesh['face'=8,'tile'=16] {'face','tile'}, use_global_device_ids=true, to_apply=%region_11.15 | all-reduce | flops 2560 | bytes 20480 | tf_op jit(solution)/shard_map/psum | solution.py:150
  264.9 0.9 slice_bitcast_fusion.9
  267.5 1.4 collective-permute-start.4
  268.9 1.0 collective-permute-start.7
  270.6 3.8 collective-permute-start.5
  274.4 51.6 %fusion.8 = f32[4,64,64,256]{3,1,0,2:T(8,128)} fusion(f32[4,64,64,256]{3,1,0,2:T(8,128)} %get-tuple-element.123, f32[256]{0:T(256)S(1)} %bitcast.134, f32[256]{0:T(256)S(1)} %bitcast.136, f32[256]{0:T(256)S(1)} %bitcast.138, f32[256]{0:T(256)S(1)} %bitcast.140, f32[256]{0:T(256)S(1)} %bitcast.142, f32[256]{0:T(256)S(1)} %bitcast.144, f32[256]{0:T(256)S(1)} %bitcast.146, ...), kind=kLoop, calls=%fused_computation.44 | loop fusion | flops 75497472 | bytes 41952256 | tf_op jit(solution)/shard_map/add | solution.py:157
  326.5 12.8 %all-reduce.6.cloned.1.call-done = f32[256,256]{1,0:T(8,128)} async-done(((f32[256,256]{1,0:T(8,128)}), f32[256,256]{1,0:T(8,128)}) %all-reduce.6.cloned.1.call-update) | async-done | bytes 262160 | tf_op jit(solution)/shard_map/psum | solution.py:150
  339.3 1.7 broadcast_multiply_fusion
  342.4 1.9 slice_add_fusion.1
  344.3 6.9 %scatter-add.24 = f32[4,64,64,256]{3,1,0,2:T(8,128)} dynamic-update-slice(f32[4,64,64,256]{3,1,0,2:T(8,128)} %fusion.8, f32[4,1,64,256]{3,1,0,2:T(1,128)S(1)} %slice_add_fusion.1, s32[]{:T(128)} %constant.237.clone.1, s32[]{:T(128)} %constant.237.clone.1, s32[]{:T(128)} %constant.237.clone.1, s32[]{:T(128)} %constant.237.clone.1) | dynamic-update-slice | bytes 524292 | tf_op jit(solution)/shard_map/scatter-add | solution.py:182
  351.2 1.7 fusion.55
  352.9 2.0 slice_add_fusion
  354.9 6.9 %scatter-add.26 = f32[4,64,64,256]{3,1,0,2:T(8,128)} dynamic-update-slice(f32[4,64,64,256]{3,1,0,2:T(8,128)} %fusion.55, f32[4,1,64,256]{3,1,0,2:T(1,128)S(1)} %slice_add_fusion, s32[]{:T(128)} %constant.237.clone.1, s32[]{:T(128)} %constant.249.clone.1, s32[]{:T(128)} %constant.237.clone.1, s32[]{:T(128)} %constant.237.clone.1) | dynamic-update-slice | bytes 524292 | tf_op jit(solution)/shard_map/scatter-add | solution.py:186
  361.8 1.7 fusion.53
  363.5 9.1 %convert_element_type.121 = bf16[4,64,64,256]{3,1,0,2:T(8,128)(2,1)} convert(f32[4,64,64,256]{3,1,0,2:T(8,128)} %fusion.53) | non-fusion elementwise | flops 4194304 | bytes 25165824 | tf_op jit(solution)/shard_map/convert_element_type | solution.py:190
  372.5 11.6 %copy.80 = bf16[4,64,64,256]{3,2,1,0:T(8,128)(2,1)} copy(bf16[4,64,64,256]{3,1,0,2:T(8,128)(2,1)} %convert_element_type.121) | data formatting | bytes 16777216
  (93 shorter events, 11.0 us)
Async XLA Ops:
  7.2 100.0 %copy-start = (bf16[256,256]{1,0:T(8,128)(2,1)S(1)}, bf16[256,256]{1,0:T(8,128)(2,1)}, u32[]{:S(2)}) copy-start(bf16[256,256]{1,0:T(8,128)(2,1)} %param.33) | copy-start | bytes 393220
  7.2 25.0 %copy-start.7 = (s32[4]{0:T(128)S(1)}, s32[4]{0:T(128)}, u32[]{:S(2)}) copy-start(s32[4]{0:T(128)} %constant.280) | copy-start | bytes 52
  7.2 25.0 %copy-start.6 = (s32[4]{0:T(128)S(1)}, s32[4]{0:T(128)}, u32[]{:S(2)}) copy-start(s32[4]{0:T(128)} %constant.281) | copy-start | bytes 52
  7.2 24.3 %copy-start.4 = (f32[9,256]{1,0:T(8,128)S(1)}, f32[9,256]{1,0:T(8,128)}, u32[]{:S(2)}) copy-start(f32[9,256]{1,0:T(8,128)} %param.31) | copy-start | bytes 27652
  7.2 24.3 %copy-start.8 = (s32[1,4]{1,0:T(1,128)S(1)}, s32[1,4]{1,0:T(1,128)}, u32[]{:S(2)}) copy-start(s32[1,4]{1,0:T(1,128)} %param.35) | copy-start | bytes 52
  7.2 24.3 %copy-start.2 = (s32[1,4]{1,0:T(1,128)S(1)}, s32[1,4]{1,0:T(1,128)}, u32[]{:S(2)}) copy-start(s32[1,4]{1,0:T(1,128)} %param.36) | copy-start | bytes 52
  7.2 332.0 %all-reduce.6.cloned.1.call-start = ((), (), s32[]{:S(2)}) async-start(), calls=%async_computation | async-start | bytes 524288 | tf_op jit(solution)/shard_map/psum | solution.py:150
  22.7 13.5 %collective-permute-start = (bf16[1,4,64,256]{3,2,1,0:T(8,128)(2,1)S(1)}, bf16[1,4,64,256]{3,2,1,0:T(8,128)(2,1)S(1)}, u32[]{:S(2)}, u32[]{:S(2)}) collective-permute-start(bf16[1,4,64,256]{3,2,1,0:T(8,128)(2,1)S(1)} %get-tuple-element.148), channel_id=1, source_target_pairs={{0,16},{16,32},{32,48},{48,64},{64,80},{80,96},{96,112},{112,0},{1... | collective-permute-start | bytes 393224 | tf_op jit(solution)/shard_map/ppermute | solution.py:16
  27.2 9.0 %collective-permute-start.3 = (bf16[1,4,64,256]{3,2,1,0:T(8,128)(2,1)S(1)}, bf16[1,4,64,256]{3,2,1,0:T(8,128)(2,1)S(1)}, u32[]{:S(2)}, u32[]{:S(2)}) collective-permute-start(bf16[1,4,64,256]{3,2,1,0:T(8,128)(2,1)S(1)} %get-tuple-element.149), channel_id=1, source_target_pairs={{0,1},{1,2},{2,3},{3,4},{4,5},{5,6},{6,7},{7,8},{8,9},{9,10},{10,1... | collective-permute-start | bytes 393224 | tf_op jit(solution)/shard_map/ppermute | solution.py:16
  29.3 8.2 %collective-permute-start.2 = (bf16[1,4,64,256]{3,2,1,0:T(8,128)(2,1)S(1)}, bf16[1,4,64,256]{3,2,1,0:T(8,128)(2,1)S(1)}, u32[]{:S(2)}, u32[]{:S(2)}) collective-permute-start(bf16[1,4,64,256]{3,2,1,0:T(8,128)(2,1)S(1)} %get-tuple-element.150), channel_id=1, source_target_pairs={{16,0},{32,16},{48,32},{64,48},{80,64},{96,80},{112,96},{0,112},{1... | collective-permute-start | bytes 393224 | tf_op jit(solution)/shard_map/ppermute | solution.py:19
  31.3 6.2 %collective-permute-start.1 = (bf16[1,4,64,256]{3,2,1,0:T(8,128)(2,1)S(1)}, bf16[1,4,64,256]{3,2,1,0:T(8,128)(2,1)S(1)}, u32[]{:S(2)}, u32[]{:S(2)}) collective-permute-start(bf16[1,4,64,256]{3,2,1,0:T(8,128)(2,1)S(1)} %get-tuple-element.151), channel_id=1, source_target_pairs={{1,0},{2,1},{3,2},{4,3},{5,4},{6,5},{7,6},{8,7},{9,8},{10,9},{11,1... | collective-permute-start | bytes 393224 | tf_op jit(solution)/shard_map/ppermute | solution.py:19
  38.9 17.2 %copy-start.5 = (f32[256]{0:T(256)S(1)}, f32[256]{0:T(256)}, u32[]{:S(2)}) copy-start(f32[256]{0:T(256)} %param.32) | copy-start | bytes 3076
  56.0 35.1 %copy-start.3 = (bf16[4,65,66,256]{3,1,0,2:T(8,128)(2,1)}, bf16[4,65,66,256]{3,1,0,2:T(8,128)(2,1)S(1)}, u32[]{:S(2)}) copy-start(bf16[4,65,66,256]{3,1,0,2:T(8,128)(2,1)S(1)} %get-tuple-element.118) | copy-start | bytes 26357764
  267.5 73.5 %collective-permute-start.4 = (bf16[1,4,64,256]{3,2,1,0:T(8,128)(2,1)S(1)}, bf16[1,4,64,256]{3,2,1,0:T(8,128)(2,1)S(1)}, u32[]{:S(2)}, u32[]{:S(2)}) collective-permute-start(bf16[1,4,64,256]{3,2,1,0:T(8,128)(2,1)S(1)} %get-tuple-element.138), channel_id=1, source_target_pairs={{0,16},{16,32},{32,48},{48,64},{64,80},{80,96},{96,112},{112,0},{1... | collective-permute-start | bytes 393224 | tf_op jit(solution)/shard_map/ppermute | solution.py:16
  268.9 72.1 %collective-permute-start.7 = (bf16[1,4,64,256]{3,2,1,0:T(8,128)(2,1)S(1)}, bf16[1,4,64,256]{3,2,1,0:T(8,128)(2,1)S(1)}, u32[]{:S(2)}, u32[]{:S(2)}) collective-permute-start(bf16[1,4,64,256]{3,2,1,0:T(8,128)(2,1)S(1)} %get-tuple-element.139), channel_id=1, source_target_pairs={{1,0},{2,1},{3,2},{4,3},{5,4},{6,5},{7,6},{8,7},{9,8},{10,9},{11,1... | collective-permute-start | bytes 393224 | tf_op jit(solution)/shard_map/ppermute | solution.py:19
  269.9 71.1 %collective-permute-start.6 = (bf16[1,4,64,256]{3,2,1,0:T(8,128)(2,1)S(1)}, bf16[1,4,64,256]{3,2,1,0:T(8,128)(2,1)S(1)}, u32[]{:S(2)}, u32[]{:S(2)}) collective-permute-start(bf16[1,4,64,256]{3,2,1,0:T(8,128)(2,1)S(1)} %get-tuple-element.140), channel_id=1, source_target_pairs={{0,1},{1,2},{2,3},{3,4},{4,5},{5,6},{6,7},{7,8},{8,9},{9,10},{10,1... | collective-permute-start | bytes 393224 | tf_op jit(solution)/shard_map/ppermute | solution.py:16
  270.6 70.4 %collective-permute-start.5 = (bf16[1,4,64,256]{3,2,1,0:T(8,128)(2,1)S(1)}, bf16[1,4,64,256]{3,2,1,0:T(8,128)(2,1)S(1)}, u32[]{:S(2)}, u32[]{:S(2)}) collective-permute-start(bf16[1,4,64,256]{3,2,1,0:T(8,128)(2,1)S(1)} %get-tuple-element.141), channel_id=1, source_target_pairs={{16,0},{32,16},{48,32},{64,48},{80,64},{96,80},{112,96},{0,112},{1... | collective-permute-start | bytes 393224 | tf_op jit(solution)/shard_map/ppermute | solution.py:19
  361.8 22.4 %copy-start.1 = (bf16[256,256]{1,0:T(8,128)(2,1)S(1)}, bf16[256,256]{1,0:T(8,128)(2,1)}, u32[]{:S(2)}) copy-start(bf16[256,256]{1,0:T(8,128)(2,1)} %param.33) | copy-start | bytes 393220
Sparse Core Ops, SparseCore 0:
  198.6 140.6 all-reduce.5
where the time goes:
time: 398 us; the launch traced here: 391 us
  other arithmetic  189 us (47%)
  blocking collectives  65.7 us (17%)
  local copies, waits for them, and re-layouts  48 us (12%)
  matrix products  40.9 us (10%)
  between operations  17.4 us (4%)
  starting transfers between devices  15.7 us (4%)
  waiting for transfers between devices  14.1 us (4%)
    psum x1, blocking collectives, shards(): lax.psum((point_part, depth_part, bias_part), ('face', 'tile'))  65.7 us
    add x1, other arithmetic, shards(): inner_grad + tap_table[row_off, col_off] * grad_padded[:, 2 - row_off:2 -...  51.6 us
    reduce_sum x1, other arithmetic, shards(): depth_list.append(jnp.sum(grad32 * window, axis=(0, 1, 2)))  35.5 us
    convert_element_type x1, other arithmetic, shards(): act = output.astype(jnp.bfloat16)  35.1 us
    dot_general x1, matrix products, shards(): lax.dot_general(cot_rows, point_weight, (((1,), (1,)), ((), ())), preferr...  25.4 us
    unnamed x26, local copies, waits for them, and re-layouts  23.3 us
    concatenate x1, other arithmetic, padded_tile(): return jnp.concatenate([top_row[:, None], middle, low_row[:, None]], axis=1)  16.4 us
    add x1, other arithmetic, gelu_pair(): 0.5 * (1.0 + tanh_val)  16 us
  transfers between devices with their start and end apart: 9, of which 2 were waited for; matrix products, arithmetic and copies ran while one was open for 15% of the time, Pallas kernels for 0%

commit v1 on v0

v1 whole, which is shorter than its diff:
```python
import functools

import jax
import jax.numpy as jnp
from jax import lax
from jax.experimental import pallas as pl
from jax.experimental.pallas import tpu as pltpu
from jax.sharding import PartitionSpec as P

ROOT = 0.7978845608028654
CUBIC = 0.044715
F32 = jnp.float32
BF16 = jnp.bfloat16
LANES = 128
SUB = 8
PAD = 8


def gelu_pair(h):
    h2 = h * h
    s = 0.5 * jnp.tanh(h * ((CUBIC * ROOT) * h2 + ROOT)) + 0.5
    act = h * s
    slope = s + act * (1.0 - s) * ((6.0 * CUBIC * ROOT) * h2 + 2.0 * ROOT)
    return act, slope


def inner_body(rows_at_once, x_ref, cot_ref, w_ref, tap_ref, bias_ref, gh_ref, pg_ref, dg_ref, xf, ga, act, acc):
    step = pl.program_id(0)
    side = x_ref.shape[1]
    cols = x_ref.shape[2]

    @pl.when(step == 0)
    def _():
        edge = jnp.zeros((side, PAD, LANES), F32)
        for hf in range(2):
            xf[hf, :, 0:PAD, :] = edge
            xf[hf, :, PAD + cols : 2 * PAD + cols, :] = edge
        act[0] = jnp.zeros(act.shape[1:], BF16)
        act[side - 1] = jnp.zeros(act.shape[1:], BF16)
        acc[...] = jnp.zeros_like(acc)
        pg_ref[...] = jnp.zeros_like(pg_ref)

    gh_ref[0, 0] = jnp.zeros(gh_ref.shape[2:], BF16)
    gh_ref[0, side - 1] = jnp.zeros(gh_ref.shape[2:], BF16)

    def widen(i, _):
        v = x_ref[0, i].astype(F32)
        xf[0, i, PAD : PAD + cols, :] = v[:, :LANES]
        xf[1, i, PAD : PAD + cols, :] = v[:, LANES:]
        return 0

    lax.fori_loop(0, side, widen, 0, unroll=4)
    w = w_ref[...]

    def back_rows(k, _):
        c = cot_ref[0, pl.ds(k * 8, 8)].reshape(8 * cols, 2 * LANES)
        g = lax.dot_general(c, w, (((1,), (1,)), ((), ())), preferred_element_type=F32)
        g = g.reshape(8, cols, 2 * LANES)
        ga[0, pl.ds(k * 8, 8)] = g[:, :, :LANES]
        ga[1, pl.ds(k * 8, 8)] = g[:, :, LANES:]
        return 0

    lax.fori_loop(0, side // 8, back_rows, 0)
    row = lax.broadcasted_iota(jnp.int32, (SUB, LANES), 0)
    inner = side - 2
    for hf in range(2):
        lanes = slice(hf * LANES, hf * LANES + LANES)
        for jb in range(cols // 16):

            def body(it, carry, count, base):
                i = base + it * count
                accs = list(carry)
                win = {}
                for q in range(count):
                    pair = []
                    for part in range(2):
                        j = PAD + jb * 16 + part * SUB
                        for r in range(3):
                            for c in range(3):
                                if (q + r, c, part) not in win:
                                    win[q + r, c, part] = xf[hf, i - 1 + q + r, j - 1 + c : j - 1 + c + SUB, :]
                        h = bias_ref[hf]
                        for r in range(3):
                            for c in range(3):
                                h = h + tap_ref[hf, 3 * r + c] * win[q + r, c, part]
                        a, slope = gelu_pair(h)
                        g = ga[hf, i + q, jb * 16 + part * SUB : jb * 16 + part * SUB + SUB, :] * slope
                        if jb == 0 and part == 0:
                            g = jnp.where(row > 0, g, 0.0)
                            a = jnp.where(row > 0, a, 0.0)
                        if jb == cols // 16 - 1 and part == 1:
                            g = jnp.where(row < SUB - 1, g, 0.0)
                            a = jnp.where(row < SUB - 1, a, 0.0)
                        pair.append((a, g))
                        for r in range(3):
                            for c in range(3):
                                accs[3 * r + c] = accs[3 * r + c] + g * win[q + r, c, part]
                        accs[9] = accs[9] + g
                    act[i + q, jb * 16 : jb * 16 + 16, lanes] = jnp.concatenate(
                        [pair[0][0], pair[1][0]], axis=0
                    ).astype(BF16)
                    gh_ref[0, i + q, jb * 16 : jb * 16 + 16, lanes] = jnp.concatenate(
                        [pair[0][1], pair[1][1]], axis=0
                    ).astype(BF16)
                return tuple(accs)

            out = tuple(acc[hf, k] for k in range(10))
            trips = inner // rows_at_once
            out = lax.fori_loop(0, trips, functools.partial(body, count=rows_at_once, base=1), out)
            if inner % rows_at_once:
                out = body(0, out, inner % rows_at_once, 1 + trips * rows_at_once)
            for k in range(10):
                acc[hf, k] = out[k]

    def outer_rows(k, _):
        a = act[pl.ds(k * 16, 16)].reshape(16 * cols, 2 * LANES)
        c = cot_ref[0, pl.ds(k * 16, 16)].reshape(16 * cols, 2 * LANES)
        pg_ref[...] += lax.dot_general(a, c, (((0,), (0,)), ((), ())), preferred_element_type=F32)
        return 0

    lax.fori_loop(0, side // 16, outer_rows, 0)

    @pl.when(step == pl.num_programs(0) - 1)
    def _():
        dg_ref[...] = acc[...]


def inner_call(state, cotangent, weight, taps, bias):
    batch, side, cols, channels = state.shape
    tile = pl.BlockSpec((1, side, cols, channels), lambda b: (b, 0, 0, 0))
    return pl.pallas_call(
        functools.partial(inner_body, 4),
        grid=(batch,),
        in_specs=[
            tile,
            tile,
            pl.BlockSpec((channels, channels), lambda b: (0, 0)),
            pl.BlockSpec((2, 9, SUB, LANES), lambda b: (0, 0, 0, 0)),
            pl.BlockSpec((2, SUB, LANES), lambda b: (0, 0, 0)),
        ],
        out_specs=[
            tile,
            pl.BlockSpec((channels, channels), lambda b: (0, 0)),
            pl.BlockSpec((2, 10, SUB, LANES), lambda b: (0, 0, 0, 0)),
        ],
        out_shape=[
            jax.ShapeDtypeStruct(state.shape, BF16),
            jax.ShapeDtypeStruct((channels, channels), F32),
            jax.ShapeDtypeStruct((2, 10, SUB, LANES), F32),
        ],
        scratch_shapes=[
            pltpu.VMEM((2, side, cols + 2 * PAD, LANES), F32),
            pltpu.VMEM((2, side, cols, LANES), F32),
            pltpu.VMEM((side, cols, channels), BF16),
            pltpu.VMEM((2, 10, SUB, LANES), F32),
        ],
        compiler_params=pltpu.CompilerParams(vmem_limit_bytes=56 << 20),
        cost_estimate=pl.CostEstimate(
            flops=40_000_000_000, bytes_accessed=26 << 20, transcendentals=state.size
        ),
        name="inner",
    )(state, cotangent, weight, taps, bias)


LOW = (0, 1, 3, 0)
HIGH = (1, 2, 2, 3)


def ring_body(
    mask_ref, top_ref, low_ref, left_ref, right_ref, ctop_ref, clow_ref, cleft_ref, cright_ref,
    rim_ref, w_ref, tap_ref, bias_ref, gr_ref, rg_ref, pg_ref, dg_ref, strip, ext, acts, acc,
):
    step = pl.program_id(0)
    side = rim_ref.shape[2]

    @pl.when(step == 0)
    def _():
        acc[...] = jnp.zeros_like(acc)
        pg_ref[...] = jnp.zeros_like(pg_ref)
        ext[...] = jnp.zeros_like(ext)

    rims = [rim_ref[s, 0].astype(F32) for s in range(4)]
    top = top_ref[0].astype(F32)
    low = low_ref[0].astype(F32)
    left = left_ref[0].astype(F32)
    right = right_ref[0].astype(F32)
    last = left.shape[1] - 1
    end = side - 1

    def corner(k, first, second):
        return (mask_ref[k] * 0.5 * (first + second)).astype(BF16).astype(F32)

    def at(s, i):
        return rims[s][i : i + 1]

    nw = corner(0, at(0, 0), at(3, 0))
    ne = corner(1, at(0, end), at(1, 0))
    se = corner(2, at(1, end), at(2, end))
    sw = corner(3, at(2, 0), at(3, end))
    lines = (
        ((rims[0], nw, ne), (top[0], at(3, 0), at(1, 0)), (top[1], at(3, 1), at(1, 1))),
        (
            (right[:, last - 1], at(0, end - 1), at(2, end - 1)),
            (right[:, last], at(0, end), at(2, end)),
            (rims[1], ne, se),
        ),
        (
            (low[0], at(3, end - 1), at(1, end - 1)),
            (low[1], at(3, end), at(1, end)),
            (rims[2], sw, se),
        ),
        ((rims[3], nw, sw), (left[:, 0], at(0, 0), at(2, 0)), (left[:, 1], at(0, 1), at(2, 1))),
    )
    for s in range(4):
        for a in range(3):
            line, before, after = lines[s][a]
            for hf in range(2):
                lanes = slice(hf * LANES, hf * LANES + LANES)
                strip[s, hf, a, PAD : PAD + side, :] = line[:, lanes]
                strip[s, hf, a, PAD - 1 : PAD, :] = before[:, lanes]
                strip[s, hf, a, PAD + side : PAD + side + 1, :] = after[:, lanes]
    cots = jnp.concatenate(
        [
            ctop_ref[0, 0].astype(F32),
            cright_ref[0].astype(F32)[:, last],
            clow_ref[0, 0].astype(F32),
            cleft_ref[0].astype(F32)[:, 0],
        ],
        axis=0,
    ).astype(BF16)
    ga = lax.dot_general(cots, w_ref[...], (((1,), (1,)), ((), ())), preferred_element_type=F32)
    row = lax.broadcasted_iota(jnp.int32, (side, LANES), 0)
    middle = jnp.logical_and(row > 0, row < end)
    for s in range(4):
        upright = s % 2 == 0
        rim_line = 0 if s in (0, 3) else 2
        for hf in range(2):
            lanes = slice(hf * LANES, hf * LANES + LANES)

            def tap(a, b):
                k = 3 * a + b if upright else 3 * b + a
                return k, tap_ref[hf, k, 0:1, :]

            h = jnp.zeros((side, LANES), F32) + bias_ref[hf, 0:1, :]
            for a in range(3):
                for b in range(3):
                    h = h + tap(a, b)[1] * strip[s, hf, a, PAD - 1 + b : PAD - 1 + b + side, :]
            act, slope = gelu_pair(h)
            g = (ga[s * side : s * side + side, lanes] * slope).astype(BF16)
            gr_ref[s, 0, :, lanes] = g
            g = g.astype(F32)
            counted = g
            if not upright:
                counted = jnp.where(middle, g, 0.0)
                act = jnp.where(middle, act, 0.0)
            acts[s * side : s * side + side, lanes] = act.astype(BF16)
            for a in range(3):
                for b in range(3):
                    k = tap(a, b)[0]
                    term = counted * strip[s, hf, a, PAD - 1 + b : PAD - 1 + b + side, :]
                    acc[hf, k] += jnp.sum(term.reshape(side // SUB, SUB, LANES), axis=0)
            acc[hf, 9] += jnp.sum(counted.reshape(side // SUB, SUB, LANES), axis=0)
            ext[PAD : PAD + side, :] = g
            first, mid, final = (tap(rim_line, b)[1] for b in range(3))
            back = (
                first * ext[PAD + 1 : PAD + 1 + side, :]
                + mid * g
                + final * ext[PAD - 1 : PAD - 1 + side, :]
            )
            back = back + jnp.where(row == 0, (0.5 * mask_ref[LOW[s]]) * first * g, 0.0)
            back = back + jnp.where(row == end, (0.5 * mask_ref[HIGH[s]]) * final * g, 0.0)
            rg_ref[s, 0, :, lanes] = back.astype(BF16)
    pg_ref[...] += lax.dot_general(acts[...], cots, (((0,), (0,)), ((), ())), preferred_element_type=F32)

    @pl.when(step == pl.num_programs(0) - 1)
    def _():
        dg_ref[...] = acc[...]


def ring_call(mask, state, cotangent, rims, weight, taps, bias):
    batch, side, cols, channels = state.shape
    wide = 16
    two = lambda at: pl.BlockSpec((1, 2, cols, channels), lambda b: (b, at, 0, 0))
    one = lambda at: pl.BlockSpec((1, 1, cols, channels), lambda b: (b, at, 0, 0))
    column = lambda at: pl.BlockSpec((1, side, wide, channels), lambda b: (b, 0, at, 0))
    strips = pl.BlockSpec((4, 1, side, channels), lambda b: (0, b, 0, 0))
    far = cols // wide - 1
    return pl.pallas_call(
        ring_body,
        grid=(batch,),
        in_specs=[
            pl.BlockSpec(memory_space=pltpu.SMEM),
            two(0),
            two(side // 2 - 1),
            column(0),
            column(far),
            one(0),
            one(side - 1),
            column(0),
            column(far),
            strips,
            pl.BlockSpec((channels, channels), lambda b: (0, 0)),
            pl.BlockSpec((2, 9, SUB, LANES), lambda b: (0, 0, 0, 0)),
            pl.BlockSpec((2, SUB, LANES), lambda b: (0, 0, 0)),
        ],
        out_specs=[
            strips,
            strips,
            pl.BlockSpec((channels, channels), lambda b: (0, 0)),
            pl.BlockSpec((2, 10, SUB, LANES), lambda b: (0, 0, 0, 0)),
        ],
        out_shape=[
            jax.ShapeDtypeStruct((4, batch, side, channels), BF16),
            jax.ShapeDtypeStruct((4, batch, side, channels), BF16),
            jax.ShapeDtypeStruct((channels, channels), F32),
            jax.ShapeDtypeStruct((2, 10, SUB, LANES), F32),
        ],
        scratch_shapes=[
            pltpu.VMEM((4, 2, 3, cols + 2 * PAD, LANES), F32),
            pltpu.VMEM((cols + 2 * PAD, LANES), F32),
            pltpu.VMEM((4 * side, channels), BF16),
            pltpu.VMEM((2, 10, SUB, LANES), F32),
        ],
        compiler_params=pltpu.CompilerParams(vmem_limit_bytes=40 << 20),
        cost_estimate=pl.CostEstimate(
            flops=3_000_000_000, bytes_accessed=12 << 20, transcendentals=state.size // 16
        ),
        name="ring",
    )(mask, state, state, state, state, cotangent, cotangent, cotangent, cotangent, rims, weight, taps, bias)


def spread_body(rows_at_once, gh_ref, gr_ref, in_ref, tap_ref, out_ref, gf, near, far):
    side = gh_ref.shape[1]
    cols = gh_ref.shape[2]
    for hf in range(2):
        gf[hf, 0] = jnp.zeros(gf.shape[2:], F32)
        gf[hf, side + 1] = jnp.zeros(gf.shape[2:], F32)
        gf[hf, :, 0:PAD, :] = jnp.zeros((side + 2, PAD, LANES), F32)
        gf[hf, :, PAD + cols : 2 * PAD + cols, :] = jnp.zeros((side + 2, PAD, LANES), F32)
    near[...] = jnp.zeros_like(near)
    far[...] = jnp.zeros_like(far)

    def widen(i, _):
        v = gh_ref[0, i].astype(F32)
        gf[0, i + 1, PAD : PAD + cols, :] = v[:, :LANES]
        gf[1, i + 1, PAD : PAD + cols, :] = v[:, LANES:]
        return 0

    lax.fori_loop(1, side - 1, widen, 0)
    ring = [gr_ref[s, 0].astype(F32) for s in range(4)]
    back = [in_ref[s, 0].astype(F32) for s in (1, 3)]
    for hf in range(2):
        lanes = slice(hf * LANES, hf * LANES + LANES)
        gf[hf, 1 : side + 1, PAD : PAD + 1, :] = ring[3][:, lanes].reshape(side, 1, LANES)
        gf[hf, 1 : side + 1, PAD + cols - 1 : PAD + cols, :] = ring[1][:, lanes].reshape(side, 1, LANES)
        gf[hf, 1, PAD : PAD + cols, :] = ring[0][:, lanes]
        gf[hf, side, PAD : PAD + cols, :] = ring[2][:, lanes]
        near[hf, :, 0:1, :] = back[1][:, lanes].reshape(side, 1, LANES)
        far[hf, :, SUB - 1 : SUB, :] = back[0][:, lanes].reshape(side, 1, LANES)
    for hf in range(2):
        lanes = slice(hf * LANES, hf * LANES + LANES)
        for jb in range(cols // 16):

            def body(it, carry):
                i = it * rows_at_once
                win = {}
                for q in range(rows_at_once):
                    pair = []
                    for part in range(2):
                        j = PAD + jb * 16 + part * SUB
                        total = None
                        for r in range(3):
                            for c in range(3):
                                at = (q + 2 - r, 2 - c, part)
                                if at not in win:
                                    win[at] = gf[hf, i + at[0], j - 1 + at[1] : j - 1 + at[1] + SUB, :]
                                term = tap_ref[hf, 3 * r + c] * win[at]
                                total = term if total is None else total + term
                        if jb == 0 and part == 0:
                            total = total + near[hf, i + q]
                        if jb == cols // 16 - 1 and part == 1:
                            total = total + far[hf, i + q]
                        pair.append(total)
                    out_ref[0, i + q, jb * 16 : jb * 16 + 16, lanes] = jnp.concatenate(pair, axis=0).astype(BF16)
                return carry

            lax.fori_loop(0, side // rows_at_once, body, 0)
    for at, s in ((0, 0), (side - 1, 2)):
        out_ref[0, at] = (out_ref[0, at].astype(F32) + in_ref[s, 0].astype(F32)).astype(BF16)


def spread_call(grad, ring, incoming, taps):
    batch, side, cols, channels = grad.shape
    tile = pl.BlockSpec((1, side, cols, channels), lambda b: (b, 0, 0, 0))
    strips = pl.BlockSpec((4, 1, side, channels), lambda b: (0, b, 0, 0))
    return pl.pallas_call(
        functools.partial(spread_body, 4),
        grid=(batch,),
        in_specs=[tile, strips, strips, pl.BlockSpec((2, 9, SUB, LANES), lambda b: (0, 0, 0, 0))],
        out_specs=tile,
        out_shape=jax.ShapeDtypeStruct(grad.shape, BF16),
        scratch_shapes=[
            pltpu.VMEM((2, side + 2, cols + 2 * PAD, LANES), F32),
            pltpu.VMEM((2, side, SUB, LANES), F32),
            pltpu.VMEM((2, side, SUB, LANES), F32),
        ],
        compiler_params=pltpu.CompilerParams(vmem_limit_bytes=40 << 20),
        cost_estimate=pl.CostEstimate(flops=15_000_000_000, bytes_accessed=17 << 20, transcendentals=0),
        name="spread",
    )(grad, ring, incoming, taps)


def exchange(by_side, side_of_dir, dir_of_side, flips):
    facing = jnp.take(by_side, side_of_dir, axis=0)
    turned = jnp.take(flips, side_of_dir, axis=0)[:, None, None, None] == 1
    facing = jnp.where(turned, facing[:, :, ::-1], facing)
    got = [None] * 4
    for axis, low, high in (("face", 0, 2), ("tile", 3, 1)):
        count = lax.axis_size(axis)
        up = [(i, (i + 1) % count) for i in range(count)]
        down = [(target, source) for source, target in up]
        got[low] = lax.ppermute(facing[high], axis, up)
        got[high] = lax.ppermute(facing[low], axis, down)
    return jnp.take(jnp.stack(got, axis=0), dir_of_side, axis=0)


def all_sum(part):
    for axis in ("tile", "face"):
        count = lax.axis_size(axis)
        bit = 1
        while bit < count:
            part = part + lax.ppermute(part, axis, [(i, i ^ bit) for i in range(count)])
            bit *= 2
    return part


def shards(
    state, cotangent, depth_weight, depth_bias, point_weight, tile_links, link_sides, link_flips, corner_masks
):
    batch, side, cols, channels = state.shape
    face_count = lax.axis_size("face")
    tile_count = lax.axis_size("tile")
    face_pos = lax.axis_index("face")
    tile_pos = lax.axis_index("tile")
    toward = jnp.stack(
        [
            (face_pos - 1) % face_count * tile_count + tile_pos,
            face_pos * tile_count + (tile_pos + 1) % tile_count,
            (face_pos + 1) % face_count * tile_count + tile_pos,
            face_pos * tile_count + (tile_pos - 1) % tile_count,
        ]
    )
    matched = tile_links[0][:, None] == toward[None, :]
    counter = jnp.arange(4, dtype=jnp.int32)
    dir_of_side = jnp.sum(jnp.where(matched, counter[None, :], 0), axis=1)
    side_of_dir = jnp.sum(jnp.where(matched, counter[:, None], 0), axis=0)
    flips = link_flips[0]
    mask = corner_masks[0].astype(F32)

    taps = jnp.broadcast_to(
        depth_weight.reshape(9, 2, 1, LANES).transpose(1, 0, 2, 3), (2, 9, SUB, LANES)
    )
    bias = jnp.broadcast_to(depth_bias.reshape(2, 1, LANES), (2, SUB, LANES))

    edges = jnp.stack([state[:, 0], state[:, :, -1], state[:, -1], state[:, :, 0]], axis=0)
    rims = exchange(edges, side_of_dir, dir_of_side, flips)
    grad, point_inner, depth_inner = inner_call(state, cotangent, point_weight, taps, bias)
    ring, rim_grads, point_ring, depth_ring = ring_call(
        mask, state, cotangent, rims, point_weight, taps, bias
    )
    incoming = exchange(rim_grads, side_of_dir, dir_of_side, flips)
    field_grad = spread_call(grad, ring, incoming, taps)

    depth_part = jnp.sum(depth_inner + depth_ring, axis=2).transpose(1, 0, 2).reshape(10, channels)
    part = jnp.concatenate(
        [point_inner + point_ring, depth_part, jnp.zeros((6, channels), F32)], axis=0
    )
    total = all_sum(part) * float(batch * side * cols * face_count * tile_count) ** -0.5
    return field_grad, total[channels : channels + 9], total[channels + 9], total[:channels]


def solution(mesh):
    tiles = P(None, "face", "tile", None)
    table = P(("face", "tile"), None)
    return jax.shard_map(
        shards,
        mesh=mesh,
        in_specs=(tiles, tiles, P(), P(), P(), table, table, table, table),
        out_specs=(tiles, P(), P(), P()),
        check_vma=False,
    )
```

time: 398 us -> 160 us (0.40)
  the two profiles are of different devices: /device:TPU:1 before, /device:TPU:32 now
where the time goes in v1:
time: 160 us
  Pallas kernels  80 us (50%)
  waiting for transfers between devices  37.6 us (24%)
  starting transfers between devices  22.1 us (14%)
  local copies, waits for them, and re-layouts  16.8 us (10%)
  other arithmetic  2.37 us (1%)
    pallas_call x1, Pallas kernels, inner_call(): pl.pallas_call(functools.partial(inner_body, 4), grid=(batch,), in_specs=...  55.2 us
    ppermute x7, waiting for transfers between devices, all_sum(): part = part + lax.ppermute(part, axis, [(i, i ^ bit) for i in range(count)])  36.6 us
    pallas_call x1, Pallas kernels, spread_call(): pl.pallas_call(functools.partial(spread_body, 4), grid=(batch,), in_specs...  18.9 us
    ppermute x7, starting transfers between devices, all_sum(): part = part + lax.ppermute(part, axis, [(i, i ^ bit) for i in range(count)])  8.5 us
    ppermute x4, starting transfers between devices, exchange(): got[high] = lax.ppermute(facing[low], axis, down)  6.84 us
    unnamed x24, local copies, waits for them, and re-layouts  6.81 us
    ppermute x4, starting transfers between devices, exchange(): got[low] = lax.ppermute(facing[high], axis, up)  6.71 us
    pallas_call x1, Pallas kernels, ring_call(): pl.pallas_call(ring_body, grid=(batch,), in_specs=[pl.BlockSpec(memory_sp...  5.92 us
  transfers between devices with their start and end apart: 15, of which 7 were waited for; matrix products, arithmetic and copies ran while one was open for 2% of the time, Pallas kernels for 46%

profile of v1, /device:TPU:32, one launch (start us, length us, event | category | flops | bytes accessed | tf_op | source)
XLA Modules:
  0.0 160.0 jit_solution(6920455227294610633)
XLA Ops:
  0.7 2.0 %fusion.2 = (bf16[4,64,1,256]{3,2,1,0:T(2,128)(2,1)S(1)}, bf16[4,64,1,256]{3,2,1,0:T(2,128)(2,1)S(1)}) fusion(bf16[4,64,64,256]{3,2,1,0:T(8,128)(2,1)} %right_ref.1), kind=kLoop, calls=%fused_computation.43 | loop fusion | bytes 524288 | tf_op jit(solution)/shard_map/slice | solution.py:465
  2.7 1.0 slice_bitcast_fusion.9
  3.8 0.8 fusion.1
  4.8 0.6 gather_fusion.1
  5.4 0.6 gather_fusion
  6.7 3.0 %collective-permute-start = (bf16[4,64,256]{2,1,0:T(8,128)(2,1)S(1)}, bf16[4,64,256]{2,1,0:T(8,128)(2,1)S(1)}, u32[]{:S(2)}, u32[]{:S(2)}) collective-permute-start(bf16[4,64,256]{2,1,0:T(8,128)(2,1)S(1)} %get-tuple-element.32), channel_id=1, source_target_pairs={{0,16},{16,32},{32,48},{48,64},{64,80},{80,96},{96,112},{112,0},{1... | collective-permute-start | bytes 393224 | tf_op jit(solution)/shard_map/ppermute | solution.py:422
  9.8 2.6 %collective-permute-start.1 = (bf16[4,64,256]{2,1,0:T(8,128)(2,1)S(1)}, bf16[4,64,256]{2,1,0:T(8,128)(2,1)S(1)}, u32[]{:S(2)}, u32[]{:S(2)}) collective-permute-start(bf16[4,64,256]{2,1,0:T(8,128)(2,1)S(1)} %get-tuple-element.35), channel_id=1, source_target_pairs={{1,0},{2,1},{3,2},{4,3},{5,4},{6,5},{7,6},{8,7},{9,8},{10,9},{11,1... | collective-permute-start | bytes 393224 | tf_op jit(solution)/shard_map/ppermute | solution.py:423
  12.4 2.0 %collective-permute-start.2 = (bf16[4,64,256]{2,1,0:T(8,128)(2,1)S(1)}, bf16[4,64,256]{2,1,0:T(8,128)(2,1)S(1)}, u32[]{:S(2)}, u32[]{:S(2)}) collective-permute-start(bf16[4,64,256]{2,1,0:T(8,128)(2,1)S(1)} %get-tuple-element.34), channel_id=1, source_target_pairs={{16,0},{32,16},{48,32},{64,48},{80,64},{96,80},{112,96},{0,112},{1... | collective-permute-start | bytes 393224 | tf_op jit(solution)/shard_map/ppermute | solution.py:423
  14.4 0.6 broadcast_in_dim.68.tap_ref
  15.0 0.6 broadcast_in_dim.70.bias_ref
  15.6 55.2 %inner.1 = (bf16[4,64,64,256]{3,2,1,0:T(8,128)(2,1)}, f32[256,256]{1,0:T(8,128)}, f32[2,10,8,128]{3,2,1,0:T(8,128)}) custom-call(bf16[4,64,64,256]{3,2,1,0:T(8,128)(2,1)} %right_ref.1, bf16[4,64,64,256]{3,2,1,0:T(8,128)(2,1)} %cright_ref.1, bf16[256,256]{1,0:T(8,128)(2,1)} %w_ref.3, f32[2,9,8,128]{3,2,1,0:T(8,128)} %broadcast_in_dim.68.tap_ref, ...), custom_call_target="tpu_custom_call" | custom-call | flops 40000000000 | bytes 27262976 | tf_op jit(solution)/shard_map/inner/pallas_call | solution.py:131
  71.1 0.6 gather_fusion.2
  71.9 3.4 %copy-done.1 = bf16[4,64,64,256]{3,2,1,0:T(8,128)(2,1)S(1)} copy-done((bf16[4,64,64,256]{3,2,1,0:T(8,128)(2,1)S(1)}, bf16[4,64,64,256]{3,2,1,0:T(8,128)(2,1)}, u32[]{:S(2)}) %copy-start.1) | copy-done | bytes 8388632
  75.2 5.9 %ring.1 = (bf16[4,4,64,256]{3,2,1,0:T(8,128)(2,1)S(1)}, bf16[4,4,64,256]{3,2,1,0:T(8,128)(2,1)S(1)}, f32[256,256]{1,0:T(8,128)S(1)}, f32[2,10,8,128]{3,2,1,0:T(8,128)S(1)}) custom-call(f32[4]{0:T(128)S(1)} %convert_bitcast_fusion.mask_ref, bf16[4,64,64,256]{3,2,1,0:T(8,128)(2,1)S(1)} %copy-done.1, bf16[4,64,64,256]{3,2,1,0:T(8,128)(2,1)S(1)} %copy-done.1, ...), custom_call_target="tpu_custom_call" | custom-call | flops 3000000000 | bytes 12582912 | tf_op jit(solution)/shard_map/ring/pallas_call | solution.py:288
  81.5 1.5 collective-permute-done.8
  83.2 1.1 collective-permute-start.9
  84.2 7.7 %collective-permute-done.9 = f32[272,256]{1,0:T(8,128)S(1)} collective-permute-done((f32[272,256]{1,0:T(8,128)S(1)}, f32[272,256]{1,0:T(8,128)S(1)}, u32[]{:S(2)}, u32[]{:S(2)}) %collective-permute-start.9) | collective-permute-done | bytes 278560 | tf_op jit(solution)/shard_map/ppermute | solution.py:432
  92.0 4.8 %collective-permute-start.10 = (f32[272,256]{1,0:T(8,128)S(1)}, f32[272,256]{1,0:T(8,128)S(1)}, u32[]{:S(2)}, u32[]{:S(2)}) collective-permute-start(f32[272,256]{1,0:T(8,128)S(1)} %add.79), channel_id=1, source_target_pairs={{0,4},{1,5},{2,6},{3,7},{4,0},{5,1},{6,2},{7,3},{8,12},{9,13},{10,... | collective-permute-start | bytes 835592 | tf_op jit(solution)/shard_map/ppermute | solution.py:432
  96.8 0.6 gather_fusion.3
  97.4 6.0 %collective-permute-done.10 = f32[272,256]{1,0:T(8,128)S(1)} collective-permute-done((f32[272,256]{1,0:T(8,128)S(1)}, f32[272,256]{1,0:T(8,128)S(1)}, u32[]{:S(2)}, u32[]{:S(2)}) %collective-permute-start.10) | collective-permute-done | bytes 278560 | tf_op jit(solution)/shard_map/ppermute | solution.py:432
  104.5 6.8 %collective-permute-done.11 = f32[272,256]{1,0:T(8,128)S(1)} collective-permute-done((f32[272,256]{1,0:T(8,128)S(1)}, f32[272,256]{1,0:T(8,128)S(1)}, u32[]{:S(2)}, u32[]{:S(2)}) %collective-permute-start.11) | collective-permute-done | bytes 278560 | tf_op jit(solution)/shard_map/ppermute | solution.py:432
  111.5 3.6 %collective-permute-start.4 = (bf16[4,64,256]{2,1,0:T(8,128)(2,1)S(1)}, bf16[4,64,256]{2,1,0:T(8,128)(2,1)S(1)}, u32[]{:S(2)}, u32[]{:S(2)}) collective-permute-start(bf16[4,64,256]{2,1,0:T(8,128)(2,1)S(1)} %get-tuple-element.28), channel_id=1, source_target_pairs={{0,16},{16,32},{32,48},{48,64},{64,80},{80,96},{96,112},{112,0},{1... | collective-permute-start | bytes 393224 | tf_op jit(solution)/shard_map/ppermute | solution.py:422
  115.1 2.3 %collective-permute-start.6 = (bf16[4,64,256]{2,1,0:T(8,128)(2,1)S(1)}, bf16[4,64,256]{2,1,0:T(8,128)(2,1)S(1)}, u32[]{:S(2)}, u32[]{:S(2)}) collective-permute-start(bf16[4,64,256]{2,1,0:T(8,128)(2,1)S(1)} %get-tuple-element.30), channel_id=1, source_target_pairs={{16,0},{32,16},{48,32},{64,48},{80,64},{96,80},{112,96},{0,112},{1... | collective-permute-start | bytes 393224 | tf_op jit(solution)/shard_map/ppermute | solution.py:423
  117.4 8.0 %collective-permute-done.12 = f32[272,256]{1,0:T(8,128)S(1)} collective-permute-done((f32[272,256]{1,0:T(8,128)S(1)}, f32[272,256]{1,0:T(8,128)S(1)}, u32[]{:S(2)}, u32[]{:S(2)}) %collective-permute-start.12) | collective-permute-done | bytes 278560 | tf_op jit(solution)/shard_map/ppermute | solution.py:432
  125.8 1.0 collective-permute-done.6
  126.9 0.6 gather_fusion.4
  127.6 6.5 %collective-permute-done.13 = f32[272,256]{1,0:T(8,128)S(1)} collective-permute-done((f32[272,256]{1,0:T(8,128)S(1)}, f32[272,256]{1,0:T(8,128)S(1)}, u32[]{:S(2)}, u32[]{:S(2)}) %collective-permute-start.13) | collective-permute-done | bytes 278560 | tf_op jit(solution)/shard_map/ppermute | solution.py:432
  134.2 1.6 %collective-permute-start.14 = (f32[272,256]{1,0:T(8,128)S(1)}, f32[272,256]{1,0:T(8,128)S(1)}, u32[]{:S(2)}, u32[]{:S(2)}) collective-permute-start(f32[272,256]{1,0:T(8,128)S(1)} %add.83), channel_id=1, source_target_pairs={{0,64},{16,80},{32,96},{48,112},{64,0},{80,16},{96,32},{112,48},{1... | collective-permute-start | bytes 835592 | tf_op jit(solution)/shard_map/ppermute | solution.py:432
  135.8 3.4 %copy-done.5 = bf16[4,64,64,256]{3,2,1,0:T(8,128)(2,1)S(1)} copy-done((bf16[4,64,64,256]{3,2,1,0:T(8,128)(2,1)S(1)}, bf16[4,64,64,256]{3,2,1,0:T(8,128)(2,1)}, u32[]{:S(2)}) %copy-start.5) | copy-done | bytes 8388632
  139.2 18.9 %spread.1 = bf16[4,64,64,256]{3,2,1,0:T(8,128)(2,1)} custom-call(bf16[4,64,64,256]{3,2,1,0:T(8,128)(2,1)S(1)} %copy-done.5, bf16[4,4,64,256]{3,2,1,0:T(8,128)(2,1)S(1)} %get-tuple-element.14.gr_ref, bf16[4,4,64,256]{3,2,1,0:T(8,128)(2,1)S(1)} %broadcast_select_fusion.in_ref, f32[2,9,8,128]{3,2,1,0:T(8,128)S(1)} %copy-done.2), custom_call_target="tpu_custom_call" | custom-call | flops 15000000512 | bytes 17825792 | tf_op jit(solution)/shard_map/spread/pallas_call | solution.py:396
  158.1 0.7 slice.80
  158.8 0.6 slice.78
  (74 shorter events, 4.2 us)
Async XLA Ops:
  0.6 4.8 %copy-start = (s32[1,4]{1,0:T(1,128)S(1)}, s32[1,4]{1,0:T(1,128)}, u32[]{:S(2)}) copy-start(s32[1,4]{1,0:T(1,128)} %param.19) | copy-start | bytes 52
  0.6 13.7 %copy-start.8 = (f32[9,256]{1,0:T(8,128)S(1)}, f32[9,256]{1,0:T(8,128)}, u32[]{:S(2)}) copy-start(f32[9,256]{1,0:T(8,128)} %param.15) | copy-start | bytes 27652
  0.7 14.4 %copy-start.9 = (f32[256]{0:T(256)S(1)}, f32[256]{0:T(256)}, u32[]{:S(2)}) copy-start(f32[256]{0:T(256)} %param.16) | copy-start | bytes 3076
  6.7 64.3 %collective-permute-start = (bf16[4,64,256]{2,1,0:T(8,128)(2,1)S(1)}, bf16[4,64,256]{2,1,0:T(8,128)(2,1)S(1)}, u32[]{:S(2)}, u32[]{:S(2)}) collective-permute-start(bf16[4,64,256]{2,1,0:T(8,128)(2,1)S(1)} %get-tuple-element.32), channel_id=1, source_target_pairs={{0,16},{16,32},{32,48},{48,64},{64,80},{80,96},{96,112},{112,0},{1... | collective-permute-start | bytes 393224 | tf_op jit(solution)/shard_map/ppermute | solution.py:422
  9.8 61.2 %collective-permute-start.1 = (bf16[4,64,256]{2,1,0:T(8,128)(2,1)S(1)}, bf16[4,64,256]{2,1,0:T(8,128)(2,1)S(1)}, u32[]{:S(2)}, u32[]{:S(2)}) collective-permute-start(bf16[4,64,256]{2,1,0:T(8,128)(2,1)S(1)} %get-tuple-element.35), channel_id=1, source_target_pairs={{1,0},{2,1},{3,2},{4,3},{5,4},{6,5},{7,6},{8,7},{9,8},{10,9},{11,1... | collective-permute-start | bytes 393224 | tf_op jit(solution)/shard_map/ppermute | solution.py:423
  12.4 58.6 %collective-permute-start.2 = (bf16[4,64,256]{2,1,0:T(8,128)(2,1)S(1)}, bf16[4,64,256]{2,1,0:T(8,128)(2,1)S(1)}, u32[]{:S(2)}, u32[]{:S(2)}) collective-permute-start(bf16[4,64,256]{2,1,0:T(8,128)(2,1)S(1)} %get-tuple-element.34), channel_id=1, source_target_pairs={{16,0},{32,16},{48,32},{64,48},{80,64},{96,80},{112,96},{0,112},{1... | collective-permute-start | bytes 393224 | tf_op jit(solution)/shard_map/ppermute | solution.py:423
  14.3 56.7 %collective-permute-start.3 = (bf16[4,64,256]{2,1,0:T(8,128)(2,1)S(1)}, bf16[4,64,256]{2,1,0:T(8,128)(2,1)S(1)}, u32[]{:S(2)}, u32[]{:S(2)}) collective-permute-start(bf16[4,64,256]{2,1,0:T(8,128)(2,1)S(1)} %get-tuple-element.33), channel_id=1, source_target_pairs={{0,1},{1,2},{2,3},{3,4},{4,5},{5,6},{6,7},{7,8},{8,9},{9,10},{10,1... | collective-permute-start | bytes 393224 | tf_op jit(solution)/shard_map/ppermute | solution.py:422
  15.6 55.3 %copy-start.10 = (s32[1,4]{1,0:T(1,128)S(1)}, s32[1,4]{1,0:T(1,128)}, u32[]{:S(2)}) copy-start(s32[1,4]{1,0:T(1,128)} %param.20) | copy-start | bytes 52
  15.6 56.2 %copy-start.2 = (f32[2,9,8,128]{3,2,1,0:T(8,128)S(1)}, f32[2,9,8,128]{3,2,1,0:T(8,128)}, u32[]{:S(2)}) copy-start(f32[2,9,8,128]{3,2,1,0:T(8,128)} %broadcast_in_dim.68.tap_ref) | copy-start | bytes 221188
  15.6 56.2 %copy-start.3 = (bf16[256,256]{1,0:T(8,128)(2,1)S(1)}, bf16[256,256]{1,0:T(8,128)(2,1)}, u32[]{:S(2)}) copy-start(bf16[256,256]{1,0:T(8,128)(2,1)} %w_ref.3) | copy-start | bytes 393220
  15.6 56.2 %copy-start.4 = (f32[2,8,128]{2,1,0:T(8,128)S(1)}, f32[2,8,128]{2,1,0:T(8,128)}, u32[]{:S(2)}) copy-start(f32[2,8,128]{2,1,0:T(8,128)} %broadcast_in_dim.70.bias_ref) | copy-start | bytes 24580
  71.8 3.4 %copy-start.1 = (bf16[4,64,64,256]{3,2,1,0:T(8,128)(2,1)S(1)}, bf16[4,64,64,256]{3,2,1,0:T(8,128)(2,1)}, u32[]{:S(2)}) copy-start(bf16[4,64,64,256]{3,2,1,0:T(8,128)(2,1)} %right_ref.1) | copy-start | bytes 25165828
  75.2 5.9 %copy-start.7 = (f32[2,10,8,128]{3,2,1,0:T(8,128)S(1)}, f32[2,10,8,128]{3,2,1,0:T(8,128)}, u32[]{:S(2)}) copy-start(f32[2,10,8,128]{3,2,1,0:T(8,128)} %get-tuple-element.18) | copy-start | bytes 245764
  75.2 6.0 %copy-start.6 = (f32[256,256]{1,0:T(8,128)S(1)}, f32[256,256]{1,0:T(8,128)}, u32[]{:S(2)}) copy-start(f32[256,256]{1,0:T(8,128)} %get-tuple-element.16) | copy-start | bytes 786436
  81.4 1.6 %collective-permute-start.8 = (f32[272,256]{1,0:T(8,128)S(1)}, f32[272,256]{1,0:T(8,128)S(1)}, u32[]{:S(2)}, u32[]{:S(2)}) collective-permute-start(f32[272,256]{1,0:T(8,128)S(1)} %maximum_maximum_fusion), channel_id=1, source_target_pairs={{0,1},{1,0},{2,3},{3,2},{4,5},{5,4},{6,7},{7,6},{8,9},{9,8},{10,11... | collective-permute-start | bytes 835592 | tf_op jit(solution)/shard_map/ppermute | solution.py:432
  83.2 8.8 %collective-permute-start.9 = (f32[272,256]{1,0:T(8,128)S(1)}, f32[272,256]{1,0:T(8,128)S(1)}, u32[]{:S(2)}, u32[]{:S(2)}) collective-permute-start(f32[272,256]{1,0:T(8,128)S(1)} %fusion.3), channel_id=1, source_target_pairs={{0,2},{1,3},{2,0},{3,1},{4,6},{5,7},{6,4},{7,5},{8,10},{9,11},{10,... | collective-permute-start | bytes 835592 | tf_op jit(solution)/shard_map/ppermute | solution.py:432
  92.0 11.4 %collective-permute-start.10 = (f32[272,256]{1,0:T(8,128)S(1)}, f32[272,256]{1,0:T(8,128)S(1)}, u32[]{:S(2)}, u32[]{:S(2)}) collective-permute-start(f32[272,256]{1,0:T(8,128)S(1)} %add.79), channel_id=1, source_target_pairs={{0,4},{1,5},{2,6},{3,7},{4,0},{5,1},{6,2},{7,3},{8,12},{9,13},{10,... | collective-permute-start | bytes 835592 | tf_op jit(solution)/shard_map/ppermute | solution.py:432
  103.4 7.9 %collective-permute-start.11 = (f32[272,256]{1,0:T(8,128)S(1)}, f32[272,256]{1,0:T(8,128)S(1)}, u32[]{:S(2)}, u32[]{:S(2)}) collective-permute-start(f32[272,256]{1,0:T(8,128)S(1)} %add.80), channel_id=1, source_target_pairs={{0,8},{1,9},{2,10},{3,11},{4,12},{5,13},{6,14},{7,15},{8,0},{9,1},... | collective-permute-start | bytes 835592 | tf_op jit(solution)/shard_map/ppermute | solution.py:432
  111.3 14.1 %collective-permute-start.12 = (f32[272,256]{1,0:T(8,128)S(1)}, f32[272,256]{1,0:T(8,128)S(1)}, u32[]{:S(2)}, u32[]{:S(2)}) collective-permute-start(f32[272,256]{1,0:T(8,128)S(1)} %add.81), channel_id=1, source_target_pairs={{0,16},{16,0},{32,48},{48,32},{64,80},{80,64},{96,112},{112,96},{1... | collective-permute-start | bytes 835592 | tf_op jit(solution)/shard_map/ppermute | solution.py:432
  111.5 14.3 %collective-permute-start.4 = (bf16[4,64,256]{2,1,0:T(8,128)(2,1)S(1)}, bf16[4,64,256]{2,1,0:T(8,128)(2,1)S(1)}, u32[]{:S(2)}, u32[]{:S(2)}) collective-permute-start(bf16[4,64,256]{2,1,0:T(8,128)(2,1)S(1)} %get-tuple-element.28), channel_id=1, source_target_pairs={{0,16},{16,32},{32,48},{48,64},{64,80},{80,96},{96,112},{112,0},{1... | collective-permute-start | bytes 393224 | tf_op jit(solution)/shard_map/ppermute | solution.py:422
  115.1 10.8 %collective-permute-start.5 = (bf16[4,64,256]{2,1,0:T(8,128)(2,1)S(1)}, bf16[4,64,256]{2,1,0:T(8,128)(2,1)S(1)}, u32[]{:S(2)}, u32[]{:S(2)}) collective-permute-start(bf16[4,64,256]{2,1,0:T(8,128)(2,1)S(1)} %get-tuple-element.31), channel_id=1, source_target_pairs={{1,0},{2,1},{3,2},{4,3},{5,4},{6,5},{7,6},{8,7},{9,8},{10,9},{11,1... | collective-permute-start | bytes 393224 | tf_op jit(solution)/shard_map/ppermute | solution.py:423
  115.1 11.8 %collective-permute-start.6 = (bf16[4,64,256]{2,1,0:T(8,128)(2,1)S(1)}, bf16[4,64,256]{2,1,0:T(8,128)(2,1)S(1)}, u32[]{:S(2)}, u32[]{:S(2)}) collective-permute-start(bf16[4,64,256]{2,1,0:T(8,128)(2,1)S(1)} %get-tuple-element.30), channel_id=1, source_target_pairs={{16,0},{32,16},{48,32},{64,48},{80,64},{96,80},{112,96},{0,112},{1... | collective-permute-start | bytes 393224 | tf_op jit(solution)/shard_map/ppermute | solution.py:423
  117.3 9.5 %collective-permute-start.7 = (bf16[4,64,256]{2,1,0:T(8,128)(2,1)S(1)}, bf16[4,64,256]{2,1,0:T(8,128)(2,1)S(1)}, u32[]{:S(2)}, u32[]{:S(2)}) collective-permute-start(bf16[4,64,256]{2,1,0:T(8,128)(2,1)S(1)} %get-tuple-element.29), channel_id=1, source_target_pairs={{0,1},{1,2},{2,3},{3,4},{4,5},{5,6},{6,7},{7,8},{8,9},{9,10},{10,1... | collective-permute-start | bytes 393224 | tf_op jit(solution)/shard_map/ppermute | solution.py:422
  125.5 8.7 %collective-permute-start.13 = (f32[272,256]{1,0:T(8,128)S(1)}, f32[272,256]{1,0:T(8,128)S(1)}, u32[]{:S(2)}, u32[]{:S(2)}) collective-permute-start(f32[272,256]{1,0:T(8,128)S(1)} %add.82), channel_id=1, source_target_pairs={{0,32},{16,48},{32,0},{48,16},{64,96},{80,112},{96,64},{112,80},{1... | collective-permute-start | bytes 835592 | tf_op jit(solution)/shard_map/ppermute | solution.py:432
  134.2 23.9 %collective-permute-start.14 = (f32[272,256]{1,0:T(8,128)S(1)}, f32[272,256]{1,0:T(8,128)S(1)}, u32[]{:S(2)}, u32[]{:S(2)}) collective-permute-start(f32[272,256]{1,0:T(8,128)S(1)} %add.83), channel_id=1, source_target_pairs={{0,64},{16,80},{32,96},{48,112},{64,0},{80,16},{96,32},{112,48},{1... | collective-permute-start | bytes 835592 | tf_op jit(solution)/shard_map/ppermute | solution.py:432
  135.8 3.4 %copy-start.5 = (bf16[4,64,64,256]{3,2,1,0:T(8,128)(2,1)S(1)}, bf16[4,64,64,256]{3,2,1,0:T(8,128)(2,1)}, u32[]{:S(2)}) copy-start(bf16[4,64,64,256]{3,2,1,0:T(8,128)(2,1)} %get-tuple-element.13.gh_ref) | copy-start | bytes 25165828

commit v2 on v1

--- a/solution.py
+++ b/solution.py
@@ -154,7 +154,7 @@
             pltpu.VMEM((side, cols, channels), BF16),
             pltpu.VMEM((2, 10, SUB, LANES), F32),
         ],
-        compiler_params=pltpu.CompilerParams(vmem_limit_bytes=56 << 20),
+        compiler_params=pltpu.CompilerParams(vmem_limit_bytes=60 << 20),
         cost_estimate=pl.CostEstimate(
             flops=40_000_000_000, bytes_accessed=26 << 20, transcendentals=state.size
         ),
@@ -168,15 +168,15 @@
 
 def ring_body(
     mask_ref, top_ref, low_ref, left_ref, right_ref, ctop_ref, clow_ref, cleft_ref, cright_ref,
-    rim_ref, w_ref, tap_ref, bias_ref, gr_ref, rg_ref, pg_ref, dg_ref, strip, ext, acts, acc,
+    rim_ref, w_ref, tap_ref, bias_ref, pg_ref, dg_ref, gr_ref, rg_ref, part_ref, strip, ext, acts, acc,
 ):
     step = pl.program_id(0)
     side = rim_ref.shape[2]
 
     @pl.when(step == 0)
     def _():
-        acc[...] = jnp.zeros_like(acc)
-        pg_ref[...] = jnp.zeros_like(pg_ref)
+        acc[...] = dg_ref[...]
+        part_ref[0 : 2 * LANES, :] = pg_ref[...]
         ext[...] = jnp.zeros_like(ext)
 
     rims = [rim_ref[s, 0].astype(F32) for s in range(4)]
@@ -270,14 +270,20 @@
             back = back + jnp.where(row == 0, (0.5 * mask_ref[LOW[s]]) * first * g, 0.0)
             back = back + jnp.where(row == end, (0.5 * mask_ref[HIGH[s]]) * final * g, 0.0)
             rg_ref[s, 0, :, lanes] = back.astype(BF16)
-    pg_ref[...] += lax.dot_general(acts[...], cots, (((0,), (0,)), ((), ())), preferred_element_type=F32)
+    part_ref[0 : 2 * LANES, :] += lax.dot_general(
+        acts[...], cots, (((0,), (0,)), ((), ())), preferred_element_type=F32
+    )
 
     @pl.when(step == pl.num_programs(0) - 1)
     def _():
-        dg_ref[...] = acc[...]
-
-
-def ring_call(mask, state, cotangent, rims, weight, taps, bias):
+        part_ref[2 * LANES :, :] = jnp.zeros((16, 2 * LANES), F32)
+        for hf in range(2):
+            for k in range(10):
+                line = jnp.sum(acc[hf, k], axis=0, keepdims=True)
+                part_ref[2 * LANES + k : 2 * LANES + k + 1, hf * LANES : hf * LANES + LANES] = line
+
+
+def ring_call(mask, state, cotangent, rims, weight, taps, bias, point_inner, depth_inner):
     batch, side, cols, channels = state.shape
     wide = 16
     two = lambda at: pl.BlockSpec((1, 2, cols, channels), lambda b: (b, at, 0, 0))
@@ -302,18 +308,14 @@
             pl.BlockSpec((channels, channels), lambda b: (0, 0)),
             pl.BlockSpec((2, 9, SUB, LANES), lambda b: (0, 0, 0, 0)),
             pl.BlockSpec((2, SUB, LANES), lambda b: (0, 0, 0)),
-        ],
-        out_specs=[
-            strips,
-            strips,
             pl.BlockSpec((channels, channels), lambda b: (0, 0)),
             pl.BlockSpec((2, 10, SUB, LANES), lambda b: (0, 0, 0, 0)),
         ],
+        out_specs=[strips, strips, pl.BlockSpec((channels + 16, channels), lambda b: (0, 0))],
         out_shape=[
             jax.ShapeDtypeStruct((4, batch, side, channels), BF16),
             jax.ShapeDtypeStruct((4, batch, side, channels), BF16),
-            jax.ShapeDtypeStruct((channels, channels), F32),
-            jax.ShapeDtypeStruct((2, 10, SUB, LANES), F32),
+            jax.ShapeDtypeStruct((channels + 16, channels), F32),
         ],
         scratch_shapes=[
             pltpu.VMEM((4, 2, 3, cols + 2 * PAD, LANES), F32),
@@ -321,93 +323,195 @@
             pltpu.VMEM((4 * side, channels), BF16),
             pltpu.VMEM((2, 10, SUB, LANES), F32),
         ],
-        compiler_params=pltpu.CompilerParams(vmem_limit_bytes=40 << 20),
+        compiler_params=pltpu.CompilerParams(vmem_limit_bytes=60 << 20),
         cost_estimate=pl.CostEstimate(
             flops=3_000_000_000, bytes_accessed=12 << 20, transcendentals=state.size // 16
         ),
         name="ring",
-    )(mask, state, state, state, state, cotangent, cotangent, cotangent, cotangent, rims, weight, taps, bias)
-
-
-def spread_body(rows_at_once, gh_ref, gr_ref, in_ref, tap_ref, out_ref, gf, near, far):
-    side = gh_ref.shape[1]
+    )(mask, state, state, state, state, cotangent, cotangent, cotangent, cotangent, rims, weight, taps, bias,
+      point_inner, depth_inner)
+
+
+def spread_body(rows, gh_ref, above_ref, below_ref, gr_ref, in_ref, tap_ref, *rest):
+    out_ref, token_ref, gf, near, far, ring = rest[-6:]
+    step = pl.program_id(0) + rest[-7]
+    side = gr_ref.shape[2]
     cols = gh_ref.shape[2]
-    for hf in range(2):
-        gf[hf, 0] = jnp.zeros(gf.shape[2:], F32)
-        gf[hf, side + 1] = jnp.zeros(gf.shape[2:], F32)
-        gf[hf, :, 0:PAD, :] = jnp.zeros((side + 2, PAD, LANES), F32)
-        gf[hf, :, PAD + cols : 2 * PAD + cols, :] = jnp.zeros((side + 2, PAD, LANES), F32)
-    near[...] = jnp.zeros_like(near)
-    far[...] = jnp.zeros_like(far)
-
-    def widen(i, _):
-        v = gh_ref[0, i].astype(F32)
-        gf[0, i + 1, PAD : PAD + cols, :] = v[:, :LANES]
-        gf[1, i + 1, PAD : PAD + cols, :] = v[:, LANES:]
-        return 0
-
-    lax.fori_loop(1, side - 1, widen, 0)
-    ring = [gr_ref[s, 0].astype(F32) for s in range(4)]
-    back = [in_ref[s, 0].astype(F32) for s in (1, 3)]
+    count = gh_ref.shape[1]
+    chunks = side // count
+    token_ref[...] = jnp.zeros_like(token_ref)
+    start = step * count
+
+    @pl.when(pl.program_id(0) == 0)
+    def _():
+        for hf in range(2):
+            lanes = slice(hf * LANES, hf * LANES + LANES)
+            gf[hf, :, 0:PAD, :] = jnp.zeros((count + 2, PAD, LANES), F32)
+            gf[hf, :, PAD + cols : 2 * PAD + cols, :] = jnp.zeros((count + 2, PAD, LANES), F32)
+            for k, s in enumerate((1, 3)):
+                ring[k, hf, 0:PAD, :] = jnp.zeros((PAD, LANES), F32)
+                ring[k, hf, PAD + side :, :] = jnp.zeros((PAD, LANES), F32)
+                ring[k, hf, PAD : PAD + side, :] = gr_ref[s, 0, :, lanes].astype(F32)
+        near[...] = jnp.zeros_like(near)
+        far[...] = jnp.zeros_like(far)
+
+    def put(i, v):
+        v = v.astype(F32)
+        gf[0, i, PAD : PAD + cols, :] = v[:, :LANES]
+        gf[1, i, PAD : PAD + cols, :] = v[:, LANES:]
+
+    put(0, jnp.where(step > 0, above_ref[0, 0], jnp.zeros_like(above_ref[0, 0])))
+    put(count + 1, jnp.where(step < chunks - 1, below_ref[0, 0], jnp.zeros_like(below_ref[0, 0])))
+    for i in range(count):
+        put(i + 1, gh_ref[0, i])
+    back = [in_ref[s, 0, pl.ds(pl.multiple_of(start, count), count), :].astype(F32) for s in (1, 3)]
     for hf in range(2):
         lanes = slice(hf * LANES, hf * LANES + LANES)
-        gf[hf, 1 : side + 1, PAD : PAD + 1, :] = ring[3][:, lanes].reshape(side, 1, LANES)
-        gf[hf, 1 : side + 1, PAD + cols - 1 : PAD + cols, :] = ring[1][:, lanes].reshape(side, 1, LANES)
-        gf[hf, 1, PAD : PAD + cols, :] = ring[0][:, lanes]
-        gf[hf, side, PAD : PAD + cols, :] = ring[2][:, lanes]
-        near[hf, :, 0:1, :] = back[1][:, lanes].reshape(side, 1, LANES)
-        far[hf, :, SUB - 1 : SUB, :] = back[0][:, lanes].reshape(side, 1, LANES)
+        for k, j in ((0, PAD + cols - 1), (1, PAD)):
+            own = ring[k, hf, pl.ds(pl.multiple_of(PAD + start, SUB), count), :]
+            gf[hf, 1 : count + 1, j : j + 1, :] = own.reshape(count, 1, LANES)
+            gf[hf, 0, j : j + 1, :] = ring[k, hf, pl.ds(PAD + start - 1, 1), :]
+            gf[hf, count + 1, j : j + 1, :] = ring[k, hf, pl.ds(PAD + start + count, 1), :]
+        near[hf, :, 0:1, :] = back[1][:, lanes].reshape(count, 1, LANES)
+        far[hf, :, SUB - 1 : SUB, :] = back[0][:, lanes].reshape(count, 1, LANES)
+
+    def line(i, s):
+        v = gr_ref[s, 0].astype(F32)
+        for hf in range(2):
+            gf[hf, i, PAD : PAD + cols, :] = v[:, hf * LANES : hf * LANES + LANES]
+
+    @pl.when(step == 0)
+    def _():
+        line(1, 0)
+
+    @pl.when(step == chunks - 1)
+    def _():
+        line(count, 2)
+
     for hf in range(2):
         lanes = slice(hf * LANES, hf * LANES + LANES)
+
         for jb in range(cols // 16):
 
             def body(it, carry):
-                i = it * rows_at_once
+                i = it * rows
                 win = {}
-                for q in range(rows_at_once):
+                for q in range(rows):
                     pair = []
-                    for part in range(2):
-                        j = PAD + jb * 16 + part * SUB
+                    for half in range(2):
+                        j = PAD + jb * 16 + half * SUB
                         total = None
                         for r in range(3):
                             for c in range(3):
-                                at = (q + 2 - r, 2 - c, part)
+                                at = (q + 2 - r, 2 - c, half)
                                 if at not in win:
                                     win[at] = gf[hf, i + at[0], j - 1 + at[1] : j - 1 + at[1] + SUB, :]
                                 term = tap_ref[hf, 3 * r + c] * win[at]
                                 total = term if total is None else total + term
-                        if jb == 0 and part == 0:
+                        if jb == 0 and half == 0:
                             total = total + near[hf, i + q]
-                        if jb == cols // 16 - 1 and part == 1:
+                        if jb == cols // 16 - 1 and half == 1:
                             total = total + far[hf, i + q]
                         pair.append(total)
                     out_ref[0, i + q, jb * 16 : jb * 16 + 16, lanes] = jnp.concatenate(pair, axis=0).astype(BF16)
                 return carry
 
-            lax.fori_loop(0, side // rows_at_once, body, 0)
-    for at, s in ((0, 0), (side - 1, 2)):
-        out_ref[0, at] = (out_ref[0, at].astype(F32) + in_ref[s, 0].astype(F32)).astype(BF16)
-
-
-def spread_call(grad, ring, incoming, taps):
+            lax.fori_loop(0, count // rows, body, 0)
+
+    def add(i, s):
+        out_ref[0, i] = (out_ref[0, i].astype(F32) + in_ref[s, 0].astype(F32)).astype(BF16)
+
+    @pl.when(step == 0)
+    def _():
+        add(0, 0)
+
+    @pl.when(step == chunks - 1)
+    def _():
+        add(count - 1, 2)
+
+
+CHUNK = 16
+STEPS = 2
+
+
+def spread_call(part, grad, ring, incoming, taps, into):
     batch, side, cols, channels = grad.shape
-    tile = pl.BlockSpec((1, side, cols, channels), lambda b: (b, 0, 0, 0))
-    strips = pl.BlockSpec((4, 1, side, channels), lambda b: (0, b, 0, 0))
+    parts = side // (CHUNK * STEPS)
+    b, first = part // parts, part % parts * STEPS
+    low, high = first * CHUNK, side - 1
+    strips = pl.BlockSpec((4, 1, side, channels), lambda i: (0, b, 0, 0))
+    in_specs = [
+        pl.BlockSpec((1, CHUNK, cols, channels), lambda i: (b, i + first, 0, 0)),
+        pl.BlockSpec((1, 1, cols, channels), lambda i: (b, jnp.maximum((i + first) * CHUNK - 1, 0), 0, 0)),
+        pl.BlockSpec((1, 1, cols, channels), lambda i: (b, jnp.minimum((i + first + 1) * CHUNK, high), 0, 0)),
+        strips,
+        strips,
+        pl.BlockSpec((2, 9, SUB, LANES), lambda i: (0, 0, 0, 0)),
+    ]
+    operands = [grad, grad, grad, ring, incoming, taps]
+    aliases = {}
+    if into is not None:
+        in_specs.append(pl.BlockSpec(memory_space=pl.ANY))
+        operands.append(into)
+        aliases = {6: 0}
+
+    def body(*refs):
+        n = len(operands)
+        spread_body(4, *refs[:6], first, *refs[n:])
+
     return pl.pallas_call(
-        functools.partial(spread_body, 4),
-        grid=(batch,),
-        in_specs=[tile, strips, strips, pl.BlockSpec((2, 9, SUB, LANES), lambda b: (0, 0, 0, 0))],
-        out_specs=tile,
-        out_shape=jax.ShapeDtypeStruct(grad.shape, BF16),
+        body,
+        grid=(STEPS,),
+        in_specs=in_specs,
+        out_specs=[
+            pl.BlockSpec((1, CHUNK, cols, channels), lambda i: (b, i + first, 0, 0)),
+            pl.BlockSpec((SUB, LANES), lambda i: (0, 0)),
+        ],
+        out_shape=[jax.ShapeDtypeStruct(grad.shape, BF16), jax.ShapeDtypeStruct((SUB, LANES), F32)],
         scratch_shapes=[
-            pltpu.VMEM((2, side + 2, cols + 2 * PAD, LANES), F32),
-            pltpu.VMEM((2, side, SUB, LANES), F32),
-            pltpu.VMEM((2, side, SUB, LANES), F32),
-        ],
-        compiler_params=pltpu.CompilerParams(vmem_limit_bytes=40 << 20),
-        cost_estimate=pl.CostEstimate(flops=15_000_000_000, bytes_accessed=17 << 20, transcendentals=0),
+            pltpu.VMEM((2, CHUNK + 2, cols + 2 * PAD, LANES), F32),
+            pltpu.VMEM((2, CHUNK, SUB, LANES), F32),
+            pltpu.VMEM((2, CHUNK, SUB, LANES), F32),
+            pltpu.VMEM((2, 2, side + 2 * PAD, LANES), F32),
+        ],
+        input_output_aliases=aliases,
+        compiler_params=pltpu.CompilerParams(vmem_limit_bytes=60 << 20),
+        cost_estimate=pl.CostEstimate(
+            flops=1_500_000_000, bytes_accessed=grad.size * 4 // (batch * parts), transcendentals=0
+        ),
         name="spread",
-    )(grad, ring, incoming, taps)
+    )(*operands)
+
+
+def finish_body(scale, bit_ref, mine_ref, other_ref, dg_ref, bg_ref, pg_ref):
+    rows = mine_ref.shape[0]
+    channels = pg_ref.shape[0]
+    own = mine_ref[...] * scale
+    far = other_ref[...] * scale
+    first = bit_ref[0] == 0
+    low = jnp.where(first, own, far)
+    high = jnp.where(first, far, own)
+    pg_ref[0:rows, :] = low
+    pg_ref[rows:channels, :] = high[: channels - rows]
+    tail = high[channels - rows :]
+    dg_ref[...] = tail[0:9]
+    bg_ref[...] = tail[9:10]
+
+
+def finish_call(scale, bit, mine, other):
+    channels = mine.shape[1]
+    vmem = pl.BlockSpec(memory_space=pltpu.VMEM)
+    return pl.pallas_call(
+        functools.partial(finish_body, scale),
+        in_specs=[pl.BlockSpec(memory_space=pltpu.SMEM), vmem, vmem],
+        out_specs=[vmem, vmem, vmem],
+        out_shape=[
+            jax.ShapeDtypeStruct((9, channels), F32),
+            jax.ShapeDtypeStruct((1, channels), F32),
+            jax.ShapeDtypeStruct((channels, channels), F32),
+        ],
+        name="finish",
+    )(bit, mine, other)
 
 
 def exchange(by_side, side_of_dir, dir_of_side, flips):
@@ -424,14 +528,13 @@
     return jnp.take(jnp.stack(got, axis=0), dir_of_side, axis=0)
 
 
-def all_sum(part):
-    for axis in ("tile", "face"):
-        count = lax.axis_size(axis)
-        bit = 1
-        while bit < count:
-            part = part + lax.ppermute(part, axis, [(i, i ^ bit) for i in range(count)])
-            bit *= 2
-    return part
+def swap(value, mask):
+    devices = lax.axis_size("face") * lax.axis_size("tile")
+    return lax.ppermute(value, ("face", "tile"), [(i, i ^ mask) for i in range(devices)])
+
+
+def after(value, *others):
+    return lax.optimization_barrier((value, *others))[0]
 
 
 def shards(
@@ -465,18 +568,29 @@
     edges = jnp.stack([state[:, 0], state[:, :, -1], state[:, -1], state[:, :, 0]], axis=0)
     rims = exchange(edges, side_of_dir, dir_of_side, flips)
     grad, point_inner, depth_inner = inner_call(state, cotangent, point_weight, taps, bias)
-    ring, rim_grads, point_ring, depth_ring = ring_call(
-        mask, state, cotangent, rims, point_weight, taps, bias
+    ring, rim_grads, part = ring_call(
+        mask, state, cotangent, rims, point_weight, taps, bias, point_inner, depth_inner
     )
     incoming = exchange(rim_grads, side_of_dir, dir_of_side, flips)
-    field_grad = spread_call(grad, ring, incoming, taps)
-
-    depth_part = jnp.sum(depth_inner + depth_ring, axis=2).transpose(1, 0, 2).reshape(10, channels)
-    part = jnp.concatenate(
-        [point_inner + point_ring, depth_part, jnp.zeros((6, channels), F32)], axis=0
-    )
-    total = all_sum(part) * float(batch * side * cols * face_count * tile_count) ** -0.5
-    return field_grad, total[channels : channels + 9], total[channels + 9], total[:channels]
+
+    core = tile_pos % 2
+    half = part.shape[0] // 2
+    low, high = part[:half], part[half:]
+    mine = jnp.where(core == 0, low, high)
+    sent = jnp.where(core == 0, high, low)
+    pieces = batch * side // (CHUNK * STEPS)
+    field_grad = None
+    for stage, mask_bits in enumerate((1, 2, 6, 8, 24, 32, 96, 1)):
+        got = swap(sent if stage == 0 else mine, mask_bits)
+        if stage < pieces:
+            held = after(taps, mine if stage else sent)
+            field_grad, token = spread_call(stage, grad, ring, incoming, held, field_grad)
+            got = after(got, token)
+        if stage < 7:
+            mine = mine + got
+    scale = float(batch * side * cols * face_count * tile_count) ** -0.5
+    depth_grad, bias_grad, point_grad = finish_call(scale, core.reshape(1), mine, got)
+    return field_grad, depth_grad, bias_grad.reshape(channels), point_grad
 
 
 def solution(mesh):

time: 160 us -> 150 us (0.938)
  the two profiles are of different devices: /device:TPU:32 before, /device:TPU:1 now
where the time goes in v2:
time: 150 us; the launch traced here: 149 us
  Pallas kernels  96.8 us (65%)
  starting transfers between devices  34.9 us (23%)
  local copies, waits for them, and re-layouts  9.72 us (6%)
  other arithmetic  5.13 us (3%)
  waiting for transfers between devices  1.57 us (1%)
    pallas_call x1, Pallas kernels, inner_call(): pl.pallas_call(functools.partial(inner_body, 4), grid=(batch,), in_specs=...  54.3 us
    pallas_call x8, Pallas kernels, spread_call(): pl.pallas_call(body, grid=(STEPS,), in_specs=in_specs, out_specs=[pl.Bloc...  33.3 us
    ppermute x8, starting transfers between devices, swap(): lax.ppermute(value, ('face', 'tile'), [(i, i ^ mask) for i in range(devic...  18.1 us
    ppermute x4, starting transfers between devices, exchange(): got[high] = lax.ppermute(facing[low], axis, down)  9.78 us
    pallas_call x1, Pallas kernels, ring_call(): pl.pallas_call(ring_body, grid=(batch,), in_specs=[pl.BlockSpec(memory_sp...  7.51 us
    ppermute x4, starting transfers between devices, exchange(): got[low] = lax.ppermute(facing[high], axis, up)  7 us
  transfers between devices with their start and end apart: 16, of which 2 were waited for; matrix products, arithmetic and copies ran while one was open for 3% of the time, Pallas kernels for 59%

profile of v2, /device:TPU:1, one launch (start us, length us, event | category | flops | bytes accessed | tf_op | source)
XLA Modules:
  0.0 149.2 jit_solution(15490448378384255598)
XLA Ops:
  0.7 2.0 %fusion.2 = (bf16[4,64,1,256]{3,2,1,0:T(2,128)(2,1)S(1)}, bf16[4,64,1,256]{3,2,1,0:T(2,128)(2,1)S(1)}) fusion(bf16[4,64,64,256]{3,2,1,0:T(8,128)(2,1)} %right_ref.1), kind=kLoop, calls=%fused_computation.42 | loop fusion | bytes 524288 | tf_op jit(solution)/shard_map/slice | solution.py:568
  2.7 1.0 slice_bitcast_fusion.9
  3.8 0.8 fusion.1
  5.4 0.6 gather_fusion
  6.7 4.5 %collective-permute-start = (bf16[4,64,256]{2,1,0:T(8,128)(2,1)S(1)}, bf16[4,64,256]{2,1,0:T(8,128)(2,1)S(1)}, u32[]{:S(2)}, u32[]{:S(2)}) collective-permute-start(bf16[4,64,256]{2,1,0:T(8,128)(2,1)S(1)} %get-tuple-element.68), channel_id=1, source_target_pairs={{0,16},{16,32},{32,48},{48,64},{64,80},{80,96},{96,112},{112,0},{1... | collective-permute-start | bytes 393224 | tf_op jit(solution)/shard_map/ppermute | solution.py:526
  11.2 1.0 collective-permute-start.1
  12.2 2.0 %collective-permute-start.2 = (bf16[4,64,256]{2,1,0:T(8,128)(2,1)S(1)}, bf16[4,64,256]{2,1,0:T(8,128)(2,1)S(1)}, u32[]{:S(2)}, u32[]{:S(2)}) collective-permute-start(bf16[4,64,256]{2,1,0:T(8,128)(2,1)S(1)} %get-tuple-element.70), channel_id=1, source_target_pairs={{16,0},{32,16},{48,32},{64,48},{80,64},{96,80},{112,96},{0,112},{1... | collective-permute-start | bytes 393224 | tf_op jit(solution)/shard_map/ppermute | solution.py:527
  14.2 1.5 %collective-permute-start.3 = (bf16[4,64,256]{2,1,0:T(8,128)(2,1)S(1)}, bf16[4,64,256]{2,1,0:T(8,128)(2,1)S(1)}, u32[]{:S(2)}, u32[]{:S(2)}) collective-permute-start(bf16[4,64,256]{2,1,0:T(8,128)(2,1)S(1)} %get-tuple-element.69), channel_id=1, source_target_pairs={{0,1},{1,2},{2,3},{3,4},{4,5},{5,6},{6,7},{7,8},{8,9},{9,10},{10,1... | collective-permute-start | bytes 393224 | tf_op jit(solution)/shard_map/ppermute | solution.py:526
  15.7 0.6 broadcast_in_dim.65.tap_ref.refs_5_
  17.0 54.3 %inner.1 = (bf16[4,64,64,256]{3,2,1,0:T(8,128)(2,1)}, f32[256,256]{1,0:T(8,128)}, f32[2,10,8,128]{3,2,1,0:T(8,128)}) custom-call(bf16[4,64,64,256]{3,2,1,0:T(8,128)(2,1)} %right_ref.1, bf16[4,64,64,256]{3,2,1,0:T(8,128)(2,1)} %cright_ref.1, bf16[256,256]{1,0:T(8,128)(2,1)} %w_ref.3, f32[2,9,8,128]{3,2,1,0:T(8,128)} %broadcast_in_dim.65.tap_ref.refs_5_, ...), custom_call_target="tpu_custom_call" | custom-call | flops 40000000000 | bytes 27262976 | tf_op jit(solution)/shard_map/inner/pallas_call | solution.py:131
  72.5 0.9 broadcast_select_fusion.1.rim_ref
  73.4 7.5 %ring.1 = (bf16[4,4,64,256]{3,2,1,0:T(8,128)(2,1)}, bf16[4,4,64,256]{3,2,1,0:T(8,128)(2,1)}, f32[272,256]{1,0:T(8,128)}) custom-call(f32[4]{0:T(128)} %convert_bitcast_fusion.mask_ref, bf16[4,64,64,256]{3,2,1,0:T(8,128)(2,1)} %right_ref.1, bf16[4,64,64,256]{3,2,1,0:T(8,128)(2,1)} %right_ref.1, bf16[4,64,64,256]{3,2,1,0:T(8,128)(2,1)} %right_ref.1, ...), custom_call_target="tpu_custom_call" | custom-call | flops 3000000000 | bytes 12582912 | tf_op jit(solution)/shard_map/ring/pallas_call | solution.py:294
  81.0 1.6 %gather_fusion.3 = bf16[4,4,64,256]{3,2,1,0:T(8,128)(2,1)S(1)} fusion(bf16[4,4,64,256]{3,2,1,0:T(8,128)(2,1)} %get-tuple-element.35, s32[1024]{0:T(1024)S(1)} %pad_clamp_fusion.1), kind=kCustom, calls=%fused_computation.3.clone | custom fusion | bytes 1048592 | tf_op jit(solution)/shard_map/jit(_take)/gather | solution.py:518
  83.3 1.0 collective-permute-start.4
  84.2 1.7 %collective-permute-start.5 = (bf16[4,64,256]{2,1,0:T(8,128)(2,1)S(1)}, bf16[4,64,256]{2,1,0:T(8,128)(2,1)S(1)}, u32[]{:S(2)}, u32[]{:S(2)}) collective-permute-start(bf16[4,64,256]{2,1,0:T(8,128)(2,1)S(1)} %get-tuple-element.67), channel_id=1, source_target_pairs={{1,0},{2,1},{3,2},{4,3},{5,4},{6,5},{7,6},{8,7},{9,8},{10,9},{11,1... | collective-permute-start | bytes 393224 | tf_op jit(solution)/shard_map/ppermute | solution.py:527
  85.9 5.1 %collective-permute-start.6 = (bf16[4,64,256]{2,1,0:T(8,128)(2,1)S(1)}, bf16[4,64,256]{2,1,0:T(8,128)(2,1)S(1)}, u32[]{:S(2)}, u32[]{:S(2)}) collective-permute-start(bf16[4,64,256]{2,1,0:T(8,128)(2,1)S(1)} %get-tuple-element.66), channel_id=1, source_target_pairs={{16,0},{32,16},{48,32},{64,48},{80,64},{96,80},{112,96},{0,112},{1... | collective-permute-start | bytes 393224 | tf_op jit(solution)/shard_map/ppermute | solution.py:527
  91.0 1.0 slice_select_fusion
  92.0 4.6 %collective-permute-start.8 = (f32[136,256]{1,0:T(8,128)S(1)}, f32[136,256]{1,0:T(8,128)S(1)}, u32[]{:S(2)}, u32[]{:S(2)}) collective-permute-start(f32[136,256]{1,0:T(8,128)S(1)} %slice_select_fusion), channel_id=1, source_target_pairs={{0,1},{1,0},{2,3},{3,2},{4,5},{5,4},{6,7},{7,6},{8,9},{9,8},{10,11... | collective-permute-start | bytes 417800 | tf_op jit(solution)/shard_map/ppermute | solution.py:533
  97.3 0.9 broadcast_select_fusion.refs_4_
  98.2 4.2 %spread.8 = (bf16[4,64,64,256]{3,2,1,0:T(8,128)(2,1)}, f32[8,128]{1,0:T(8,128)}) custom-call(bf16[4,64,64,256]{3,2,1,0:T(8,128)(2,1)} %get-tuple-element.31.refs_0_.refs_1_.refs_2_, bf16[4,64,64,256]{3,2,1,0:T(8,128)(2,1)} %get-tuple-element.31.refs_0_.refs_1_.refs_2_, bf16[4,64,64,256]{3,2,1,0:T(8,128)(2,1)} %get-tuple-element.31.refs_0_.refs_1_.refs_2_, ...), custom_call_target="tpu_custom_call" | custom-call | flops 1500000000 | bytes 2097152 | tf_op jit(solution)/shard_map/spread/pallas_call | solution.py:462
  102.5 4.2 %spread.9 = (bf16[4,64,64,256]{3,2,1,0:T(8,128)(2,1)}, f32[8,128]{1,0:T(8,128)}) custom-call(bf16[4,64,64,256]{3,2,1,0:T(8,128)(2,1)} %get-tuple-element.31.refs_0_.refs_1_.refs_2_, bf16[4,64,64,256]{3,2,1,0:T(8,128)(2,1)} %get-tuple-element.31.refs_0_.refs_1_.refs_2_, ...), custom_call_target="tpu_custom_call", output_to_operand_aliasing={{0}: (6, {})} | custom-call | flops 1500000000 | bytes 2097152 | tf_op jit(solution)/shard_map/spread/pallas_call | solution.py:462
  106.7 2.7 %collective-permute-start.10 = (f32[136,256]{1,0:T(8,128)S(1)}, f32[136,256]{1,0:T(8,128)S(1)}, u32[]{:S(2)}, u32[]{:S(2)}) collective-permute-start(f32[136,256]{1,0:T(8,128)S(1)} %add.75), channel_id=1, source_target_pairs={{0,6},{1,7},{2,4},{3,5},{4,2},{5,3},{6,0},{7,1},{8,14},{9,15},{10,... | collective-permute-start | bytes 417800 | tf_op jit(solution)/shard_map/ppermute | solution.py:533
  109.4 4.1 %spread.10 = (bf16[4,64,64,256]{3,2,1,0:T(8,128)(2,1)}, f32[8,128]{1,0:T(8,128)}) custom-call(bf16[4,64,64,256]{3,2,1,0:T(8,128)(2,1)} %get-tuple-element.31.refs_0_.refs_1_.refs_2_, bf16[4,64,64,256]{3,2,1,0:T(8,128)(2,1)} %get-tuple-element.31.refs_0_.refs_1_.refs_2_, ...), custom_call_target="tpu_custom_call", output_to_operand_aliasing={{0}: (6, {})} | custom-call | flops 1500000000 | bytes 2097152 | tf_op jit(solution)/shard_map/spread/pallas_call | solution.py:462
  113.6 3.4 %collective-permute-start.11 = (f32[136,256]{1,0:T(8,128)S(1)}, f32[136,256]{1,0:T(8,128)S(1)}, u32[]{:S(2)}, u32[]{:S(2)}) collective-permute-start(f32[136,256]{1,0:T(8,128)S(1)} %add.76), channel_id=1, source_target_pairs={{0,8},{1,9},{2,10},{3,11},{4,12},{5,13},{6,14},{7,15},{8,0},{9,1},... | collective-permute-start | bytes 417800 | tf_op jit(solution)/shard_map/ppermute | solution.py:533
  117.0 4.1 %spread.11 = (bf16[4,64,64,256]{3,2,1,0:T(8,128)(2,1)}, f32[8,128]{1,0:T(8,128)}) custom-call(bf16[4,64,64,256]{3,2,1,0:T(8,128)(2,1)} %get-tuple-element.31.refs_0_.refs_1_.refs_2_, bf16[4,64,64,256]{3,2,1,0:T(8,128)(2,1)} %get-tuple-element.31.refs_0_.refs_1_.refs_2_, ...), custom_call_target="tpu_custom_call", output_to_operand_aliasing={{0}: (6, {})} | custom-call | flops 1500000000 | bytes 2097152 | tf_op jit(solution)/shard_map/spread/pallas_call | solution.py:462
  121.3 4.2 %spread.12 = (bf16[4,64,64,256]{3,2,1,0:T(8,128)(2,1)}, f32[8,128]{1,0:T(8,128)}) custom-call(bf16[4,64,64,256]{3,2,1,0:T(8,128)(2,1)} %get-tuple-element.31.refs_0_.refs_1_.refs_2_, bf16[4,64,64,256]{3,2,1,0:T(8,128)(2,1)} %get-tuple-element.31.refs_0_.refs_1_.refs_2_, ...), custom_call_target="tpu_custom_call", output_to_operand_aliasing={{0}: (6, {})} | custom-call | flops 1500000000 | bytes 2097152 | tf_op jit(solution)/shard_map/spread/pallas_call | solution.py:462
  125.4 0.9 collective-permute-done.12
  126.7 4.2 %spread.13 = (bf16[4,64,64,256]{3,2,1,0:T(8,128)(2,1)}, f32[8,128]{1,0:T(8,128)}) custom-call(bf16[4,64,64,256]{3,2,1,0:T(8,128)(2,1)} %get-tuple-element.31.refs_0_.refs_1_.refs_2_, bf16[4,64,64,256]{3,2,1,0:T(8,128)(2,1)} %get-tuple-element.31.refs_0_.refs_1_.refs_2_, ...), custom_call_target="tpu_custom_call", output_to_operand_aliasing={{0}: (6, {})} | custom-call | flops 1500000000 | bytes 2097152 | tf_op jit(solution)/shard_map/spread/pallas_call | solution.py:462
  131.3 4.1 %spread.14 = (bf16[4,64,64,256]{3,2,1,0:T(8,128)(2,1)}, f32[8,128]{1,0:T(8,128)}) custom-call(bf16[4,64,64,256]{3,2,1,0:T(8,128)(2,1)} %get-tuple-element.31.refs_0_.refs_1_.refs_2_, bf16[4,64,64,256]{3,2,1,0:T(8,128)(2,1)} %get-tuple-element.31.refs_0_.refs_1_.refs_2_, ...), custom_call_target="tpu_custom_call", output_to_operand_aliasing={{0}: (6, {})} | custom-call | flops 1500000000 | bytes 2097152 | tf_op jit(solution)/shard_map/spread/pallas_call | solution.py:462
  136.1 6.6 %collective-permute-start.15 = (f32[136,256]{1,0:T(8,128)S(1)}, f32[136,256]{1,0:T(8,128)S(1)}, u32[]{:S(2)}, u32[]{:S(2)}) collective-permute-start(f32[136,256]{1,0:T(8,128)S(1)} %add.80.mine_ref), channel_id=1, source_target_pairs={{0,1},{1,0},{2,3},{3,2},{4,5},{5,4},{6,7},{7,6},{8,9},{9,8},{10,11... | collective-permute-start | bytes 417800 | tf_op jit(solution)/shard_map/ppermute | solution.py:533
  142.6 4.1 %spread.15 = (bf16[4,64,64,256]{3,2,1,0:T(8,128)(2,1)}, f32[8,128]{1,0:T(8,128)}) custom-call(bf16[4,64,64,256]{3,2,1,0:T(8,128)(2,1)} %get-tuple-element.31.refs_0_.refs_1_.refs_2_, bf16[4,64,64,256]{3,2,1,0:T(8,128)(2,1)} %get-tuple-element.31.refs_0_.refs_1_.refs_2_, ...), custom_call_target="tpu_custom_call", output_to_operand_aliasing={{0}: (6, {})} | custom-call | flops 1500000000 | bytes 2097152 | tf_op jit(solution)/shard_map/spread/pallas_call | solution.py:462
  147.4 1.7 %finish.1 = (f32[9,256]{1,0:T(8,128)}, f32[1,256]{1,0:T(1,128)}, f32[256,256]{1,0:T(8,128)}) custom-call(s32[1]{0:T(128)} %bitcast.30.bit_ref, f32[136,256]{1,0:T(8,128)} %copy-done.2, f32[136,256]{1,0:T(8,128)} %copy-done.3), custom_call_target="tpu_custom_call" | custom-call | tf_op jit(solution)/shard_map/finish/pallas_call | solution.py:504
  (66 shorter events, 6.9 us)
Async XLA Ops:
  0.6 4.8 %copy-start = (s32[1,4]{1,0:T(1,128)S(1)}, s32[1,4]{1,0:T(1,128)}, u32[]{:S(2)}) copy-start(s32[1,4]{1,0:T(1,128)} %param.19) | copy-start | bytes 52
  0.6 15.1 %copy-start.4 = (f32[9,256]{1,0:T(8,128)S(1)}, f32[9,256]{1,0:T(8,128)}, u32[]{:S(2)}) copy-start(f32[9,256]{1,0:T(8,128)} %param.15) | copy-start | bytes 27652
  0.7 15.7 %copy-start.5 = (f32[256]{0:T(256)S(1)}, f32[256]{0:T(256)}, u32[]{:S(2)}) copy-start(f32[256]{0:T(256)} %param.16) | copy-start | bytes 3076
  6.7 65.1 %collective-permute-start = (bf16[4,64,256]{2,1,0:T(8,128)(2,1)S(1)}, bf16[4,64,256]{2,1,0:T(8,128)(2,1)S(1)}, u32[]{:S(2)}, u32[]{:S(2)}) collective-permute-start(bf16[4,64,256]{2,1,0:T(8,128)(2,1)S(1)} %get-tuple-element.68), channel_id=1, source_target_pairs={{0,16},{16,32},{32,48},{48,64},{64,80},{80,96},{96,112},{112,0},{1... | collective-permute-start | bytes 393224 | tf_op jit(solution)/shard_map/ppermute | solution.py:526
  11.2 60.6 %collective-permute-start.1 = (bf16[4,64,256]{2,1,0:T(8,128)(2,1)S(1)}, bf16[4,64,256]{2,1,0:T(8,128)(2,1)S(1)}, u32[]{:S(2)}, u32[]{:S(2)}) collective-permute-start(bf16[4,64,256]{2,1,0:T(8,128)(2,1)S(1)} %get-tuple-element.71), channel_id=1, source_target_pairs={{1,0},{2,1},{3,2},{4,3},{5,4},{6,5},{7,6},{8,7},{9,8},{10,9},{11,1... | collective-permute-start | bytes 393224 | tf_op jit(solution)/shard_map/ppermute | solution.py:527
  12.2 59.7 %collective-permute-start.2 = (bf16[4,64,256]{2,1,0:T(8,128)(2,1)S(1)}, bf16[4,64,256]{2,1,0:T(8,128)(2,1)S(1)}, u32[]{:S(2)}, u32[]{:S(2)}) collective-permute-start(bf16[4,64,256]{2,1,0:T(8,128)(2,1)S(1)} %get-tuple-element.70), channel_id=1, source_target_pairs={{16,0},{32,16},{48,32},{64,48},{80,64},{96,80},{112,96},{0,112},{1... | collective-permute-start | bytes 393224 | tf_op jit(solution)/shard_map/ppermute | solution.py:527
  14.2 57.7 %collective-permute-start.3 = (bf16[4,64,256]{2,1,0:T(8,128)(2,1)S(1)}, bf16[4,64,256]{2,1,0:T(8,128)(2,1)S(1)}, u32[]{:S(2)}, u32[]{:S(2)}) collective-permute-start(bf16[4,64,256]{2,1,0:T(8,128)(2,1)S(1)} %get-tuple-element.69), channel_id=1, source_target_pairs={{0,1},{1,2},{2,3},{3,4},{4,5},{5,6},{6,7},{7,8},{8,9},{9,10},{10,1... | collective-permute-start | bytes 393224 | tf_op jit(solution)/shard_map/ppermute | solution.py:526
  17.0 54.3 %copy-start.6 = (s32[1,4]{1,0:T(1,128)S(1)}, s32[1,4]{1,0:T(1,128)}, u32[]{:S(2)}) copy-start(s32[1,4]{1,0:T(1,128)} %param.20) | copy-start | bytes 52
  83.3 13.3 %collective-permute-start.4 = (bf16[4,64,256]{2,1,0:T(8,128)(2,1)S(1)}, bf16[4,64,256]{2,1,0:T(8,128)(2,1)S(1)}, u32[]{:S(2)}, u32[]{:S(2)}) collective-permute-start(bf16[4,64,256]{2,1,0:T(8,128)(2,1)S(1)} %get-tuple-element.64), channel_id=1, source_target_pairs={{0,16},{16,32},{32,48},{48,64},{64,80},{80,96},{96,112},{112,0},{1... | collective-permute-start | bytes 393224 | tf_op jit(solution)/shard_map/ppermute | solution.py:526
  84.2 12.4 %collective-permute-start.5 = (bf16[4,64,256]{2,1,0:T(8,128)(2,1)S(1)}, bf16[4,64,256]{2,1,0:T(8,128)(2,1)S(1)}, u32[]{:S(2)}, u32[]{:S(2)}) collective-permute-start(bf16[4,64,256]{2,1,0:T(8,128)(2,1)S(1)} %get-tuple-element.67), channel_id=1, source_target_pairs={{1,0},{2,1},{3,2},{4,3},{5,4},{6,5},{7,6},{8,7},{9,8},{10,9},{11,1... | collective-permute-start | bytes 393224 | tf_op jit(solution)/shard_map/ppermute | solution.py:527
  85.9 10.7 %collective-permute-start.6 = (bf16[4,64,256]{2,1,0:T(8,128)(2,1)S(1)}, bf16[4,64,256]{2,1,0:T(8,128)(2,1)S(1)}, u32[]{:S(2)}, u32[]{:S(2)}) collective-permute-start(bf16[4,64,256]{2,1,0:T(8,128)(2,1)S(1)} %get-tuple-element.66), channel_id=1, source_target_pairs={{16,0},{32,16},{48,32},{64,48},{80,64},{96,80},{112,96},{0,112},{1... | collective-permute-start | bytes 393224 | tf_op jit(solution)/shard_map/ppermute | solution.py:527
  91.0 5.6 %collective-permute-start.7 = (bf16[4,64,256]{2,1,0:T(8,128)(2,1)S(1)}, bf16[4,64,256]{2,1,0:T(8,128)(2,1)S(1)}, u32[]{:S(2)}, u32[]{:S(2)}) collective-permute-start(bf16[4,64,256]{2,1,0:T(8,128)(2,1)S(1)} %get-tuple-element.65), channel_id=1, source_target_pairs={{0,1},{1,2},{2,3},{3,4},{4,5},{5,6},{6,7},{7,8},{8,9},{9,10},{10,1... | collective-permute-start | bytes 393224 | tf_op jit(solution)/shard_map/ppermute | solution.py:526
  92.0 10.3 %collective-permute-start.8 = (f32[136,256]{1,0:T(8,128)S(1)}, f32[136,256]{1,0:T(8,128)S(1)}, u32[]{:S(2)}, u32[]{:S(2)}) collective-permute-start(f32[136,256]{1,0:T(8,128)S(1)} %slice_select_fusion), channel_id=1, source_target_pairs={{0,1},{1,0},{2,3},{3,2},{4,5},{5,4},{6,7},{7,6},{8,9},{9,8},{10,11... | collective-permute-start | bytes 417800 | tf_op jit(solution)/shard_map/ppermute | solution.py:533
  98.2 4.2 %copy-start.1 = (f32[272,256]{1,0:T(8,128)S(1)}, f32[272,256]{1,0:T(8,128)}, u32[]{:S(2)}) copy-start(f32[272,256]{1,0:T(8,128)} %get-tuple-element.36) | copy-start | bytes 835588
  102.4 4.3 %collective-permute-start.9 = (f32[136,256]{1,0:T(8,128)S(1)}, f32[136,256]{1,0:T(8,128)S(1)}, u32[]{:S(2)}, u32[]{:S(2)}) collective-permute-start(f32[136,256]{1,0:T(8,128)S(1)} %select_add_fusion), channel_id=1, source_target_pairs={{0,2},{1,3},{2,0},{3,1},{4,6},{5,7},{6,4},{7,5},{8,10},{9,11},{10,... | collective-permute-start | bytes 417800 | tf_op jit(solution)/shard_map/ppermute | solution.py:533
  106.7 6.8 %collective-permute-start.10 = (f32[136,256]{1,0:T(8,128)S(1)}, f32[136,256]{1,0:T(8,128)S(1)}, u32[]{:S(2)}, u32[]{:S(2)}) collective-permute-start(f32[136,256]{1,0:T(8,128)S(1)} %add.75), channel_id=1, source_target_pairs={{0,6},{1,7},{2,4},{3,5},{4,2},{5,3},{6,0},{7,1},{8,14},{9,15},{10,... | collective-permute-start | bytes 417800 | tf_op jit(solution)/shard_map/ppermute | solution.py:533
  113.6 7.6 %collective-permute-start.11 = (f32[136,256]{1,0:T(8,128)S(1)}, f32[136,256]{1,0:T(8,128)S(1)}, u32[]{:S(2)}, u32[]{:S(2)}) collective-permute-start(f32[136,256]{1,0:T(8,128)S(1)} %add.76), channel_id=1, source_target_pairs={{0,8},{1,9},{2,10},{3,11},{4,12},{5,13},{6,14},{7,15},{8,0},{9,1},... | collective-permute-start | bytes 417800 | tf_op jit(solution)/shard_map/ppermute | solution.py:533
  121.2 5.2 %collective-permute-start.12 = (f32[136,256]{1,0:T(8,128)S(1)}, f32[136,256]{1,0:T(8,128)S(1)}, u32[]{:S(2)}, u32[]{:S(2)}) collective-permute-start(f32[136,256]{1,0:T(8,128)S(1)} %add.77), channel_id=1, source_target_pairs={{0,24},{1,25},{2,26},{3,27},{4,28},{5,29},{6,30},{7,31},{8,16},{9,... | collective-permute-start | bytes 417800 | tf_op jit(solution)/shard_map/ppermute | solution.py:533
  126.4 4.5 %collective-permute-start.13 = (f32[136,256]{1,0:T(8,128)S(1)}, f32[136,256]{1,0:T(8,128)S(1)}, u32[]{:S(2)}, u32[]{:S(2)}) collective-permute-start(f32[136,256]{1,0:T(8,128)S(1)} %add.78), channel_id=1, source_target_pairs={{0,32},{1,33},{2,34},{3,35},{4,36},{5,37},{6,38},{7,39},{8,40},{9,... | collective-permute-start | bytes 417800 | tf_op jit(solution)/shard_map/ppermute | solution.py:533
  130.9 5.2 %collective-permute-start.14 = (f32[136,256]{1,0:T(8,128)S(1)}, f32[136,256]{1,0:T(8,128)S(1)}, u32[]{:S(2)}, u32[]{:S(2)}) collective-permute-start(f32[136,256]{1,0:T(8,128)S(1)} %add.79), channel_id=1, source_target_pairs={{0,96},{1,97},{2,98},{3,99},{4,100},{5,101},{6,102},{7,103},{8,104... | collective-permute-start | bytes 417800 | tf_op jit(solution)/shard_map/ppermute | solution.py:533
  136.1 10.7 %copy-start.2 = (f32[136,256]{1,0:T(8,128)}, f32[136,256]{1,0:T(8,128)S(1)}, u32[]{:S(2)}) copy-start(f32[136,256]{1,0:T(8,128)S(1)} %add.80.mine_ref) | copy-start | bytes 417796
  136.1 10.7 %collective-permute-start.15 = (f32[136,256]{1,0:T(8,128)S(1)}, f32[136,256]{1,0:T(8,128)S(1)}, u32[]{:S(2)}, u32[]{:S(2)}) collective-permute-start(f32[136,256]{1,0:T(8,128)S(1)} %add.80.mine_ref), channel_id=1, source_target_pairs={{0,1},{1,0},{2,3},{3,2},{4,5},{5,4},{6,7},{7,6},{8,9},{9,8},{10,11... | collective-permute-start | bytes 417800 | tf_op jit(solution)/shard_map/ppermute | solution.py:533
  146.8 0.6 copy-start.3

commit v3 on v2

v3 whole, which is shorter than its diff:
```python
import functools

import jax
import jax.numpy as jnp
from jax import lax
from jax.experimental import pallas as pl
from jax.experimental.pallas import tpu as pltpu
from jax.sharding import PartitionSpec as P

ROOT = 0.7978845608028654
CUBIC = 0.044715
F32 = jnp.float32
BF16 = jnp.bfloat16
LANES = 128
SUB = 8
PAD = 8


def gelu_pair(h):
    h2 = h * h
    s = 0.5 * jnp.tanh(h * ((CUBIC * ROOT) * h2 + ROOT)) + 0.5
    act = h * s
    slope = s + act * (1.0 - s) * ((6.0 * CUBIC * ROOT) * h2 + 2.0 * ROOT)
    return act, slope


ALPHA = (CUBIC * ROOT) ** (1.0 / 3.0)
KAPPA = ROOT / ALPHA


def gelu_scaled(h):
    h2 = h * h
    t = jnp.tanh(h * (h2 + KAPPA))
    up = 1.0 + t
    act = h * up
    return act, up + act * (1.0 - t) * (3.0 * h2 + KAPPA)


def tap_at(ref, hf, k):
    return jnp.broadcast_to(ref[k : k + 1, hf * LANES : hf * LANES + LANES], (SUB, LANES))


def inner_body(pairs, x_ref, cot_ref, w_ref, tap_ref, bias_ref, gh_ref, pg_ref, dg_ref, u, hide, acc, half_w, *bufs):
    step = pl.program_id(0)
    side = x_ref.shape[1]
    cols = x_ref.shape[2]
    sets = (bufs[0:4], bufs[4:8])

    @pl.when(step == 0)
    def _():
        for hf in range(2):
            for c in range(3):
                w0, w1, w2 = (tap_at(tap_ref, hf, 3 * r + c) * ALPHA for r in range(3))
                u[hf, c] = w0
                u[hf, 3 + c] = (w0 + w1 + w2) * 0.5
                u[hf, 6 + c] = (w0 - w1 + w2) * 0.5
                u[hf, 9 + c] = w2
            u[hf, 12] = tap_at(bias_ref, hf, 0) * ALPHA
        half_w[...] = w_ref[...] * jnp.asarray(0.5, BF16)
        for qt, _, _, _ in sets:
            edge = jnp.zeros((2, pairs, 4, PAD, LANES), F32)
            qt[:, :, :, 0:PAD, :] = edge
            qt[:, :, :, PAD + cols :, :] = edge
        col = lax.broadcasted_iota(jnp.int32, (cols, 2 * LANES), 0)
        keep = jnp.logical_and(col > 0, col < cols - 1)
        hide[0] = jnp.where(keep, 1.0, 0.0).astype(BF16)
        hide[1] = jnp.zeros((cols, 2 * LANES), BF16)
        acc[...] = jnp.zeros_like(acc)
        pg_ref[...] = jnp.zeros_like(pg_ref)

    rows = 2 * pairs

    def outer(buf):
        _, _, act, cot = buf
        pg_ref[...] += lax.dot_general(
            act[...], cot[...], (((0,), (0,)), ((), ())), preferred_element_type=F32
        )

    def chunk(t, buf):
        qt, ga, act, cot = buf
        base = t * rows
        for q in range(rows):
            i = base + q
            kind = jnp.where(jnp.logical_or(i == 0, i == side - 1), 1, 0)
            cot[q * cols : q * cols + cols, :] = cot_ref[0, i] * hide[kind]
        g = lax.dot_general(cot[...], half_w[...], (((1,), (1,)), ((), ())), preferred_element_type=F32)
        ga[0] = g[:, :LANES]
        ga[1] = g[:, LANES:]
        for hf in range(2):
            lanes = slice(hf * LANES, hf * LANES + LANES)
            line = [x_ref[0, jnp.maximum(base - 1, 0), :, lanes].astype(F32)]
            for q in range(rows):
                line.append(x_ref[0, base + q, :, lanes].astype(F32))
            line.append(x_ref[0, jnp.minimum(base + rows, side - 1), :, lanes].astype(F32))
            for p in range(pairs):
                q0, q1, q2, q3 = line[2 * p : 2 * p + 4]
                for k, v in enumerate((q0 - q2, q1 + q2, q2 - q1, q1 - q3)):
                    qt[hf, p, k, PAD : PAD + cols, :] = v
        for hf in range(2):
            lanes = slice(hf * LANES, hf * LANES + LANES)
            sums = [acc[hf, k] for k in range(13)]
            for p in range(pairs):
                for jb in range(cols // 16):
                    halves = []
                    for half in range(2):
                        j = jb * 16 + half * SUB
                        win = [
                            [qt[hf, p, k, PAD - 1 + j + c : PAD - 1 + j + c + SUB, :] for c in range(3)]
                            for k in range(4)
                        ]
                        m = []
                        for k in range(4):
                            v = u[hf, 3 * k] * win[k][0]
                            v = v + u[hf, 3 * k + 1] * win[k][1]
                            m.append(v + u[hf, 3 * k + 2] * win[k][2])
                        both = m[1] + u[hf, 12]
                        found = []
                        for q, h in enumerate((both + m[0] + m[2], both - m[2] - m[3])):
                            a, slope = gelu_scaled(h)
                            at = (2 * p + q) * cols + j
                            found.append((a, ga[hf, at : at + SUB, :] * slope))
                        g0, g1 = found[0][1], found[1][1]
                        plus, minus = g0 + g1, g0 - g1
                        for k, v in enumerate((g0, plus, minus, g1)):
                            for c in range(3):
                                sums[3 * k + c] = sums[3 * k + c] + v * win[k][c]
                        sums[12] = sums[12] + plus
                        halves.append(found)
                    for q in range(2):
                        at = (2 * p + q) * cols + jb * 16
                        act[at : at + 16, lanes] = jnp.concatenate(
                            [halves[0][q][0], halves[1][q][0]], axis=0
                        ).astype(BF16)
                        gh_ref[0, base + 2 * p + q, jb * 16 : jb * 16 + 16, lanes] = jnp.concatenate(
                            [halves[0][q][1], halves[1][q][1]], axis=0
                        ).astype(BF16)
            for k in range(13):
                acc[hf, k] = sums[k]

    def body(t, carry):
        chunk(2 * t, sets[0])
        outer(sets[1])
        chunk(2 * t + 1, sets[1])
        outer(sets[0])
        return carry

    sets[1][2][...] = jnp.zeros_like(sets[1][2])
    sets[1][3][...] = jnp.zeros_like(sets[1][3])
    lax.fori_loop(0, side // (2 * rows), body, 0)
    outer(sets[1])

    @pl.when(step == pl.num_programs(0) - 1)
    def _():
        for hf in range(2):
            for c in range(3):
                d1, d2, d3, d4 = (acc[hf, 3 * k + c] for k in range(4))
                even = 0.5 * (d2 + d3)
                dg_ref[hf, c] = d1 + even
                dg_ref[hf, 3 + c] = 0.5 * (d2 - d3)
                dg_ref[hf, 6 + c] = even - d4
            dg_ref[hf, 9] = acc[hf, 12]
        pg_ref[...] = pg_ref[...] * (0.5 / ALPHA)


PAIRS = 4


def inner_call(state, cotangent, weight, taps, bias):
    batch, side, cols, channels = state.shape
    tile = pl.BlockSpec((1, side, cols, channels), lambda b: (b, 0, 0, 0))
    buf = [
        pltpu.VMEM((2, PAIRS, 4, cols + 2 * PAD, LANES), F32),
        pltpu.VMEM((2, 2 * PAIRS * cols, LANES), F32),
        pltpu.VMEM((2 * PAIRS * cols, channels), BF16),
        pltpu.VMEM((2 * PAIRS * cols, channels), BF16),
    ]
    return pl.pallas_call(
        functools.partial(inner_body, PAIRS),
        grid=(batch,),
        in_specs=[
            tile,
            tile,
            pl.BlockSpec((channels, channels), lambda b: (0, 0)),
            pl.BlockSpec((9, channels), lambda b: (0, 0)),
            pl.BlockSpec((1, channels), lambda b: (0, 0)),
        ],
        out_specs=[
            tile,
            pl.BlockSpec((channels, channels), lambda b: (0, 0)),
            pl.BlockSpec((2, 10, SUB, LANES), lambda b: (0, 0, 0, 0)),
        ],
        out_shape=[
            jax.ShapeDtypeStruct(state.shape, BF16),
            jax.ShapeDtypeStruct((channels, channels), F32),
            jax.ShapeDtypeStruct((2, 10, SUB, LANES), F32),
        ],
        scratch_shapes=[
            pltpu.VMEM((2, 13, SUB, LANES), F32),
            pltpu.VMEM((2, cols, channels), BF16),
            pltpu.VMEM((2, 13, SUB, LANES), F32),
            pltpu.VMEM((channels, channels), BF16),
            *buf,
            *buf,
        ],
        compiler_params=pltpu.CompilerParams(vmem_limit_bytes=57 << 20),
        cost_estimate=pl.CostEstimate(
            flops=40_000_000_000, bytes_accessed=26 << 20, transcendentals=state.size
        ),
        name="inner",
    )(state, cotangent, weight, taps, bias)


DIR_OF_SIDE, SIDE_OF_DIR, FLIPS, MASKS = 0, 4, 8, 12


def from_dir(table, got, s):
    d = table[DIR_OF_SIDE + s]
    rows = got[3][0]
    for k in range(3):
        rows = jnp.where(d == k, got[k][0], rows)
    return rows


def turn(table, s, rows):
    count = rows.shape[0]
    i = lax.broadcasted_iota(jnp.int32, (count, count), 0)
    j = lax.broadcasted_iota(jnp.int32, (count, count), 1)
    source = jnp.where(table[FLIPS + s] == 1, count - 1 - i, i)
    pick = jnp.where(j == source, 1.0, 0.0).astype(BF16)
    return jnp.dot(pick, rows, preferred_element_type=F32).astype(BF16)


def edges_body(table, top_ref, low_ref, left_ref, right_ref, to0, to1, to2, to3, turned):
    last = right_ref.shape[2] - 1
    turned[0] = turn(table, 0, top_ref[0, 0])
    turned[1] = turn(table, 1, right_ref[0].astype(F32)[:, last].astype(BF16))
    turned[2] = turn(table, 2, low_ref[0, 0])
    turned[3] = turn(table, 3, left_ref[0].astype(F32)[:, 0].astype(BF16))
    for d, to in enumerate((to0, to1, to2, to3)):
        to[0] = turned[table[SIDE_OF_DIR + d]]


def edges_call(table, state):
    batch, side, cols, channels = state.shape
    wide = 16
    one = lambda at: pl.BlockSpec((1, 1, cols, channels), lambda b: (b, at, 0, 0))
    column = lambda at: pl.BlockSpec((1, side, wide, channels), lambda b: (b, 0, at, 0))
    facing = pl.BlockSpec((1, side, channels), lambda b: (b, 0, 0))
    return pl.pallas_call(
        edges_body,
        grid=(batch,),
        in_specs=[
            pl.BlockSpec(memory_space=pltpu.SMEM),
            one(0),
            one(side - 1),
            column(0),
            column(cols // wide - 1),
        ],
        out_specs=[facing] * 4,
        out_shape=[jax.ShapeDtypeStruct((batch, side, channels), BF16)] * 4,
        scratch_shapes=[pltpu.VMEM((4, side, channels), BF16)],
        compiler_params=pltpu.CompilerParams(vmem_limit_bytes=57 << 20),
        name="edges",
    )(table, state, state, state, state)


LOW = (0, 1, 3, 0)
HIGH = (1, 2, 2, 3)


def ring_body(
    table, top_ref, low_ref, left_ref, right_ref, ctop_ref, clow_ref, cleft_ref, cright_ref,
    got0, got1, got2, got3, w_ref, tap_ref, bias_ref, pg_ref, dg_ref,
    gr_ref, to0, to1, to2, to3, part_ref, strip, ext, acts, acc, turned,
):
    step = pl.program_id(0)
    side = got0.shape[1]
    got = (got0, got1, got2, got3)
    masks = [table[MASKS + k].astype(F32) for k in range(4)]

    @pl.when(step == 0)
    def _():
        acc[...] = dg_ref[...]
        part_ref[0 : 2 * LANES, :] = pg_ref[...]
        ext[...] = jnp.zeros_like(ext)

    rims = [from_dir(table, got, s).astype(F32) for s in range(4)]
    top = top_ref[0].astype(F32)
    low = low_ref[0].astype(F32)
    left = left_ref[0].astype(F32)
    right = right_ref[0].astype(F32)
    last = left.shape[1] - 1
    end = side - 1

    def corner(k, first, second):
        return (masks[k] * 0.5 * (first + second)).astype(BF16).astype(F32)

    def at(s, i):
        return rims[s][i : i + 1]

    nw = corner(0, at(0, 0), at(3, 0))
    ne = corner(1, at(0, end), at(1, 0))
    se = corner(2, at(1, end), at(2, end))
    sw = corner(3, at(2, 0), at(3, end))
    lines = (
        ((rims[0], nw, ne), (top[0], at(3, 0), at(1, 0)), (top[1], at(3, 1), at(1, 1))),
        (
            (right[:, last - 1], at(0, end - 1), at(2, end - 1)),
            (right[:, last], at(0, end), at(2, end)),
            (rims[1], ne, se),
        ),
        (
            (low[0], at(3, end - 1), at(1, end - 1)),
            (low[1], at(3, end), at(1, end)),
            (rims[2], sw, se),
        ),
        ((rims[3], nw, sw), (left[:, 0], at(0, 0), at(2, 0)), (left[:, 1], at(0, 1), at(2, 1))),
    )
    for s in range(4):
        for a in range(3):
            line, before, after = lines[s][a]
            for hf in range(2):
                lanes = slice(hf * LANES, hf * LANES + LANES)
                strip[s, hf, a, PAD : PAD + side, :] = line[:, lanes]
                strip[s, hf, a, PAD - 1 : PAD, :] = before[:, lanes]
                strip[s, hf, a, PAD + side : PAD + side + 1, :] = after[:, lanes]
    cots = jnp.concatenate(
        [
            ctop_ref[0, 0].astype(F32),
            cright_ref[0].astype(F32)[:, last],
            clow_ref[0, 0].astype(F32),
            cleft_ref[0].astype(F32)[:, 0],
        ],
        axis=0,
    ).astype(BF16)
    ga = lax.dot_general(cots, w_ref[...], (((1,), (1,)), ((), ())), preferred_element_type=F32)
    row = lax.broadcasted_iota(jnp.int32, (side, LANES), 0)
    middle = jnp.logical_and(row > 0, row < end)
    for s in range(4):
        upright = s % 2 == 0
        rim_line = 0 if s in (0, 3) else 2
        for hf in range(2):
            lanes = slice(hf * LANES, hf * LANES + LANES)

            def tap(a, b):
                k = 3 * a + b if upright else 3 * b + a
                return k, tap_ref[k : k + 1, lanes]

            h = jnp.zeros((side, LANES), F32) + bias_ref[0:1, lanes]
            for a in range(3):
                for b in range(3):
                    h = h + tap(a, b)[1] * strip[s, hf, a, PAD - 1 + b : PAD - 1 + b + side, :]
            act, slope = gelu_pair(h)
            g = (ga[s * side : s * side + side, lanes] * slope).astype(BF16)
            gr_ref[s, 0, :, lanes] = g
            g = g.astype(F32)
            counted = g
            if not upright:
                counted = jnp.where(middle, g, 0.0)
                act = jnp.where(middle, act, 0.0)
            acts[s * side : s * side + side, lanes] = act.astype(BF16)
            for a in range(3):
                for b in range(3):
                    k = tap(a, b)[0]
                    term = counted * strip[s, hf, a, PAD - 1 + b : PAD - 1 + b + side, :]
                    acc[hf, k] += jnp.sum(term.reshape(side // SUB, SUB, LANES), axis=0)
            acc[hf, 9] += jnp.sum(counted.reshape(side // SUB, SUB, LANES), axis=0)
            ext[PAD : PAD + side, :] = g
            first, mid, final = (tap(rim_line, b)[1] for b in range(3))
            back = (
                first * ext[PAD + 1 : PAD + 1 + side, :]
                + mid * g
                + final * ext[PAD - 1 : PAD - 1 + side, :]
            )
            back = back + jnp.where(row == 0, (0.5 * masks[LOW[s]]) * first * g, 0.0)
            back = back + jnp.where(row == end, (0.5 * masks[HIGH[s]]) * final * g, 0.0)
            turned[s, :, lanes] = turn(table, s, back.astype(BF16))
    for d, to in enumerate((to0, to1, to2, to3)):
        to[0] = turned[table[SIDE_OF_DIR + d]]
    part_ref[0 : 2 * LANES, :] += lax.dot_general(
        acts[...], cots, (((0,), (0,)), ((), ())), preferred_element_type=F32
    )

    @pl.when(step == pl.num_programs(0) - 1)
    def _():
        part_ref[2 * LANES :, :] = jnp.zeros((16, 2 * LANES), F32)
        for hf in range(2):
            for k in range(10):
                line = jnp.sum(acc[hf, k], axis=0, keepdims=True)
                part_ref[2 * LANES + k : 2 * LANES + k + 1, hf * LANES : hf * LANES + LANES] = line


def ring_call(table, state, cotangent, got, weight, taps, bias, point_inner, depth_inner):
    batch, side, cols, channels = state.shape
    wide = 16
    two = lambda at: pl.BlockSpec((1, 2, cols, channels), lambda b: (b, at, 0, 0))
    one = lambda at: pl.BlockSpec((1, 1, cols, channels), lambda b: (b, at, 0, 0))
    column = lambda at: pl.BlockSpec((1, side, wide, channels), lambda b: (b, 0, at, 0))
    strips = pl.BlockSpec((4, 1, side, channels), lambda b: (0, b, 0, 0))
    facing = pl.BlockSpec((1, side, channels), lambda b: (b, 0, 0))
    far = cols // wide - 1
    return pl.pallas_call(
        ring_body,
        grid=(batch,),
        in_specs=[
            pl.BlockSpec(memory_space=pltpu.SMEM),
            two(0),
            two(side // 2 - 1),
            column(0),
            column(far),
            one(0),
            one(side - 1),
            column(0),
            column(far),
            *[facing] * 4,
            pl.BlockSpec((channels, channels), lambda b: (0, 0)),
            pl.BlockSpec((9, channels), lambda b: (0, 0)),
            pl.BlockSpec((1, channels), lambda b: (0, 0)),
            pl.BlockSpec((channels, channels), lambda b: (0, 0)),
            pl.BlockSpec((2, 10, SUB, LANES), lambda b: (0, 0, 0, 0)),
        ],
        out_specs=[strips, *[facing] * 4, pl.BlockSpec((channels + 16, channels), lambda b: (0, 0))],
        out_shape=[
            jax.ShapeDtypeStruct((4, batch, side, channels), BF16),
            *[jax.ShapeDtypeStruct((batch, side, channels), BF16)] * 4,
            jax.ShapeDtypeStruct((channels + 16, channels), F32),
        ],
        scratch_shapes=[
            pltpu.VMEM((4, 2, 3, cols + 2 * PAD, LANES), F32),
            pltpu.VMEM((cols + 2 * PAD, LANES), F32),
            pltpu.VMEM((4 * side, channels), BF16),
            pltpu.VMEM((2, 10, SUB, LANES), F32),
            pltpu.VMEM((4, side, channels), BF16),
        ],
        compiler_params=pltpu.CompilerParams(vmem_limit_bytes=57 << 20),
        cost_estimate=pl.CostEstimate(
            flops=3_000_000_000, bytes_accessed=12 << 20, transcendentals=state.size // 16
        ),
        name="ring",
    )(table, state, state, state, state, cotangent, cotangent, cotangent, cotangent, *got, weight, taps, bias,
      point_inner, depth_inner)


def spread_body(rows, first, table, gh_ref, above_ref, below_ref, gr_ref, got0, got1, got2, got3, tap_ref, out_ref, token_ref, gf, near, far, ring, back):
    got = (got0, got1, got2, got3)
    side = gr_ref.shape[2]
    cols = gh_ref.shape[2]
    count = gh_ref.shape[1]
    chunks = side // count
    step = (pl.program_id(0) + first) % chunks
    token_ref[...] = jnp.zeros_like(token_ref)
    start = step * count

    @pl.when(jnp.logical_or(pl.program_id(0) == 0, step == 0))
    def _():
        for k, s in enumerate((1, 3)):
            back[k] = from_dir(table, got, s)
        for hf in range(2):
            lanes = slice(hf * LANES, hf * LANES + LANES)
            gf[hf, :, 0:PAD, :] = jnp.zeros((count + 2, PAD, LANES), F32)
            gf[hf, :, PAD + cols : 2 * PAD + cols, :] = jnp.zeros((count + 2, PAD, LANES), F32)
            for k, s in enumerate((1, 3)):
                ring[k, hf, 0:PAD, :] = jnp.zeros((PAD, LANES), F32)
                ring[k, hf, PAD + side :, :] = jnp.zeros((PAD, LANES), F32)
                ring[k, hf, PAD : PAD + side, :] = gr_ref[s, 0, :, lanes].astype(F32)
        near[...] = jnp.zeros_like(near)
        far[...] = jnp.zeros_like(far)

    def put(i, v):
        v = v.astype(F32)
        gf[0, i, PAD : PAD + cols, :] = v[:, :LANES]
        gf[1, i, PAD : PAD + cols, :] = v[:, LANES:]

    put(0, jnp.where(step > 0, above_ref[0, 0], jnp.zeros_like(above_ref[0, 0])))
    put(count + 1, jnp.where(step < chunks - 1, below_ref[0, 0], jnp.zeros_like(below_ref[0, 0])))
    for i in range(count):
        put(i + 1, gh_ref[0, i])
    cut = [back[k, pl.ds(pl.multiple_of(start, count), count), :].astype(F32) for k in range(2)]
    for hf in range(2):
        lanes = slice(hf * LANES, hf * LANES + LANES)
        for k, j in ((0, PAD + cols - 1), (1, PAD)):
            own = ring[k, hf, pl.ds(pl.multiple_of(PAD + start, SUB), count), :]
            gf[hf, 1 : count + 1, j : j + 1, :] = own.reshape(count, 1, LANES)
            gf[hf, 0, j : j + 1, :] = ring[k, hf, pl.ds(PAD + start - 1, 1), :]
            gf[hf, count + 1, j : j + 1, :] = ring[k, hf, pl.ds(PAD + start + count, 1), :]
        near[hf, :, 0:1, :] = cut[1][:, lanes].reshape(count, 1, LANES)
        far[hf, :, SUB - 1 : SUB, :] = cut[0][:, lanes].reshape(count, 1, LANES)

    def line(i, s):
        v = gr_ref[s, 0].astype(F32)
        for hf in range(2):
            gf[hf, i, PAD : PAD + cols, :] = v[:, hf * LANES : hf * LANES + LANES]

    @pl.when(step == 0)
    def _():
        line(1, 0)

    @pl.when(step == chunks - 1)
    def _():
        line(count, 2)

    for hf in range(2):
        lanes = slice(hf * LANES, hf * LANES + LANES)
        taps = [tap_at(tap_ref, hf, k) for k in range(9)]
        for jb in range(cols // 16):

            def body(it, carry):
                i = it * rows
                win = {}
                for q in range(rows):
                    pair = []
                    for half in range(2):
                        j = PAD + jb * 16 + half * SUB
                        total = None
                        for r in range(3):
                            for c in range(3):
                                at = (q + 2 - r, 2 - c, half)
                                if at not in win:
                                    win[at] = gf[hf, i + at[0], j - 1 + at[1] : j - 1 + at[1] + SUB, :]
                                term = taps[3 * r + c] * win[at]
                                total = term if total is None else total + term
                        if jb == 0 and half == 0:
                            total = total + near[hf, i + q]
                        if jb == cols // 16 - 1 and half == 1:
                            total = total + far[hf, i + q]
                        pair.append(total)
                    out_ref[0, i + q, jb * 16 : jb * 16 + 16, lanes] = jnp.concatenate(pair, axis=0).astype(BF16)
                return carry

            lax.fori_loop(0, count // rows, body, 0)

    def add(i, s):
        out_ref[0, i] = (out_ref[0, i].astype(F32) + from_dir(table, got, s).astype(F32)).astype(BF16)

    @pl.when(step == 0)
    def _():
        add(0, 0)

    @pl.when(step == chunks - 1)
    def _():
        add(count - 1, 2)


CHUNK = 16


def spread_call(first, steps, table, grad, ring, got, taps, into):
    batch, side, cols, channels = grad.shape
    chunks = side // CHUNK
    high = side - 1
    at = lambda i: ((i + first) // chunks, (i + first) % chunks)
    strips = pl.BlockSpec((4, 1, side, channels), lambda i: (0, at(i)[0], 0, 0))
    facing = pl.BlockSpec((1, side, channels), lambda i: (at(i)[0], 0, 0))
    rows = pl.BlockSpec((1, CHUNK, cols, channels), lambda i: (*at(i), 0, 0))
    in_specs = [
        pl.BlockSpec(memory_space=pltpu.SMEM),
        rows,
        pl.BlockSpec((1, 1, cols, channels), lambda i: (at(i)[0], jnp.maximum(at(i)[1] * CHUNK - 1, 0), 0, 0)),
        pl.BlockSpec((1, 1, cols, channels), lambda i: (at(i)[0], jnp.minimum(at(i)[1] * CHUNK + CHUNK, high), 0, 0)),
        strips,
        *[facing] * 4,
        pl.BlockSpec((9, channels), lambda i: (0, 0)),
    ]
    operands = [table, grad, grad, grad, ring, *got, taps]
    aliases = {}
    if into is not None:
        aliases = {len(operands): 0}
        in_specs.append(pl.BlockSpec(memory_space=pl.ANY))
        operands.append(into)

    def body(*refs):
        spread_body(4, first, *refs[:10], *refs[len(operands) :])

    return pl.pallas_call(
        body,
        grid=(steps,),
        in_specs=in_specs,
        out_specs=[rows, pl.BlockSpec((SUB, LANES), lambda i: (0, 0))],
        out_shape=[jax.ShapeDtypeStruct(grad.shape, BF16), jax.ShapeDtypeStruct((SUB, LANES), F32)],
        scratch_shapes=[
            pltpu.VMEM((2, CHUNK + 2, cols + 2 * PAD, LANES), F32),
            pltpu.VMEM((2, CHUNK, SUB, LANES), F32),
            pltpu.VMEM((2, CHUNK, SUB, LANES), F32),
            pltpu.VMEM((2, 2, side + 2 * PAD, LANES), F32),
            pltpu.VMEM((2, side, channels), BF16),
        ],
        input_output_aliases=aliases,
        compiler_params=pltpu.CompilerParams(vmem_limit_bytes=57 << 20),
        cost_estimate=pl.CostEstimate(
            flops=750_000_000 * steps, bytes_accessed=grad.size * 4 * steps // (batch * chunks), transcendentals=0
        ),
        name="spread",
    )(*operands)


def finish_body(scale, bit_ref, mine_ref, other_ref, dg_ref, bg_ref, pg_ref):
    rows = mine_ref.shape[0]
    channels = pg_ref.shape[0]
    own = mine_ref[...] * scale
    far = other_ref[...] * scale
    first = bit_ref[0] == 0
    low = jnp.where(first, own, far)
    high = jnp.where(first, far, own)
    pg_ref[0:rows, :] = low
    pg_ref[rows:channels, :] = high[: channels - rows]
    tail = high[channels - rows :]
    dg_ref[...] = tail[0:9]
    bg_ref[...] = tail[9:10]


def finish_call(scale, bit, mine, other):
    channels = mine.shape[1]
    vmem = pl.BlockSpec(memory_space=pltpu.VMEM)
    return pl.pallas_call(
        functools.partial(finish_body, scale),
        in_specs=[pl.BlockSpec(memory_space=pltpu.SMEM), vmem, vmem],
        out_specs=[vmem, vmem, vmem],
        out_shape=[
            jax.ShapeDtypeStruct((9, channels), F32),
            jax.ShapeDtypeStruct((1, channels), F32),
            jax.ShapeDtypeStruct((channels, channels), F32),
        ],
        name="finish",
    )(bit, mine, other)


def exchange(facing):
    got = [None] * 4
    for axis, low, high in (("face", 0, 2), ("tile", 3, 1)):
        count = lax.axis_size(axis)
        up = [(i, (i + 1) % count) for i in range(count)]
        down = [(target, source) for source, target in up]
        got[low] = lax.ppermute(facing[high], axis, up)
        got[high] = lax.ppermute(facing[low], axis, down)
    return got


def swap(value, mask):
    devices = lax.axis_size("face") * lax.axis_size("tile")
    return lax.ppermute(value, ("face", "tile"), [(i, i ^ mask) for i in range(devices)])


def after(value, *others):
    return lax.optimization_barrier((value, *others))[0]


def shards(
    state, cotangent, depth_weight, depth_bias, point_weight, tile_links, link_sides, link_flips, corner_masks
):
    batch, side, cols, channels = state.shape
    face_count = lax.axis_size("face")
    tile_count = lax.axis_size("tile")
    face_pos = lax.axis_index("face")
    tile_pos = lax.axis_index("tile")
    toward = jnp.stack(
        [
            (face_pos - 1) % face_count * tile_count + tile_pos,
            face_pos * tile_count + (tile_pos + 1) % tile_count,
            (face_pos + 1) % face_count * tile_count + tile_pos,
            face_pos * tile_count + (tile_pos - 1) % tile_count,
        ]
    )
    matched = tile_links[0][:, None] == toward[None, :]
    counter = jnp.arange(4, dtype=jnp.int32)
    dir_of_side = jnp.sum(jnp.where(matched, counter[None, :], 0), axis=1)
    side_of_dir = jnp.sum(jnp.where(matched, counter[:, None], 0), axis=0)
    table = jnp.concatenate([dir_of_side, side_of_dir, link_flips[0], corner_masks[0]])
    bias = depth_bias.reshape(1, channels)
    got = exchange(edges_call(table, state))
    grad, point_inner, depth_inner = inner_call(state, cotangent, point_weight, depth_weight, bias)
    ring, *facing, part = ring_call(
        table, state, cotangent, got, point_weight, depth_weight, bias, point_inner, depth_inner
    )
    incoming = exchange(facing)

    core = tile_pos % 2
    half = part.shape[0] // 2
    low, high = part[:half], part[half:]
    mine = jnp.where(core == 0, low, high)
    sent = jnp.where(core == 0, high, low)
    first, field_grad = 0, None
    for stage, (mask_bits, steps) in enumerate(
        ((1, 0), (2, 2), (6, 3), (8, 2), (24, 3), (32, 2), (96, 2), (1, 2))
    ):
        got = swap(sent if stage == 0 else mine, mask_bits)
        if steps:
            held = after(depth_weight, mine)
            field_grad, token = spread_call(first, steps, table, grad, ring, incoming, held, field_grad)
            got = after(got, token)
            first += steps
        if stage < 7:
            mine = mine + got
    scale = float(batch * side * cols * face_count * tile_count) ** -0.5
    depth_grad, bias_grad, point_grad = finish_call(scale, core.reshape(1), mine, got)
    return field_grad, depth_grad, bias_grad.reshape(channels), point_grad


def solution(mesh):
    tiles = P(None, "face", "tile", None)
    table = P(("face", "tile"), None)
    return jax.shard_map(
        shards,
        mesh=mesh,
        in_specs=(tiles, tiles, P(), P(), P(), table, table, table, table),
        out_specs=(tiles, P(), P(), P()),
        check_vma=False,
    )
```

time: 150 us -> 125 us (0.83)
  Pallas kernels: 96.8 us -> 83.7 us
  local copies, waits for them, and re-layouts: 9.72 us -> 2.04 us
  starting transfers between devices: 34.9 us -> 30.4 us
    pallas_call x9, Pallas kernels: 87.6 us -> 73.8 us  [the longest x1 37.5 us: inner_call(): pl.pallas_call(functools.partial(inner_body, PAIRS), grid=(batch,), in_sp...]
    gather x5 -> x0, local copies, waits for them, and re-layouts: 4 us -> none  [the longest x2 2.2 us: exchange(): facing = jnp.take(by_side, side_of_dir, axis=0)]
    ppermute x8, starting transfers between devices: 18.1 us -> 14.3 us  [swap(): lax.ppermute(value, ('face', 'tile'), [(i, i ^ mask) for i in range(devic...]
    ppermute x4, waiting for transfers between devices: 0.01 us -> 2.7 us  [exchange(): got[low] = lax.ppermute(facing[high], axis, up)]
    select_n x8 -> x0, other arithmetic: 2.3 us -> none  [the longest x3 1.81 us: exchange(): return jnp.take(jnp.stack(got, axis=0), dir_of_side, axis=0)]
    slice x1 -> x0, local copies, waits for them, and re-layouts: 1.97 us -> none  [shards(): state[:, :, -1]]
    ppermute x8, waiting for transfers between devices: 1.55 us -> 0.02 us  [swap(): lax.ppermute(value, ('face', 'tile'), [(i, i ^ mask) for i in range(devic...]
  transfers between devices with their start and end apart: 16 -> 16, of which waited for: 2 -> 2; matrix products, arithmetic and copies ran while one was open for 3% -> 1% of each run, Pallas kernels for 59% -> 56%
where the time goes in v3:
time: 125 us; the launch traced here: 124 us
  Pallas kernels  83.7 us (67%)
  starting transfers between devices  30.4 us (24%)
  other arithmetic  4.32 us (3%)
  waiting for transfers between devices  2.73 us (2%)
  local copies, waits for them, and re-layouts  2.04 us (2%)
    pallas_call x1, Pallas kernels, inner_call(): pl.pallas_call(functools.partial(inner_body, PAIRS), grid=(batch,), in_sp...  37.5 us
    pallas_call x7, Pallas kernels, spread_call(): pl.pallas_call(body, grid=(steps,), in_specs=in_specs, out_specs=[rows, p...  31.8 us
    ppermute x8, starting transfers between devices, swap(): lax.ppermute(value, ('face', 'tile'), [(i, i ^ mask) for i in range(devic...  14.3 us
    ppermute x4, starting transfers between devices, exchange(): got[high] = lax.ppermute(facing[low], axis, down)  8.39 us
    pallas_call x1, Pallas kernels, ring_call(): pl.pallas_call(ring_body, grid=(batch,), in_specs=[pl.BlockSpec(memory_sp...  8.22 us
    ppermute x4, starting transfers between devices, exchange(): got[low] = lax.ppermute(facing[high], axis, up)  7.71 us
    pallas_call x1, Pallas kernels, edges_call(): pl.pallas_call(edges_body, grid=(batch,), in_specs=[pl.BlockSpec(memory_s...  4.45 us
    ppermute x4, waiting for transfers between devices, exchange(): got[low] = lax.ppermute(facing[high], axis, up)  2.7 us
  transfers between devices with their start and end apart: 16, of which 2 were waited for; matrix products, arithmetic and copies ran while one was open for 1% of the time, Pallas kernels for 56%

profile of v3, /device:TPU:1, one launch (start us, length us, event | category | flops | bytes accessed | tf_op | source)
XLA Modules:
  0.0 124.1 jit_solution(1344974806215595796)
XLA Ops:
  0.8 0.8 fusion
  1.6 1.3 %pad_add_fusion.1.table.refs_0_ = s32[16]{0:T(128)} fusion(s32[4]{0:T(128)} %bitcast.12, s32[4]{0:T(128)} %bitcast.13, s32[4]{0:T(128)S(1)} %get-tuple-element.65, s32[4]{0:T(128)S(1)} %get-tuple-element.64), kind=kLoop, calls=%fused_computation.7 | loop fusion | flops 48 | bytes 128 | tf_op jit(solution)/shard_map/concatenate | solution.py:667
  2.9 4.4 %edges.1 = (bf16[4,64,256]{2,1,0:T(8,128)(2,1)}, bf16[4,64,256]{2,1,0:T(8,128)(2,1)}, bf16[4,64,256]{2,1,0:T(8,128)(2,1)}, bf16[4,64,256]{2,1,0:T(8,128)(2,1)}) custom-call(s32[16]{0:T(128)} %pad_add_fusion.1.table.refs_0_, bf16[4,64,64,256]{3,2,1,0:T(8,128)(2,1)} %right_ref.3, bf16[4,64,64,256]{3,2,1,0:T(8,128)(2,1)} %right_ref.3, ...), custom_call_target="tpu_custom_call" | custom-call | tf_op jit(solution)/shard_map/edges/pallas_call | solution.py:249
  7.3 4.5 %collective-permute-start = (bf16[4,64,256]{2,1,0:T(8,128)(2,1)}, bf16[4,64,256]{2,1,0:T(8,128)(2,1)S(1)}, u32[]{:S(2)}, u32[]{:S(2)}) collective-permute-start(bf16[4,64,256]{2,1,0:T(8,128)(2,1)} %get-tuple-element.35), channel_id=1, source_target_pairs={{0,16},{16,32},{32,48},{48,64},{64,80},{80,96},{96,112},{112,0},{1... | collective-permute-start | bytes 393224 | tf_op jit(solution)/shard_map/ppermute | solution.py:633
  11.8 1.0 collective-permute-start.1
  12.8 2.0 %collective-permute-start.2 = (bf16[4,64,256]{2,1,0:T(8,128)(2,1)}, bf16[4,64,256]{2,1,0:T(8,128)(2,1)S(1)}, u32[]{:S(2)}, u32[]{:S(2)}) collective-permute-start(bf16[4,64,256]{2,1,0:T(8,128)(2,1)} %get-tuple-element.37), channel_id=1, source_target_pairs={{16,0},{32,16},{48,32},{64,48},{80,64},{96,80},{112,96},{0,112},{1... | collective-permute-start | bytes 393224 | tf_op jit(solution)/shard_map/ppermute | solution.py:634
  14.8 1.5 %collective-permute-start.3 = (bf16[4,64,256]{2,1,0:T(8,128)(2,1)}, bf16[4,64,256]{2,1,0:T(8,128)(2,1)S(1)}, u32[]{:S(2)}, u32[]{:S(2)}) collective-permute-start(bf16[4,64,256]{2,1,0:T(8,128)(2,1)} %get-tuple-element.38), channel_id=1, source_target_pairs={{0,1},{1,2},{2,3},{3,4},{4,5},{5,6},{6,7},{7,8},{8,9},{9,10},{10,1... | collective-permute-start | bytes 393224 | tf_op jit(solution)/shard_map/ppermute | solution.py:633
  16.3 37.5 %inner.1 = (bf16[4,64,64,256]{3,2,1,0:T(8,128)(2,1)}, f32[256,256]{1,0:T(8,128)}, f32[2,10,8,128]{3,2,1,0:T(8,128)}) custom-call(bf16[4,64,64,256]{3,2,1,0:T(8,128)(2,1)} %right_ref.3, bf16[4,64,64,256]{3,2,1,0:T(8,128)(2,1)} %cright_ref.1, bf16[256,256]{1,0:T(8,128)(2,1)} %w_ref.3, f32[9,256]{1,0:T(8,128)} %refs_9_.6, f32[1,256]{1,0:T(1,128)} %bitcast.10), custom_call_target="tpu_custom_call" | custom-call | flops 40000000000 | bytes 27262976 | tf_op jit(solution)/shard_map/inner/pallas_call | solution.py:177
  53.9 0.6 copy-done.6
  54.6 8.2 %ring.1 = (bf16[4,4,64,256]{3,2,1,0:T(8,128)(2,1)}, bf16[4,64,256]{2,1,0:T(8,128)(2,1)}, bf16[4,64,256]{2,1,0:T(8,128)(2,1)}, bf16[4,64,256]{2,1,0:T(8,128)(2,1)...) custom-call(s32[16]{0:T(128)} %pad_add_fusion.1.table.refs_0_, bf16[4,64,64,256]{3,2,1,0:T(8,128)(2,1)} %right_ref.3, ...), custom_call_target="tpu_custom_call" | custom-call | flops 3000000000 | bytes 12582912 | tf_op jit(solution)/shard_map/ring/pallas_call | solution.py:402
  62.9 1.0 slice_select_fusion
  63.9 2.5 %collective-permute-start.8 = (f32[136,256]{1,0:T(8,128)S(1)}, f32[136,256]{1,0:T(8,128)S(1)}, u32[]{:S(2)}, u32[]{:S(2)}) collective-permute-start(f32[136,256]{1,0:T(8,128)S(1)} %slice_select_fusion), channel_id=1, source_target_pairs={{0,1},{1,0},{2,3},{3,2},{4,5},{5,4},{6,7},{7,6},{8,9},{9,8},{10,11... | collective-permute-start | bytes 417800 | tf_op jit(solution)/shard_map/ppermute | solution.py:640
  66.7 5.1 %collective-permute-start.6 = (bf16[4,64,256]{2,1,0:T(8,128)(2,1)}, bf16[4,64,256]{2,1,0:T(8,128)(2,1)S(1)}, u32[]{:S(2)}, u32[]{:S(2)}) collective-permute-start(bf16[4,64,256]{2,1,0:T(8,128)(2,1)} %get-tuple-element.44), channel_id=1, source_target_pairs={{16,0},{32,16},{48,32},{64,48},{80,64},{96,80},{112,96},{0,112},{1... | collective-permute-start | bytes 393224 | tf_op jit(solution)/shard_map/ppermute | solution.py:634
  71.8 1.7 %collective-permute-start.7 = (bf16[4,64,256]{2,1,0:T(8,128)(2,1)}, bf16[4,64,256]{2,1,0:T(8,128)(2,1)S(1)}, u32[]{:S(2)}, u32[]{:S(2)}) collective-permute-start(bf16[4,64,256]{2,1,0:T(8,128)(2,1)} %get-tuple-element.45), channel_id=1, source_target_pairs={{0,1},{1,2},{2,3},{3,4},{4,5},{5,6},{6,7},{7,8},{8,9},{9,10},{10,1... | collective-permute-start | bytes 393224 | tf_op jit(solution)/shard_map/ppermute | solution.py:633
  73.4 1.0 select_add_fusion
  74.5 0.7 collective-permute-done.4.refs_5_
  75.2 2.0 %collective-permute-done.7.refs_8_ = bf16[4,64,256]{2,1,0:T(8,128)(2,1)S(1)} collective-permute-done((bf16[4,64,256]{2,1,0:T(8,128)(2,1)}, bf16[4,64,256]{2,1,0:T(8,128)(2,1)S(1)}, u32[]{:S(2)}, u32[]{:S(2)}) %collective-permute-start.7) | collective-permute-done | bytes 131104 | tf_op jit(solution)/shard_map/ppermute | solution.py:633
  77.3 0.6 copy-done.3
  77.9 4.2 %spread.7 = (bf16[4,64,64,256]{3,2,1,0:T(8,128)(2,1)}, f32[8,128]{1,0:T(8,128)}) custom-call(s32[16]{0:T(128)} %pad_add_fusion.1.table.refs_0_, bf16[4,64,64,256]{3,2,1,0:T(8,128)(2,1)} %get-tuple-element.34.refs_1_.refs_2_.refs_3_, bf16[4,64,64,256]{3,2,1,0:T(8,128)(2,1)} %get-tuple-element.34.refs_1_.refs_2_.refs_3_, ...), custom_call_target="tpu_custom_call" | custom-call | flops 1500000000 | bytes 2097152 | tf_op jit(solution)/shard_map/spread/pallas_call | solution.py:574
  82.2 4.5 %collective-permute-start.10 = (f32[136,256]{1,0:T(8,128)S(1)}, f32[136,256]{1,0:T(8,128)S(1)}, u32[]{:S(2)}, u32[]{:S(2)}) collective-permute-start(f32[136,256]{1,0:T(8,128)S(1)} %add.69), channel_id=1, source_target_pairs={{0,6},{1,7},{2,4},{3,5},{4,2},{5,3},{6,0},{7,1},{8,14},{9,15},{10,... | collective-permute-start | bytes 417800 | tf_op jit(solution)/shard_map/ppermute | solution.py:640
  86.6 5.5 %spread.8 = (bf16[4,64,64,256]{3,2,1,0:T(8,128)(2,1)}, f32[8,128]{1,0:T(8,128)}) custom-call(s32[16]{0:T(128)} %pad_add_fusion.1.table.refs_0_, bf16[4,64,64,256]{3,2,1,0:T(8,128)(2,1)} %get-tuple-element.34.refs_1_.refs_2_.refs_3_, bf16[4,64,64,256]{3,2,1,0:T(8,128)(2,1)} %get-tuple-element.34.refs_1_.refs_2_.refs_3_, ...), custom_call_target="tpu_custom_call", output_to_operand_aliasing={{0}: (10, {})} | custom-call | flops 2249999872 | bytes 3145728 | tf_op jit(solution)/shard_map/spread/pallas_call | solution.py:574
  92.1 0.7 collective-permute-start.11
  92.8 4.2 %spread.9 = (bf16[4,64,64,256]{3,2,1,0:T(8,128)(2,1)}, f32[8,128]{1,0:T(8,128)}) custom-call(s32[16]{0:T(128)} %pad_add_fusion.1.table.refs_0_, bf16[4,64,64,256]{3,2,1,0:T(8,128)(2,1)} %get-tuple-element.34.refs_1_.refs_2_.refs_3_, bf16[4,64,64,256]{3,2,1,0:T(8,128)(2,1)} %get-tuple-element.34.refs_1_.refs_2_.refs_3_, ...), custom_call_target="tpu_custom_call", output_to_operand_aliasing={{0}: (10, {})} | custom-call | flops 1500000000 | bytes 2097152 | tf_op jit(solution)/shard_map/spread/pallas_call | solution.py:574
  97.1 5.4 %spread.10 = (bf16[4,64,64,256]{3,2,1,0:T(8,128)(2,1)}, f32[8,128]{1,0:T(8,128)}) custom-call(s32[16]{0:T(128)} %pad_add_fusion.1.table.refs_0_, bf16[4,64,64,256]{3,2,1,0:T(8,128)(2,1)} %get-tuple-element.34.refs_1_.refs_2_.refs_3_, bf16[4,64,64,256]{3,2,1,0:T(8,128)(2,1)} %get-tuple-element.34.refs_1_.refs_2_.refs_3_, ...), custom_call_target="tpu_custom_call", output_to_operand_aliasing={{0}: (10, {})} | custom-call | flops 2249999872 | bytes 3145728 | tf_op jit(solution)/shard_map/spread/pallas_call | solution.py:574
  102.5 1.1 collective-permute-start.13
  103.6 4.2 %spread.11 = (bf16[4,64,64,256]{3,2,1,0:T(8,128)(2,1)}, f32[8,128]{1,0:T(8,128)}) custom-call(s32[16]{0:T(128)} %pad_add_fusion.1.table.refs_0_, bf16[4,64,64,256]{3,2,1,0:T(8,128)(2,1)} %get-tuple-element.34.refs_1_.refs_2_.refs_3_, bf16[4,64,64,256]{3,2,1,0:T(8,128)(2,1)} %get-tuple-element.34.refs_1_.refs_2_.refs_3_, ...), custom_call_target="tpu_custom_call", output_to_operand_aliasing={{0}: (10, {})} | custom-call | flops 1500000000 | bytes 2097152 | tf_op jit(solution)/shard_map/spread/pallas_call | solution.py:574
  107.8 1.9 %collective-permute-start.14 = (f32[136,256]{1,0:T(8,128)S(1)}, f32[136,256]{1,0:T(8,128)S(1)}, u32[]{:S(2)}, u32[]{:S(2)}) collective-permute-start(f32[136,256]{1,0:T(8,128)S(1)} %add.73), channel_id=1, source_target_pairs={{0,96},{1,97},{2,98},{3,99},{4,100},{5,101},{6,102},{7,103},{8,104... | collective-permute-start | bytes 417800 | tf_op jit(solution)/shard_map/ppermute | solution.py:640
  109.7 4.2 %spread.12 = (bf16[4,64,64,256]{3,2,1,0:T(8,128)(2,1)}, f32[8,128]{1,0:T(8,128)}) custom-call(s32[16]{0:T(128)} %pad_add_fusion.1.table.refs_0_, bf16[4,64,64,256]{3,2,1,0:T(8,128)(2,1)} %get-tuple-element.34.refs_1_.refs_2_.refs_3_, bf16[4,64,64,256]{3,2,1,0:T(8,128)(2,1)} %get-tuple-element.34.refs_1_.refs_2_.refs_3_, ...), custom_call_target="tpu_custom_call", output_to_operand_aliasing={{0}: (10, {})} | custom-call | flops 1500000000 | bytes 2097152 | tf_op jit(solution)/shard_map/spread/pallas_call | solution.py:574
  113.9 3.6 %collective-permute-start.15 = (f32[136,256]{1,0:T(8,128)S(1)}, f32[136,256]{1,0:T(8,128)S(1)}, u32[]{:S(2)}, u32[]{:S(2)}) collective-permute-start(f32[136,256]{1,0:T(8,128)S(1)} %add.74.mine_ref), channel_id=1, source_target_pairs={{0,1},{1,0},{2,3},{3,2},{4,5},{5,4},{6,7},{7,6},{8,9},{9,8},{10,11... | collective-permute-start | bytes 417800 | tf_op jit(solution)/shard_map/ppermute | solution.py:640
  117.5 4.2 %spread.13 = (bf16[4,64,64,256]{3,2,1,0:T(8,128)(2,1)}, f32[8,128]{1,0:T(8,128)}) custom-call(s32[16]{0:T(128)} %pad_add_fusion.1.table.refs_0_, bf16[4,64,64,256]{3,2,1,0:T(8,128)(2,1)} %get-tuple-element.34.refs_1_.refs_2_.refs_3_, bf16[4,64,64,256]{3,2,1,0:T(8,128)(2,1)} %get-tuple-element.34.refs_1_.refs_2_.refs_3_, ...), custom_call_target="tpu_custom_call", output_to_operand_aliasing={{0}: (10, {})} | custom-call | flops 1500000000 | bytes 2097152 | tf_op jit(solution)/shard_map/spread/pallas_call | solution.py:574
  121.7 0.6 copy-done.5
  122.4 1.7 %finish.1 = (f32[9,256]{1,0:T(8,128)}, f32[1,256]{1,0:T(1,128)}, f32[256,256]{1,0:T(8,128)}) custom-call(s32[1]{0:T(128)} %bitcast.8.bit_ref, f32[136,256]{1,0:T(8,128)} %copy-done.4, f32[136,256]{1,0:T(8,128)} %copy-done.5), custom_call_target="tpu_custom_call" | custom-call | tf_op jit(solution)/shard_map/finish/pallas_call | solution.py:614
  (42 shorter events, 0.9 us)
Async XLA Ops:
  7.3 46.5 %collective-permute-start = (bf16[4,64,256]{2,1,0:T(8,128)(2,1)}, bf16[4,64,256]{2,1,0:T(8,128)(2,1)S(1)}, u32[]{:S(2)}, u32[]{:S(2)}) collective-permute-start(bf16[4,64,256]{2,1,0:T(8,128)(2,1)} %get-tuple-element.35), channel_id=1, source_target_pairs={{0,16},{16,32},{32,48},{48,64},{64,80},{80,96},{96,112},{112,0},{1... | collective-permute-start | bytes 393224 | tf_op jit(solution)/shard_map/ppermute | solution.py:633
  11.8 42.0 %collective-permute-start.1 = (bf16[4,64,256]{2,1,0:T(8,128)(2,1)}, bf16[4,64,256]{2,1,0:T(8,128)(2,1)S(1)}, u32[]{:S(2)}, u32[]{:S(2)}) collective-permute-start(bf16[4,64,256]{2,1,0:T(8,128)(2,1)} %get-tuple-element.36), channel_id=1, source_target_pairs={{1,0},{2,1},{3,2},{4,3},{5,4},{6,5},{7,6},{8,7},{9,8},{10,9},{11,1... | collective-permute-start | bytes 393224 | tf_op jit(solution)/shard_map/ppermute | solution.py:634
  12.8 41.1 %collective-permute-start.2 = (bf16[4,64,256]{2,1,0:T(8,128)(2,1)}, bf16[4,64,256]{2,1,0:T(8,128)(2,1)S(1)}, u32[]{:S(2)}, u32[]{:S(2)}) collective-permute-start(bf16[4,64,256]{2,1,0:T(8,128)(2,1)} %get-tuple-element.37), channel_id=1, source_target_pairs={{16,0},{32,16},{48,32},{64,48},{80,64},{96,80},{112,96},{0,112},{1... | collective-permute-start | bytes 393224 | tf_op jit(solution)/shard_map/ppermute | solution.py:634
  14.8 39.1 %collective-permute-start.3 = (bf16[4,64,256]{2,1,0:T(8,128)(2,1)}, bf16[4,64,256]{2,1,0:T(8,128)(2,1)S(1)}, u32[]{:S(2)}, u32[]{:S(2)}) collective-permute-start(bf16[4,64,256]{2,1,0:T(8,128)(2,1)} %get-tuple-element.38), channel_id=1, source_target_pairs={{0,1},{1,2},{2,3},{3,4},{4,5},{5,6},{6,7},{7,8},{8,9},{9,10},{10,1... | collective-permute-start | bytes 393224 | tf_op jit(solution)/shard_map/ppermute | solution.py:633
  53.8 0.7 copy-start.6
  53.9 0.7 copy-start.7
  53.9 0.7 copy-start.8
  53.9 0.7 copy-start.9
  63.9 9.6 %collective-permute-start.8 = (f32[136,256]{1,0:T(8,128)S(1)}, f32[136,256]{1,0:T(8,128)S(1)}, u32[]{:S(2)}, u32[]{:S(2)}) collective-permute-start(f32[136,256]{1,0:T(8,128)S(1)} %slice_select_fusion), channel_id=1, source_target_pairs={{0,1},{1,0},{2,3},{3,2},{4,5},{5,4},{6,7},{7,6},{8,9},{9,8},{10,11... | collective-permute-start | bytes 417800 | tf_op jit(solution)/shard_map/ppermute | solution.py:640
  66.3 8.9 %collective-permute-start.4 = (bf16[4,64,256]{2,1,0:T(8,128)(2,1)}, bf16[4,64,256]{2,1,0:T(8,128)(2,1)S(1)}, u32[]{:S(2)}, u32[]{:S(2)}) collective-permute-start(bf16[4,64,256]{2,1,0:T(8,128)(2,1)} %get-tuple-element.42), channel_id=1, source_target_pairs={{0,16},{16,32},{32,48},{48,64},{64,80},{80,96},{96,112},{112,0},{1... | collective-permute-start | bytes 393224 | tf_op jit(solution)/shard_map/ppermute | solution.py:633
  66.3 8.9 %collective-permute-start.5 = (bf16[4,64,256]{2,1,0:T(8,128)(2,1)}, bf16[4,64,256]{2,1,0:T(8,128)(2,1)S(1)}, u32[]{:S(2)}, u32[]{:S(2)}) collective-permute-start(bf16[4,64,256]{2,1,0:T(8,128)(2,1)} %get-tuple-element.43), channel_id=1, source_target_pairs={{1,0},{2,1},{3,2},{4,3},{5,4},{6,5},{7,6},{8,7},{9,8},{10,9},{11,1... | collective-permute-start | bytes 393224 | tf_op jit(solution)/shard_map/ppermute | solution.py:634
  66.7 8.6 %collective-permute-start.6 = (bf16[4,64,256]{2,1,0:T(8,128)(2,1)}, bf16[4,64,256]{2,1,0:T(8,128)(2,1)S(1)}, u32[]{:S(2)}, u32[]{:S(2)}) collective-permute-start(bf16[4,64,256]{2,1,0:T(8,128)(2,1)} %get-tuple-element.44), channel_id=1, source_target_pairs={{16,0},{32,16},{48,32},{64,48},{80,64},{96,80},{112,96},{0,112},{1... | collective-permute-start | bytes 393224 | tf_op jit(solution)/shard_map/ppermute | solution.py:634
  71.8 5.5 %collective-permute-start.7 = (bf16[4,64,256]{2,1,0:T(8,128)(2,1)}, bf16[4,64,256]{2,1,0:T(8,128)(2,1)S(1)}, u32[]{:S(2)}, u32[]{:S(2)}) collective-permute-start(bf16[4,64,256]{2,1,0:T(8,128)(2,1)} %get-tuple-element.45), channel_id=1, source_target_pairs={{0,1},{1,2},{2,3},{3,4},{4,5},{5,6},{6,7},{7,8},{8,9},{9,10},{10,1... | collective-permute-start | bytes 393224 | tf_op jit(solution)/shard_map/ppermute | solution.py:633
  74.5 7.7 %collective-permute-start.9 = (f32[136,256]{1,0:T(8,128)S(1)}, f32[136,256]{1,0:T(8,128)S(1)}, u32[]{:S(2)}, u32[]{:S(2)}) collective-permute-start(f32[136,256]{1,0:T(8,128)S(1)} %select_add_fusion), channel_id=1, source_target_pairs={{0,2},{1,3},{2,0},{3,1},{4,6},{5,7},{6,4},{7,5},{8,10},{9,11},{10,... | collective-permute-start | bytes 417800 | tf_op jit(solution)/shard_map/ppermute | solution.py:640
  75.2 2.1 %copy-start = (bf16[4,64,256]{2,1,0:T(8,128)(2,1)}, bf16[4,64,256]{2,1,0:T(8,128)(2,1)S(1)}, u32[]{:S(2)}) copy-start(bf16[4,64,256]{2,1,0:T(8,128)(2,1)S(1)} %collective-permute-done.4.refs_5_) | copy-start | bytes 393220
  75.2 2.1 %copy-start.1 = (bf16[4,64,256]{2,1,0:T(8,128)(2,1)}, bf16[4,64,256]{2,1,0:T(8,128)(2,1)S(1)}, u32[]{:S(2)}) copy-start(bf16[4,64,256]{2,1,0:T(8,128)(2,1)S(1)} %collective-permute-done.5.refs_6_) | copy-start | bytes 393220
  75.2 2.0 %copy-start.2 = (bf16[4,64,256]{2,1,0:T(8,128)(2,1)}, bf16[4,64,256]{2,1,0:T(8,128)(2,1)S(1)}, u32[]{:S(2)}) copy-start(bf16[4,64,256]{2,1,0:T(8,128)(2,1)S(1)} %collective-permute-done.6.refs_7_) | copy-start | bytes 393220
  77.3 0.7 copy-start.3
  82.2 9.9 %collective-permute-start.10 = (f32[136,256]{1,0:T(8,128)S(1)}, f32[136,256]{1,0:T(8,128)S(1)}, u32[]{:S(2)}, u32[]{:S(2)}) collective-permute-start(f32[136,256]{1,0:T(8,128)S(1)} %add.69), channel_id=1, source_target_pairs={{0,6},{1,7},{2,4},{3,5},{4,2},{5,3},{6,0},{7,1},{8,14},{9,15},{10,... | collective-permute-start | bytes 417800 | tf_op jit(solution)/shard_map/ppermute | solution.py:640
  92.1 4.8 %collective-permute-start.11 = (f32[136,256]{1,0:T(8,128)S(1)}, f32[136,256]{1,0:T(8,128)S(1)}, u32[]{:S(2)}, u32[]{:S(2)}) collective-permute-start(f32[136,256]{1,0:T(8,128)S(1)} %add.70), channel_id=1, source_target_pairs={{0,8},{1,9},{2,10},{3,11},{4,12},{5,13},{6,14},{7,15},{8,0},{9,1},... | collective-permute-start | bytes 417800 | tf_op jit(solution)/shard_map/ppermute | solution.py:640
  97.0 5.5 %collective-permute-start.12 = (f32[136,256]{1,0:T(8,128)S(1)}, f32[136,256]{1,0:T(8,128)S(1)}, u32[]{:S(2)}, u32[]{:S(2)}) collective-permute-start(f32[136,256]{1,0:T(8,128)S(1)} %add.71), channel_id=1, source_target_pairs={{0,24},{1,25},{2,26},{3,27},{4,28},{5,29},{6,30},{7,31},{8,16},{9,... | collective-permute-start | bytes 417800 | tf_op jit(solution)/shard_map/ppermute | solution.py:640
  102.5 5.2 %collective-permute-start.13 = (f32[136,256]{1,0:T(8,128)S(1)}, f32[136,256]{1,0:T(8,128)S(1)}, u32[]{:S(2)}, u32[]{:S(2)}) collective-permute-start(f32[136,256]{1,0:T(8,128)S(1)} %add.72), channel_id=1, source_target_pairs={{0,32},{1,33},{2,34},{3,35},{4,36},{5,37},{6,38},{7,39},{8,40},{9,... | collective-permute-start | bytes 417800 | tf_op jit(solution)/shard_map/ppermute | solution.py:640
  107.8 6.1 %collective-permute-start.14 = (f32[136,256]{1,0:T(8,128)S(1)}, f32[136,256]{1,0:T(8,128)S(1)}, u32[]{:S(2)}, u32[]{:S(2)}) collective-permute-start(f32[136,256]{1,0:T(8,128)S(1)} %add.73), channel_id=1, source_target_pairs={{0,96},{1,97},{2,98},{3,99},{4,100},{5,101},{6,102},{7,103},{8,104... | collective-permute-start | bytes 417800 | tf_op jit(solution)/shard_map/ppermute | solution.py:640
  113.9 7.8 %copy-start.4 = (f32[136,256]{1,0:T(8,128)}, f32[136,256]{1,0:T(8,128)S(1)}, u32[]{:S(2)}) copy-start(f32[136,256]{1,0:T(8,128)S(1)} %add.74.mine_ref) | copy-start | bytes 417796
  113.9 7.8 %collective-permute-start.15 = (f32[136,256]{1,0:T(8,128)S(1)}, f32[136,256]{1,0:T(8,128)S(1)}, u32[]{:S(2)}, u32[]{:S(2)}) collective-permute-start(f32[136,256]{1,0:T(8,128)S(1)} %add.74.mine_ref), channel_id=1, source_target_pairs={{0,1},{1,0},{2,3},{3,2},{4,5},{5,4},{6,7},{7,6},{8,9},{9,8},{10,11... | collective-permute-start | bytes 417800 | tf_op jit(solution)/shard_map/ppermute | solution.py:640
  121.7 0.7 copy-start.5

commit v4 on v3

--- a/solution.py
+++ b/solution.py
@@ -40,7 +40,7 @@
     return jnp.broadcast_to(ref[k : k + 1, hf * LANES : hf * LANES + LANES], (SUB, LANES))
 
 
-def inner_body(pairs, x_ref, cot_ref, w_ref, tap_ref, bias_ref, gh_ref, pg_ref, dg_ref, u, hide, acc, half_w, *bufs):
+def inner_body(pairs, carried, x_ref, cot_ref, w_ref, tap_ref, bias_ref, gh_ref, outs, u, hide, acc, half_w, pg_ref, *bufs):
     step = pl.program_id(0)
     side = x_ref.shape[1]
     cols = x_ref.shape[2]
@@ -149,68 +149,97 @@
     lax.fori_loop(0, side // (2 * rows), body, 0)
     outer(sets[1])
 
+    def tap_sums(hf):
+        lines = [None] * 10
+        for c in range(3):
+            d1, d2, d3, d4 = (acc[hf, 3 * k + c] for k in range(4))
+            even = 0.5 * (d2 + d3)
+            lines[c] = d1 + even
+            lines[3 + c] = 0.5 * (d2 - d3)
+            lines[6 + c] = even - d4
+        lines[9] = acc[hf, 12]
+        return lines
+
     @pl.when(step == pl.num_programs(0) - 1)
     def _():
+        point = pg_ref[...] * (0.5 / ALPHA)
+        if carried is None:
+            pg_out, dg_out = outs
+            pg_out[...] = point
+            for hf in range(2):
+                for k, line in enumerate(tap_sums(hf)):
+                    dg_out[hf, k] = line
+            return
+        table, _, pg_in, dg_in = carried
+        mine, sent = outs
+        rows = mine.shape[0]
+        lines = []
         for hf in range(2):
-            for c in range(3):
-                d1, d2, d3, d4 = (acc[hf, 3 * k + c] for k in range(4))
-                even = 0.5 * (d2 + d3)
-                dg_ref[hf, c] = d1 + even
-                dg_ref[hf, 3 + c] = 0.5 * (d2 - d3)
-                dg_ref[hf, 6 + c] = even - d4
-            dg_ref[hf, 9] = acc[hf, 12]
-        pg_ref[...] = pg_ref[...] * (0.5 / ALPHA)
+            own = [jnp.sum(v + dg_in[hf, k], axis=0, keepdims=True) for k, v in enumerate(tap_sums(hf))]
+            lines.append(jnp.concatenate(own + [jnp.zeros((6, LANES), F32)], axis=0))
+        point = point + pg_in[...]
+        low = point[:rows]
+        high = jnp.concatenate([point[rows:], jnp.concatenate(lines, axis=1)], axis=0)
+        first = table[CORE] == 0
+        mine[...] = jnp.where(first, low, high)
+        sent[...] = jnp.where(first, high, low)
 
 
 PAIRS = 4
 
 
-def inner_call(state, cotangent, weight, taps, bias):
+def inner_call(first, count, state, cotangent, weight, taps, bias, carried=None):
     batch, side, cols, channels = state.shape
-    tile = pl.BlockSpec((1, side, cols, channels), lambda b: (b, 0, 0, 0))
+    tile = pl.BlockSpec((1, side, cols, channels), lambda b: (b + first, 0, 0, 0))
+    whole = lambda *shape: pl.BlockSpec(shape, lambda b: (0,) * len(shape))
     buf = [
         pltpu.VMEM((2, PAIRS, 4, cols + 2 * PAD, LANES), F32),
         pltpu.VMEM((2, 2 * PAIRS * cols, LANES), F32),
         pltpu.VMEM((2 * PAIRS * cols, channels), BF16),
         pltpu.VMEM((2 * PAIRS * cols, channels), BF16),
     ]
+    square, lines, half = (channels, channels), (2, 10, SUB, LANES), ((channels + 16) // 2, channels)
+    in_specs = [tile, tile, whole(*square), whole(9, channels), whole(1, channels)]
+    operands = [state, cotangent, weight, taps, bias]
+    shapes, aliases = (square, lines), {}
+    if carried is not None:
+        in_specs += [pl.BlockSpec(memory_space=pltpu.SMEM), pl.BlockSpec(memory_space=pl.ANY), whole(*square), whole(*lines)]
+        operands += carried
+        shapes, aliases = (half, half), {6: 0}
+    given = len(operands)
+
+    def body(*refs):
+        extra = None if carried is None else refs[5:given]
+        inner_body(PAIRS, extra, *refs[:5], refs[given], refs[given + 1 : given + 3], *refs[given + 3 :])
+
     return pl.pallas_call(
-        functools.partial(inner_body, PAIRS),
-        grid=(batch,),
-        in_specs=[
-            tile,
-            tile,
-            pl.BlockSpec((channels, channels), lambda b: (0, 0)),
-            pl.BlockSpec((9, channels), lambda b: (0, 0)),
-            pl.BlockSpec((1, channels), lambda b: (0, 0)),
-        ],
-        out_specs=[
-            tile,
-            pl.BlockSpec((channels, channels), lambda b: (0, 0)),
-            pl.BlockSpec((2, 10, SUB, LANES), lambda b: (0, 0, 0, 0)),
-        ],
+        body,
+        grid=(count,),
+        in_specs=in_specs,
+        out_specs=[tile, *(whole(*shape) for shape in shapes)],
         out_shape=[
             jax.ShapeDtypeStruct(state.shape, BF16),
-            jax.ShapeDtypeStruct((channels, channels), F32),
-            jax.ShapeDtypeStruct((2, 10, SUB, LANES), F32),
+            *(jax.ShapeDtypeStruct(shape, F32) for shape in shapes),
         ],
         scratch_shapes=[
             pltpu.VMEM((2, 13, SUB, LANES), F32),
             pltpu.VMEM((2, cols, channels), BF16),
             pltpu.VMEM((2, 13, SUB, LANES), F32),
-            pltpu.VMEM((channels, channels), BF16),
+            pltpu.VMEM(square, BF16),
+            pltpu.VMEM(square, F32),
             *buf,
             *buf,
         ],
+        input_output_aliases=aliases,
         compiler_params=pltpu.CompilerParams(vmem_limit_bytes=57 << 20),
         cost_estimate=pl.CostEstimate(
-            flops=40_000_000_000, bytes_accessed=26 << 20, transcendentals=state.size
+            flops=10_000_000_000 * count, bytes_accessed=state.size * 6 * count // batch, transcendentals=state.size
         ),
         name="inner",
-    )(state, cotangent, weight, taps, bias)
-
-
-DIR_OF_SIDE, SIDE_OF_DIR, FLIPS, MASKS = 0, 4, 8, 12
+    )(*operands)
+
+
+DIR_OF_SIDE, SIDE_OF_DIR, FLIPS, MASKS, CORE = 0, 4, 8, 12, 16
 
 
 def from_dir(table, got, s):
@@ -230,7 +259,26 @@
     return jnp.dot(pick, rows, preferred_element_type=F32).astype(BF16)
 
 
-def edges_body(table, top_ref, low_ref, left_ref, right_ref, to0, to1, to2, to3, turned):
+def edges_body(sizes, where, links, flips, masks, top_ref, low_ref, left_ref, right_ref, to0, to1, to2, to3, table, turned):
+    faces, tiles = sizes
+
+    @pl.when(pl.program_id(0) == 0)
+    def _():
+        face, tile = where[0], where[1]
+        towards = (
+            lax.rem(face + faces - 1, faces) * tiles + tile,
+            face * tiles + lax.rem(tile + 1, tiles),
+            lax.rem(face + 1, faces) * tiles + tile,
+            face * tiles + lax.rem(tile + tiles - 1, tiles),
+        )
+        met = [[jnp.where(links[0, s] == to, 1, 0) for to in towards] for s in range(4)]
+        for k in range(4):
+            table[DIR_OF_SIDE + k] = met[k][1] + 2 * met[k][2] + 3 * met[k][3]
+            table[SIDE_OF_DIR + k] = met[1][k] + 2 * met[2][k] + 3 * met[3][k]
+            table[FLIPS + k] = flips[0, k]
+            table[MASKS + k] = masks[0, k]
+        table[CORE] = lax.rem(tile, 2)
+
     last = right_ref.shape[2] - 1
     turned[0] = turn(table, 0, top_ref[0, 0])
     turned[1] = turn(table, 1, right_ref[0].astype(F32)[:, last].astype(BF16))
@@ -240,28 +288,31 @@
         to[0] = turned[table[SIDE_OF_DIR + d]]
 
 
-def edges_call(table, state):
+def edges_call(where, links, flips, masks, state):
     batch, side, cols, channels = state.shape
-    wide = 16
+    wide = 8
     one = lambda at: pl.BlockSpec((1, 1, cols, channels), lambda b: (b, at, 0, 0))
     column = lambda at: pl.BlockSpec((1, side, wide, channels), lambda b: (b, 0, at, 0))
     facing = pl.BlockSpec((1, side, channels), lambda b: (b, 0, 0))
     return pl.pallas_call(
-        edges_body,
+        functools.partial(edges_body, (lax.axis_size("face"), lax.axis_size("tile"))),
         grid=(batch,),
         in_specs=[
-            pl.BlockSpec(memory_space=pltpu.SMEM),
+            *[pl.BlockSpec(memory_space=pltpu.SMEM)] * 4,
             one(0),
             one(side - 1),
             column(0),
             column(cols // wide - 1),
         ],
-        out_specs=[facing] * 4,
-        out_shape=[jax.ShapeDtypeStruct((batch, side, channels), BF16)] * 4,
+        out_specs=[*[facing] * 4, pl.BlockSpec(memory_space=pltpu.SMEM)],
+        out_shape=[
+            *[jax.ShapeDtypeStruct((batch, side, channels), BF16)] * 4,
+            jax.ShapeDtypeStruct((CORE + 1,), jnp.int32),
+        ],
         scratch_shapes=[pltpu.VMEM((4, side, channels), BF16)],
         compiler_params=pltpu.CompilerParams(vmem_limit_bytes=57 << 20),
         name="edges",
-    )(table, state, state, state, state)
+    )(where, links, flips, masks, state, state, state, state)
 
 
 LOW = (0, 1, 3, 0)
@@ -271,7 +322,7 @@
 def ring_body(
     table, top_ref, low_ref, left_ref, right_ref, ctop_ref, clow_ref, cleft_ref, cright_ref,
     got0, got1, got2, got3, w_ref, tap_ref, bias_ref, pg_ref, dg_ref,
-    gr_ref, to0, to1, to2, to3, part_ref, strip, ext, acts, acc, turned,
+    gr_ref, to0, to1, to2, to3, point_ref, line_ref, strip, ext, acts, acc, turned,
 ):
     step = pl.program_id(0)
     side = got0.shape[1]
@@ -281,7 +332,7 @@
     @pl.when(step == 0)
     def _():
         acc[...] = dg_ref[...]
-        part_ref[0 : 2 * LANES, :] = pg_ref[...]
+        point_ref[...] = pg_ref[...]
         ext[...] = jnp.zeros_like(ext)
 
     rims = [from_dir(table, got, s).astype(F32) for s in range(4)]
@@ -377,22 +428,16 @@
             turned[s, :, lanes] = turn(table, s, back.astype(BF16))
     for d, to in enumerate((to0, to1, to2, to3)):
         to[0] = turned[table[SIDE_OF_DIR + d]]
-    part_ref[0 : 2 * LANES, :] += lax.dot_general(
-        acts[...], cots, (((0,), (0,)), ((), ())), preferred_element_type=F32
-    )
+    point_ref[...] += lax.dot_general(acts[...], cots, (((0,), (0,)), ((), ())), preferred_element_type=F32)
 
     @pl.when(step == pl.num_programs(0) - 1)
     def _():
-        part_ref[2 * LANES :, :] = jnp.zeros((16, 2 * LANES), F32)
-        for hf in range(2):
-            for k in range(10):
-                line = jnp.sum(acc[hf, k], axis=0, keepdims=True)
-                part_ref[2 * LANES + k : 2 * LANES + k + 1, hf * LANES : hf * LANES + LANES] = line
+        line_ref[...] = acc[...]
 
 
 def ring_call(table, state, cotangent, got, weight, taps, bias, point_inner, depth_inner):
     batch, side, cols, channels = state.shape
-    wide = 16
+    wide = 8
     two = lambda at: pl.BlockSpec((1, 2, cols, channels), lambda b: (b, at, 0, 0))
     one = lambda at: pl.BlockSpec((1, 1, cols, channels), lambda b: (b, at, 0, 0))
     column = lambda at: pl.BlockSpec((1, side, wide, channels), lambda b: (b, 0, at, 0))
@@ -419,11 +464,17 @@
             pl.BlockSpec((channels, channels), lambda b: (0, 0)),
             pl.BlockSpec((2, 10, SUB, LANES), lambda b: (0, 0, 0, 0)),
         ],
-        out_specs=[strips, *[facing] * 4, pl.BlockSpec((channels + 16, channels), lambda b: (0, 0))],
+        out_specs=[
+            strips,
+            *[facing] * 4,
+            pl.BlockSpec((channels, channels), lambda b: (0, 0)),
+            pl.BlockSpec((2, 10, SUB, LANES), lambda b: (0, 0, 0, 0)),
+        ],
         out_shape=[
             jax.ShapeDtypeStruct((4, batch, side, channels), BF16),
             *[jax.ShapeDtypeStruct((batch, side, channels), BF16)] * 4,
-            jax.ShapeDtypeStruct((channels + 16, channels), F32),
+            jax.ShapeDtypeStruct((channels, channels), F32),
+            jax.ShapeDtypeStruct((2, 10, SUB, LANES), F32),
         ],
         scratch_shapes=[
             pltpu.VMEM((4, 2, 3, cols + 2 * PAD, LANES), F32),
@@ -593,12 +644,12 @@
     )(*operands)
 
 
-def finish_body(scale, bit_ref, mine_ref, other_ref, dg_ref, bg_ref, pg_ref):
+def finish_body(scale, table, mine_ref, other_ref, dg_ref, bg_ref, pg_ref):
     rows = mine_ref.shape[0]
     channels = pg_ref.shape[0]
     own = mine_ref[...] * scale
     far = other_ref[...] * scale
-    first = bit_ref[0] == 0
+    first = table[CORE] == 0
     low = jnp.where(first, own, far)
     high = jnp.where(first, far, own)
     pg_ref[0:rows, :] = low
@@ -652,46 +703,33 @@
     tile_count = lax.axis_size("tile")
     face_pos = lax.axis_index("face")
     tile_pos = lax.axis_index("tile")
-    toward = jnp.stack(
-        [
-            (face_pos - 1) % face_count * tile_count + tile_pos,
-            face_pos * tile_count + (tile_pos + 1) % tile_count,
-            (face_pos + 1) % face_count * tile_count + tile_pos,
-            face_pos * tile_count + (tile_pos - 1) % tile_count,
-        ]
+    where = jnp.stack([face_pos, tile_pos])
+    bias = depth_bias.reshape(1, channels)
+    *edges, table = edges_call(where, tile_links, link_flips, corner_masks, state)
+    got = exchange(edges)
+    layer = (point_weight, depth_weight, bias)
+    early = batch // 2
+    grad, point_sum, depth_sum = inner_call(0, early, state, cotangent, *layer)
+    ring, *facing, point_sum, depth_sum = ring_call(table, state, cotangent, got, *layer, point_sum, depth_sum)
+    incoming = exchange(facing)
+    grad, mine, sent = inner_call(
+        early, batch - early, state, cotangent, *layer, (table, grad, point_sum, depth_sum)
     )
-    matched = tile_links[0][:, None] == toward[None, :]
-    counter = jnp.arange(4, dtype=jnp.int32)
-    dir_of_side = jnp.sum(jnp.where(matched, counter[None, :], 0), axis=1)
-    side_of_dir = jnp.sum(jnp.where(matched, counter[:, None], 0), axis=0)
-    table = jnp.concatenate([dir_of_side, side_of_dir, link_flips[0], corner_masks[0]])
-    bias = depth_bias.reshape(1, channels)
-    got = exchange(edges_call(table, state))
-    grad, point_inner, depth_inner = inner_call(state, cotangent, point_weight, depth_weight, bias)
-    ring, *facing, part = ring_call(
-        table, state, cotangent, got, point_weight, depth_weight, bias, point_inner, depth_inner
-    )
-    incoming = exchange(facing)
-
-    core = tile_pos % 2
-    half = part.shape[0] // 2
-    low, high = part[:half], part[half:]
-    mine = jnp.where(core == 0, low, high)
-    sent = jnp.where(core == 0, high, low)
+
     first, field_grad = 0, None
     for stage, (mask_bits, steps) in enumerate(
-        ((1, 0), (2, 2), (6, 3), (8, 2), (24, 3), (32, 2), (96, 2), (1, 2))
+        ((1, 2), (2, 2), (6, 2), (8, 2), (24, 2), (32, 2), (96, 2), (1, 2))
     ):
         got = swap(sent if stage == 0 else mine, mask_bits)
         if steps:
-            held = after(depth_weight, mine)
+            held = after(depth_weight, mine if stage else sent)
             field_grad, token = spread_call(first, steps, table, grad, ring, incoming, held, field_grad)
             got = after(got, token)
             first += steps
         if stage < 7:
             mine = mine + got
     scale = float(batch * side * cols * face_count * tile_count) ** -0.5
-    depth_grad, bias_grad, point_grad = finish_call(scale, core.reshape(1), mine, got)
+    depth_grad, bias_grad, point_grad = finish_call(scale, table, mine, got)
     return field_grad, depth_grad, bias_grad.reshape(channels), point_grad
 
 

time: 125 us -> 126 us (level)
  Pallas kernels: 83.7 us -> 88.6 us
  other arithmetic: 4.32 us -> 0.74 us
    ppermute x8, waiting for transfers between devices: 0.02 us -> 3.65 us  [swap(): lax.ppermute(value, ('face', 'tile'), [(i, i ^ mask) for i in range(devic...]
    pallas_call x2 -> x3, Pallas kernels: 42 us -> 45.5 us  [the longest x2 41.4 us: inner_call(): pl.pallas_call(body, grid=(count,), in_specs=in_specs, out_specs=[tile, *...]
    ppermute x4, waiting for transfers between devices: 2.7 us -> 0.01 us  [exchange(): got[low] = lax.ppermute(facing[high], axis, up)]
    pallas_call x7 -> x8, Pallas kernels: 31.8 us -> 33.7 us  [spread_call(): pl.pallas_call(body, grid=(steps,), in_specs=in_specs, out_specs=[rows, p...]
    ppermute x8, starting transfers between devices: 14.3 us -> 12.7 us  [swap(): lax.ppermute(value, ('face', 'tile'), [(i, i ^ mask) for i in range(devic...]
    ppermute x4, starting transfers between devices: 8.39 us -> 9.78 us  [exchange(): got[high] = lax.ppermute(facing[low], axis, down)]
    concatenate x1 -> x0, other arithmetic: 1.26 us -> none  [shards(): jnp.concatenate([dir_of_side, side_of_dir, link_flips[0], corner_masks[0]])]
  transfers between devices with their start and end apart: 16 -> 16, of which waited for: 2 -> 4; matrix products, arithmetic and copies ran while one was open for 1% -> 0% of each run, Pallas kernels for 56% -> 60%
where the time goes in v4:
time: 126 us
  Pallas kernels  88.6 us (70%)
  starting transfers between devices  29.5 us (23%)
  waiting for transfers between devices  3.67 us (3%)
  local copies, waits for them, and re-layouts  2.17 us (2%)
    pallas_call x2, Pallas kernels, inner_call(): pl.pallas_call(body, grid=(count,), in_specs=in_specs, out_specs=[tile, *...  41.4 us
    pallas_call x8, Pallas kernels, spread_call(): pl.pallas_call(body, grid=(steps,), in_specs=in_specs, out_specs=[rows, p...  33.7 us
    ppermute x8, starting transfers between devices, swap(): lax.ppermute(value, ('face', 'tile'), [(i, i ^ mask) for i in range(devic...  12.7 us
    ppermute x4, starting transfers between devices, exchange(): got[high] = lax.ppermute(facing[low], axis, down)  9.78 us
    pallas_call x1, Pallas kernels, ring_call(): pl.pallas_call(ring_body, grid=(batch,), in_specs=[pl.BlockSpec(memory_sp...  7.69 us
    ppermute x4, starting transfers between devices, exchange(): got[low] = lax.ppermute(facing[high], axis, up)  7.01 us
    pallas_call x1, Pallas kernels, edges_call(): pl.pallas_call(functools.partial(edges_body, (lax.axis_size('face'), lax....  4.12 us
    ppermute x8, waiting for transfers between devices, swap(): lax.ppermute(value, ('face', 'tile'), [(i, i ^ mask) for i in range(devic...  3.65 us
  transfers between devices with their start and end apart: 16, of which 4 were waited for; matrix products, arithmetic and copies ran while one was open for 0% of the time, Pallas kernels for 60%

profile of v4, /device:TPU:1, one launch (start us, length us, event | category | flops | bytes accessed | tf_op | source)
XLA Modules:
  0.0 125.5 jit_solution(9854620059656591720)
XLA Ops:
  0.6 0.6 pad_add_fusion.where
  1.2 4.1 %edges.1 = (bf16[4,64,256]{2,1,0:T(8,128)(2,1)}, bf16[4,64,256]{2,1,0:T(8,128)(2,1)}, bf16[4,64,256]{2,1,0:T(8,128)(2,1)}, bf16[4,64,256]{2,1,0:T(8,128)(2,1)}, s32[17]{0:T(128)}) custom-call(s32[2]{0:T(128)} %pad_add_fusion.where, s32[1,4]{1,0:T(1,128)} %links.1, s32[1,4]{1,0:T(1,128)} %flips.1, s32[1,4]{1,0:T(1,128)} %masks.1, ...), custom_call_target="tpu_custom_call" | custom-call | tf_op jit(solution)/shard_map/edges/pallas_call | solution.py:297
  5.3 4.5 %collective-permute-start = (bf16[4,64,256]{2,1,0:T(8,128)(2,1)}, bf16[4,64,256]{2,1,0:T(8,128)(2,1)S(1)}, u32[]{:S(2)}, u32[]{:S(2)}) collective-permute-start(bf16[4,64,256]{2,1,0:T(8,128)(2,1)} %get-tuple-element.43), channel_id=1, source_target_pairs={{0,16},{16,32},{32,48},{48,64},{64,80},{80,96},{96,112},{112,0},{1... | collective-permute-start | bytes 393224 | tf_op jit(solution)/shard_map/ppermute | solution.py:684
  9.8 1.0 collective-permute-start.1
  10.8 2.0 %collective-permute-start.2 = (bf16[4,64,256]{2,1,0:T(8,128)(2,1)}, bf16[4,64,256]{2,1,0:T(8,128)(2,1)S(1)}, u32[]{:S(2)}, u32[]{:S(2)}) collective-permute-start(bf16[4,64,256]{2,1,0:T(8,128)(2,1)} %get-tuple-element.45), channel_id=1, source_target_pairs={{16,0},{32,16},{48,32},{64,48},{80,64},{96,80},{112,96},{0,112},{1... | collective-permute-start | bytes 393224 | tf_op jit(solution)/shard_map/ppermute | solution.py:685
  12.8 1.6 %collective-permute-start.3 = (bf16[4,64,256]{2,1,0:T(8,128)(2,1)}, bf16[4,64,256]{2,1,0:T(8,128)(2,1)S(1)}, u32[]{:S(2)}, u32[]{:S(2)}) collective-permute-start(bf16[4,64,256]{2,1,0:T(8,128)(2,1)} %get-tuple-element.46), channel_id=1, source_target_pairs={{0,1},{1,2},{2,3},{3,4},{4,5},{5,6},{6,7},{7,8},{8,9},{9,10},{10,1... | collective-permute-start | bytes 393224 | tf_op jit(solution)/shard_map/ppermute | solution.py:684
  14.3 20.6 %inner.2 = (bf16[4,64,64,256]{3,2,1,0:T(8,128)(2,1)}, f32[256,256]{1,0:T(8,128)}, f32[2,10,8,128]{3,2,1,0:T(8,128)}) custom-call(bf16[4,64,64,256]{3,2,1,0:T(8,128)(2,1)} %refs_0_.3, bf16[4,64,64,256]{3,2,1,0:T(8,128)(2,1)} %refs_1_.3, bf16[256,256]{1,0:T(8,128)(2,1)} %refs_2_.3, f32[9,256]{1,0:T(8,128)} %refs_9_.7, f32[1,256]{1,0:T(1,128)} %bitcast.4), custom_call_target="tpu_custom_call" | custom-call | flops 20000000000 | bytes 12582912 | tf_op jit(solution)/shard_map/inner/pallas_call | solution.py:215
  35.0 0.6 copy-done.7
  35.8 7.7 %ring.1 = (bf16[4,4,64,256]{3,2,1,0:T(8,128)(2,1)}, bf16[4,64,256]{2,1,0:T(8,128)(2,1)}, bf16[4,64,256]{2,1,0:T(8,128)(2,1)}, bf16[4,64,256]{2,1,0:T(8,128)(2,1)...) custom-call(s32[17]{0:T(128)} %get-tuple-element.41.table.refs_5_.refs_0_, ...), custom_call_target="tpu_custom_call" | custom-call | flops 3000000000 | bytes 12582912 | tf_op jit(solution)/shard_map/ring/pallas_call | solution.py:447
  43.5 1.0 collective-permute-start.4
  44.4 1.7 %collective-permute-start.5 = (bf16[4,64,256]{2,1,0:T(8,128)(2,1)}, bf16[4,64,256]{2,1,0:T(8,128)(2,1)S(1)}, u32[]{:S(2)}, u32[]{:S(2)}) collective-permute-start(bf16[4,64,256]{2,1,0:T(8,128)(2,1)} %get-tuple-element.54), channel_id=1, source_target_pairs={{1,0},{2,1},{3,2},{4,3},{5,4},{6,5},{7,6},{8,7},{9,8},{10,9},{11,1... | collective-permute-start | bytes 393224 | tf_op jit(solution)/shard_map/ppermute | solution.py:685
  46.2 5.1 %collective-permute-start.6 = (bf16[4,64,256]{2,1,0:T(8,128)(2,1)}, bf16[4,64,256]{2,1,0:T(8,128)(2,1)S(1)}, u32[]{:S(2)}, u32[]{:S(2)}) collective-permute-start(bf16[4,64,256]{2,1,0:T(8,128)(2,1)} %get-tuple-element.55), channel_id=1, source_target_pairs={{16,0},{32,16},{48,32},{64,48},{80,64},{96,80},{112,96},{0,112},{1... | collective-permute-start | bytes 393224 | tf_op jit(solution)/shard_map/ppermute | solution.py:685
  51.3 20.8 %inner.3 = (bf16[4,64,64,256]{3,2,1,0:T(8,128)(2,1)}, f32[136,256]{1,0:T(8,128)}, f32[136,256]{1,0:T(8,128)}) custom-call(bf16[4,64,64,256]{3,2,1,0:T(8,128)(2,1)} %refs_0_.3, bf16[4,64,64,256]{3,2,1,0:T(8,128)(2,1)} %refs_1_.3, bf16[256,256]{1,0:T(8,128)(2,1)} %refs_2_.3, f32[9,256]{1,0:T(8,128)} %refs_9_.7, ...), custom_call_target="tpu_custom_call", output_to_operand_aliasing={{0}: (6, {})} | custom-call | flops 20000000000 | bytes 12582912 | tf_op jit(solution)/shard_map/inner/pallas_call | solution.py:215
  72.1 4.5 %collective-permute-start.8 = (f32[136,256]{1,0:T(8,128)}, f32[136,256]{1,0:T(8,128)S(1)}, u32[]{:S(2)}, u32[]{:S(2)}) collective-permute-start(f32[136,256]{1,0:T(8,128)} %get-tuple-element.58), channel_id=1, source_target_pairs={{0,1},{1,0},{2,3},{3,2},{4,5},{5,4},{6,7},{7,6},{8,9},{9,8},{10,11... | collective-permute-start | bytes 417800 | tf_op jit(solution)/shard_map/ppermute | solution.py:691
  76.6 0.6 copy-done
  77.4 4.2 %spread.8 = (bf16[4,64,64,256]{3,2,1,0:T(8,128)(2,1)}, f32[8,128]{1,0:T(8,128)}) custom-call(s32[17]{0:T(128)} %get-tuple-element.41.table.refs_5_.refs_0_, bf16[4,64,64,256]{3,2,1,0:T(8,128)(2,1)} %get-tuple-element.51.refs_1_.refs_2_.refs_3_, bf16[4,64,64,256]{3,2,1,0:T(8,128)(2,1)} %get-tuple-element.51.refs_1_.refs_2_.refs_3_, ...), custom_call_target="tpu_custom_call" | custom-call | flops 1500000000 | bytes 2097152 | tf_op jit(solution)/shard_map/spread/pallas_call | solution.py:625
  81.7 4.2 %spread.9 = (bf16[4,64,64,256]{3,2,1,0:T(8,128)(2,1)}, f32[8,128]{1,0:T(8,128)}) custom-call(s32[17]{0:T(128)} %get-tuple-element.41.table.refs_5_.refs_0_, bf16[4,64,64,256]{3,2,1,0:T(8,128)(2,1)} %get-tuple-element.51.refs_1_.refs_2_.refs_3_, bf16[4,64,64,256]{3,2,1,0:T(8,128)(2,1)} %get-tuple-element.51.refs_1_.refs_2_.refs_3_, ...), custom_call_target="tpu_custom_call", output_to_operand_aliasing={{0}: (10, {})} | custom-call | flops 1500000000 | bytes 2097152 | tf_op jit(solution)/shard_map/spread/pallas_call | solution.py:625
  85.9 1.1 collective-permute-done.9
  87.3 4.2 %spread.10 = (bf16[4,64,64,256]{3,2,1,0:T(8,128)(2,1)}, f32[8,128]{1,0:T(8,128)}) custom-call(s32[17]{0:T(128)} %get-tuple-element.41.table.refs_5_.refs_0_, bf16[4,64,64,256]{3,2,1,0:T(8,128)(2,1)} %get-tuple-element.51.refs_1_.refs_2_.refs_3_, bf16[4,64,64,256]{3,2,1,0:T(8,128)(2,1)} %get-tuple-element.51.refs_1_.refs_2_.refs_3_, ...), custom_call_target="tpu_custom_call", output_to_operand_aliasing={{0}: (10, {})} | custom-call | flops 1500000000 | bytes 2097152 | tf_op jit(solution)/shard_map/spread/pallas_call | solution.py:625
  91.5 1.4 %collective-permute-done.10 = f32[136,256]{1,0:T(8,128)S(1)} collective-permute-done((f32[136,256]{1,0:T(8,128)S(1)}, f32[136,256]{1,0:T(8,128)S(1)}, u32[]{:S(2)}, u32[]{:S(2)}) %collective-permute-start.10) | collective-permute-done | bytes 139296 | tf_op jit(solution)/shard_map/ppermute | solution.py:691
  92.9 1.9 %collective-permute-start.11 = (f32[136,256]{1,0:T(8,128)S(1)}, f32[136,256]{1,0:T(8,128)S(1)}, u32[]{:S(2)}, u32[]{:S(2)}) collective-permute-start(f32[136,256]{1,0:T(8,128)S(1)} %add.23), channel_id=1, source_target_pairs={{0,8},{1,9},{2,10},{3,11},{4,12},{5,13},{6,14},{7,15},{8,0},{9,1},... | collective-permute-start | bytes 417800 | tf_op jit(solution)/shard_map/ppermute | solution.py:691
  94.8 4.2 %spread.11 = (bf16[4,64,64,256]{3,2,1,0:T(8,128)(2,1)}, f32[8,128]{1,0:T(8,128)}) custom-call(s32[17]{0:T(128)} %get-tuple-element.41.table.refs_5_.refs_0_, bf16[4,64,64,256]{3,2,1,0:T(8,128)(2,1)} %get-tuple-element.51.refs_1_.refs_2_.refs_3_, bf16[4,64,64,256]{3,2,1,0:T(8,128)(2,1)} %get-tuple-element.51.refs_1_.refs_2_.refs_3_, ...), custom_call_target="tpu_custom_call", output_to_operand_aliasing={{0}: (10, {})} | custom-call | flops 1500000000 | bytes 2097152 | tf_op jit(solution)/shard_map/spread/pallas_call | solution.py:625
  99.1 4.2 %spread.12 = (bf16[4,64,64,256]{3,2,1,0:T(8,128)(2,1)}, f32[8,128]{1,0:T(8,128)}) custom-call(s32[17]{0:T(128)} %get-tuple-element.41.table.refs_5_.refs_0_, bf16[4,64,64,256]{3,2,1,0:T(8,128)(2,1)} %get-tuple-element.51.refs_1_.refs_2_.refs_3_, bf16[4,64,64,256]{3,2,1,0:T(8,128)(2,1)} %get-tuple-element.51.refs_1_.refs_2_.refs_3_, ...), custom_call_target="tpu_custom_call", output_to_operand_aliasing={{0}: (10, {})} | custom-call | flops 1500000000 | bytes 2097152 | tf_op jit(solution)/shard_map/spread/pallas_call | solution.py:625
  103.4 0.9 collective-permute-done.12
  104.4 4.2 %spread.13 = (bf16[4,64,64,256]{3,2,1,0:T(8,128)(2,1)}, f32[8,128]{1,0:T(8,128)}) custom-call(s32[17]{0:T(128)} %get-tuple-element.41.table.refs_5_.refs_0_, bf16[4,64,64,256]{3,2,1,0:T(8,128)(2,1)} %get-tuple-element.51.refs_1_.refs_2_.refs_3_, bf16[4,64,64,256]{3,2,1,0:T(8,128)(2,1)} %get-tuple-element.51.refs_1_.refs_2_.refs_3_, ...), custom_call_target="tpu_custom_call", output_to_operand_aliasing={{0}: (10, {})} | custom-call | flops 1500000000 | bytes 2097152 | tf_op jit(solution)/shard_map/spread/pallas_call | solution.py:625
  108.6 0.7 collective-permute-start.14
  109.3 4.2 %spread.14 = (bf16[4,64,64,256]{3,2,1,0:T(8,128)(2,1)}, f32[8,128]{1,0:T(8,128)}) custom-call(s32[17]{0:T(128)} %get-tuple-element.41.table.refs_5_.refs_0_, bf16[4,64,64,256]{3,2,1,0:T(8,128)(2,1)} %get-tuple-element.51.refs_1_.refs_2_.refs_3_, bf16[4,64,64,256]{3,2,1,0:T(8,128)(2,1)} %get-tuple-element.51.refs_1_.refs_2_.refs_3_, ...), custom_call_target="tpu_custom_call", output_to_operand_aliasing={{0}: (10, {})} | custom-call | flops 1500000000 | bytes 2097152 | tf_op jit(solution)/shard_map/spread/pallas_call | solution.py:625
  113.5 0.3 collective-permute-done.14
  113.8 5.1 %collective-permute-start.15 = (f32[136,256]{1,0:T(8,128)S(1)}, f32[136,256]{1,0:T(8,128)S(1)}, u32[]{:S(2)}, u32[]{:S(2)}) collective-permute-start(f32[136,256]{1,0:T(8,128)S(1)} %add.27.mine_ref), channel_id=1, source_target_pairs={{0,1},{1,0},{2,3},{3,2},{4,5},{5,4},{6,7},{7,6},{8,9},{9,8},{10,11... | collective-permute-start | bytes 417800 | tf_op jit(solution)/shard_map/ppermute | solution.py:691
  118.9 4.2 %spread.15 = (bf16[4,64,64,256]{3,2,1,0:T(8,128)(2,1)}, f32[8,128]{1,0:T(8,128)}) custom-call(s32[17]{0:T(128)} %get-tuple-element.41.table.refs_5_.refs_0_, bf16[4,64,64,256]{3,2,1,0:T(8,128)(2,1)} %get-tuple-element.51.refs_1_.refs_2_.refs_3_, bf16[4,64,64,256]{3,2,1,0:T(8,128)(2,1)} %get-tuple-element.51.refs_1_.refs_2_.refs_3_, ...), custom_call_target="tpu_custom_call", output_to_operand_aliasing={{0}: (10, {})} | custom-call | flops 1500000000 | bytes 2097152 | tf_op jit(solution)/shard_map/spread/pallas_call | solution.py:625
  123.2 0.6 copy-done.6
  123.8 1.7 %finish.1 = (f32[9,256]{1,0:T(8,128)}, f32[1,256]{1,0:T(1,128)}, f32[256,256]{1,0:T(8,128)}) custom-call(s32[17]{0:T(128)} %get-tuple-element.41.table.refs_5_.refs_0_, f32[136,256]{1,0:T(8,128)} %copy-done.4, f32[136,256]{1,0:T(8,128)} %copy-done.6), custom_call_target="tpu_custom_call" | custom-call | tf_op jit(solution)/shard_map/finish/pallas_call | solution.py:665
  (43 shorter events, 1.1 us)
Async XLA Ops:
  5.3 29.6 %collective-permute-start = (bf16[4,64,256]{2,1,0:T(8,128)(2,1)}, bf16[4,64,256]{2,1,0:T(8,128)(2,1)S(1)}, u32[]{:S(2)}, u32[]{:S(2)}) collective-permute-start(bf16[4,64,256]{2,1,0:T(8,128)(2,1)} %get-tuple-element.43), channel_id=1, source_target_pairs={{0,16},{16,32},{32,48},{48,64},{64,80},{80,96},{96,112},{112,0},{1... | collective-permute-start | bytes 393224 | tf_op jit(solution)/shard_map/ppermute | solution.py:684
  9.8 25.1 %collective-permute-start.1 = (bf16[4,64,256]{2,1,0:T(8,128)(2,1)}, bf16[4,64,256]{2,1,0:T(8,128)(2,1)S(1)}, u32[]{:S(2)}, u32[]{:S(2)}) collective-permute-start(bf16[4,64,256]{2,1,0:T(8,128)(2,1)} %get-tuple-element.44), channel_id=1, source_target_pairs={{1,0},{2,1},{3,2},{4,3},{5,4},{6,5},{7,6},{8,7},{9,8},{10,9},{11,1... | collective-permute-start | bytes 393224 | tf_op jit(solution)/shard_map/ppermute | solution.py:685
  10.8 24.2 %collective-permute-start.2 = (bf16[4,64,256]{2,1,0:T(8,128)(2,1)}, bf16[4,64,256]{2,1,0:T(8,128)(2,1)S(1)}, u32[]{:S(2)}, u32[]{:S(2)}) collective-permute-start(bf16[4,64,256]{2,1,0:T(8,128)(2,1)} %get-tuple-element.45), channel_id=1, source_target_pairs={{16,0},{32,16},{48,32},{64,48},{80,64},{96,80},{112,96},{0,112},{1... | collective-permute-start | bytes 393224 | tf_op jit(solution)/shard_map/ppermute | solution.py:685
  12.8 22.2 %collective-permute-start.3 = (bf16[4,64,256]{2,1,0:T(8,128)(2,1)}, bf16[4,64,256]{2,1,0:T(8,128)(2,1)S(1)}, u32[]{:S(2)}, u32[]{:S(2)}) collective-permute-start(bf16[4,64,256]{2,1,0:T(8,128)(2,1)} %get-tuple-element.46), channel_id=1, source_target_pairs={{0,1},{1,2},{2,3},{3,4},{4,5},{5,6},{6,7},{7,8},{8,9},{9,10},{10,1... | collective-permute-start | bytes 393224 | tf_op jit(solution)/shard_map/ppermute | solution.py:684
  35.0 0.7 copy-start.7
  35.0 0.7 copy-start.8
  35.0 0.7 copy-start.9
  35.0 0.8 copy-start.10
  43.5 33.1 %collective-permute-start.4 = (bf16[4,64,256]{2,1,0:T(8,128)(2,1)}, bf16[4,64,256]{2,1,0:T(8,128)(2,1)S(1)}, u32[]{:S(2)}, u32[]{:S(2)}) collective-permute-start(bf16[4,64,256]{2,1,0:T(8,128)(2,1)} %get-tuple-element.53), channel_id=1, source_target_pairs={{0,16},{16,32},{32,48},{48,64},{64,80},{80,96},{96,112},{112,0},{1... | collective-permute-start | bytes 393224 | tf_op jit(solution)/shard_map/ppermute | solution.py:684
  44.4 32.1 %collective-permute-start.5 = (bf16[4,64,256]{2,1,0:T(8,128)(2,1)}, bf16[4,64,256]{2,1,0:T(8,128)(2,1)S(1)}, u32[]{:S(2)}, u32[]{:S(2)}) collective-permute-start(bf16[4,64,256]{2,1,0:T(8,128)(2,1)} %get-tuple-element.54), channel_id=1, source_target_pairs={{1,0},{2,1},{3,2},{4,3},{5,4},{6,5},{7,6},{8,7},{9,8},{10,9},{11,1... | collective-permute-start | bytes 393224 | tf_op jit(solution)/shard_map/ppermute | solution.py:685
  46.2 30.4 %collective-permute-start.6 = (bf16[4,64,256]{2,1,0:T(8,128)(2,1)}, bf16[4,64,256]{2,1,0:T(8,128)(2,1)S(1)}, u32[]{:S(2)}, u32[]{:S(2)}) collective-permute-start(bf16[4,64,256]{2,1,0:T(8,128)(2,1)} %get-tuple-element.55), channel_id=1, source_target_pairs={{16,0},{32,16},{48,32},{64,48},{80,64},{96,80},{112,96},{0,112},{1... | collective-permute-start | bytes 393224 | tf_op jit(solution)/shard_map/ppermute | solution.py:685
  51.3 25.3 %collective-permute-start.7 = (bf16[4,64,256]{2,1,0:T(8,128)(2,1)}, bf16[4,64,256]{2,1,0:T(8,128)(2,1)S(1)}, u32[]{:S(2)}, u32[]{:S(2)}) collective-permute-start(bf16[4,64,256]{2,1,0:T(8,128)(2,1)} %get-tuple-element.56), channel_id=1, source_target_pairs={{0,1},{1,2},{2,3},{3,4},{4,5},{5,6},{6,7},{7,8},{8,9},{9,10},{10,1... | collective-permute-start | bytes 393224 | tf_op jit(solution)/shard_map/ppermute | solution.py:684
  72.1 9.6 %collective-permute-start.8 = (f32[136,256]{1,0:T(8,128)}, f32[136,256]{1,0:T(8,128)S(1)}, u32[]{:S(2)}, u32[]{:S(2)}) collective-permute-start(f32[136,256]{1,0:T(8,128)} %get-tuple-element.58), channel_id=1, source_target_pairs={{0,1},{1,0},{2,3},{3,2},{4,5},{5,4},{6,7},{7,6},{8,9},{9,8},{10,11... | collective-permute-start | bytes 417800 | tf_op jit(solution)/shard_map/ppermute | solution.py:691
  76.6 0.7 copy-start
  76.6 0.7 copy-start.1
  76.6 0.7 copy-start.2
  76.6 0.8 copy-start.3
  77.4 4.2 %copy-start.5 = (f32[136,256]{1,0:T(8,128)S(1)}, f32[136,256]{1,0:T(8,128)}, u32[]{:S(2)}) copy-start(f32[136,256]{1,0:T(8,128)} %get-tuple-element.57) | copy-start | bytes 417796
  81.6 5.4 %collective-permute-start.9 = (f32[136,256]{1,0:T(8,128)S(1)}, f32[136,256]{1,0:T(8,128)S(1)}, u32[]{:S(2)}, u32[]{:S(2)}) collective-permute-start(f32[136,256]{1,0:T(8,128)S(1)} %add.21), channel_id=1, source_target_pairs={{0,2},{1,3},{2,0},{3,1},{4,6},{5,7},{6,4},{7,5},{8,10},{9,11},{10,... | collective-permute-start | bytes 417800 | tf_op jit(solution)/shard_map/ppermute | solution.py:691
  87.0 5.9 %collective-permute-start.10 = (f32[136,256]{1,0:T(8,128)S(1)}, f32[136,256]{1,0:T(8,128)S(1)}, u32[]{:S(2)}, u32[]{:S(2)}) collective-permute-start(f32[136,256]{1,0:T(8,128)S(1)} %add.22), channel_id=1, source_target_pairs={{0,6},{1,7},{2,4},{3,5},{4,2},{5,3},{6,0},{7,1},{8,14},{9,15},{10,... | collective-permute-start | bytes 417800 | tf_op jit(solution)/shard_map/ppermute | solution.py:691
  92.9 6.1 %collective-permute-start.11 = (f32[136,256]{1,0:T(8,128)S(1)}, f32[136,256]{1,0:T(8,128)S(1)}, u32[]{:S(2)}, u32[]{:S(2)}) collective-permute-start(f32[136,256]{1,0:T(8,128)S(1)} %add.23), channel_id=1, source_target_pairs={{0,8},{1,9},{2,10},{3,11},{4,12},{5,13},{6,14},{7,15},{8,0},{9,1},... | collective-permute-start | bytes 417800 | tf_op jit(solution)/shard_map/ppermute | solution.py:691
  99.0 5.2 %collective-permute-start.12 = (f32[136,256]{1,0:T(8,128)S(1)}, f32[136,256]{1,0:T(8,128)S(1)}, u32[]{:S(2)}, u32[]{:S(2)}) collective-permute-start(f32[136,256]{1,0:T(8,128)S(1)} %add.24), channel_id=1, source_target_pairs={{0,24},{1,25},{2,26},{3,27},{4,28},{5,29},{6,30},{7,31},{8,16},{9,... | collective-permute-start | bytes 417800 | tf_op jit(solution)/shard_map/ppermute | solution.py:691
  104.3 4.3 %collective-permute-start.13 = (f32[136,256]{1,0:T(8,128)S(1)}, f32[136,256]{1,0:T(8,128)S(1)}, u32[]{:S(2)}, u32[]{:S(2)}) collective-permute-start(f32[136,256]{1,0:T(8,128)S(1)} %add.25), channel_id=1, source_target_pairs={{0,32},{1,33},{2,34},{3,35},{4,36},{5,37},{6,38},{7,39},{8,40},{9,... | collective-permute-start | bytes 417800 | tf_op jit(solution)/shard_map/ppermute | solution.py:691
  108.6 5.2 %collective-permute-start.14 = (f32[136,256]{1,0:T(8,128)S(1)}, f32[136,256]{1,0:T(8,128)S(1)}, u32[]{:S(2)}, u32[]{:S(2)}) collective-permute-start(f32[136,256]{1,0:T(8,128)S(1)} %add.26), channel_id=1, source_target_pairs={{0,96},{1,97},{2,98},{3,99},{4,100},{5,101},{6,102},{7,103},{8,104... | collective-permute-start | bytes 417800 | tf_op jit(solution)/shard_map/ppermute | solution.py:691
  113.8 9.3 %copy-start.4 = (f32[136,256]{1,0:T(8,128)}, f32[136,256]{1,0:T(8,128)S(1)}, u32[]{:S(2)}) copy-start(f32[136,256]{1,0:T(8,128)S(1)} %add.27.mine_ref) | copy-start | bytes 417796
  113.8 9.3 %collective-permute-start.15 = (f32[136,256]{1,0:T(8,128)S(1)}, f32[136,256]{1,0:T(8,128)S(1)}, u32[]{:S(2)}, u32[]{:S(2)}) collective-permute-start(f32[136,256]{1,0:T(8,128)S(1)} %add.27.mine_ref), channel_id=1, source_target_pairs={{0,1},{1,0},{2,3},{3,2},{4,5},{5,4},{6,7},{7,6},{8,9},{9,8},{10,11... | collective-permute-start | bytes 417800 | tf_op jit(solution)/shard_map/ppermute | solution.py:691
  123.2 0.7 copy-start.6

commit v5 on v4

--- a/solution.py
+++ b/solution.py
@@ -265,11 +265,13 @@
     @pl.when(pl.program_id(0) == 0)
     def _():
         face, tile = where[0], where[1]
+        face_step = 1 - 2 * lax.rem(face, 2)
+        tile_step = 1 - 2 * lax.rem(tile, 2)
         towards = (
-            lax.rem(face + faces - 1, faces) * tiles + tile,
-            face * tiles + lax.rem(tile + 1, tiles),
-            lax.rem(face + 1, faces) * tiles + tile,
-            face * tiles + lax.rem(tile + tiles - 1, tiles),
+            (face + face_step) * tiles + tile,
+            lax.rem(face - face_step + faces, faces) * tiles + tile,
+            face * tiles + tile + tile_step,
+            face * tiles + lax.rem(tile - tile_step + tiles, tiles),
         )
         met = [[jnp.where(links[0, s] == to, 1, 0) for to in towards] for s in range(4)]
         for k in range(4):
@@ -578,7 +580,8 @@
                     out_ref[0, i + q, jb * 16 : jb * 16 + 16, lanes] = jnp.concatenate(pair, axis=0).astype(BF16)
                 return carry
 
-            lax.fori_loop(0, count // rows, body, 0)
+            for it in range(count // rows):
+                body(it, 0)
 
     def add(i, s):
         out_ref[0, i] = (out_ref[0, i].astype(F32) + from_dir(table, got, s).astype(F32)).astype(BF16)
@@ -676,13 +679,17 @@
 
 
 def exchange(facing):
-    got = [None] * 4
-    for axis, low, high in (("face", 0, 2), ("tile", 3, 1)):
-        count = lax.axis_size(axis)
-        up = [(i, (i + 1) % count) for i in range(count)]
-        down = [(target, source) for source, target in up]
-        got[low] = lax.ppermute(facing[high], axis, up)
-        got[high] = lax.ppermute(facing[low], axis, down)
+    faces, tiles = lax.axis_size("face"), lax.axis_size("tile")
+    got = []
+    for d, rows in enumerate(facing):
+        pairs = []
+        for i in range(faces * tiles):
+            at = [i // tiles, i % tiles]
+            k = d // 2
+            step = 1 - 2 * (at[k] % 2)
+            at[k] = (at[k] + (step if d % 2 == 0 else -step)) % (faces, tiles)[k]
+            pairs.append((i, at[0] * tiles + at[1]))
+        got.append(lax.ppermute(rows, ("face", "tile"), pairs))
     return got
 
 

time: 126 us -> 119 us (0.944)
  Pallas kernels: 88.6 us -> 84.2 us
  waiting for transfers between devices: 3.67 us -> 2.07 us
    pallas_call x8, Pallas kernels: 33.7 us -> 29.3 us  [spread_call(): pl.pallas_call(body, grid=(steps,), in_specs=in_specs, out_specs=[rows, p...]
    ppermute x8, waiting for transfers between devices: 3.65 us -> 2.05 us  [swap(): lax.ppermute(value, ('face', 'tile'), [(i, i ^ mask) for i in range(devic...]
  transfers between devices with their start and end apart: 16 -> 16, of which waited for: 4 -> 3; matrix products, arithmetic and copies ran while one was open for 0% -> 0% of each run, Pallas kernels for 60% -> 60%
where the time goes in v5:
time: 119 us
  Pallas kernels  84.2 us (71%)
  starting transfers between devices  28.5 us (24%)
  local copies, waits for them, and re-layouts  2.14 us (2%)
  waiting for transfers between devices  2.07 us (2%)
    pallas_call x2, Pallas kernels, inner_call(): pl.pallas_call(body, grid=(count,), in_specs=in_specs, out_specs=[tile, *...  41.4 us
    pallas_call x8, Pallas kernels, spread_call(): pl.pallas_call(body, grid=(steps,), in_specs=in_specs, out_specs=[rows, p...  29.3 us
    ppermute x8, starting transfers between devices, exchange(): got.append(lax.ppermute(rows, ('face', 'tile'), pairs))  15.7 us
    ppermute x8, starting transfers between devices, swap(): lax.ppermute(value, ('face', 'tile'), [(i, i ^ mask) for i in range(devic...  12.8 us
    pallas_call x1, Pallas kernels, ring_call(): pl.pallas_call(ring_body, grid=(batch,), in_specs=[pl.BlockSpec(memory_sp...  7.7 us
    pallas_call x1, Pallas kernels, edges_call(): pl.pallas_call(functools.partial(edges_body, (lax.axis_size('face'), lax....  4.11 us
  transfers between devices with their start and end apart: 16, of which 3 were waited for; matrix products, arithmetic and copies ran while one was open for 0% of the time, Pallas kernels for 60%

profile of v5, /device:TPU:1, one launch (start us, length us, event | category | flops | bytes accessed | tf_op | source)
XLA Modules:
  0.0 118.5 jit_solution(6392750220071297832)
XLA Ops:
  1.2 4.1 %edges.1 = (bf16[4,64,256]{2,1,0:T(8,128)(2,1)}, bf16[4,64,256]{2,1,0:T(8,128)(2,1)}, bf16[4,64,256]{2,1,0:T(8,128)(2,1)}, bf16[4,64,256]{2,1,0:T(8,128)(2,1)}, s32[17]{0:T(128)}) custom-call(s32[2]{0:T(128)} %pad_add_fusion.where, s32[1,4]{1,0:T(1,128)} %links.1, s32[1,4]{1,0:T(1,128)} %flips.1, s32[1,4]{1,0:T(1,128)} %masks.1, ...), custom_call_target="tpu_custom_call" | custom-call | tf_op jit(solution)/shard_map/edges/pallas_call | solution.py:299
  5.3 4.5 %collective-permute-start = (bf16[4,64,256]{2,1,0:T(8,128)(2,1)}, bf16[4,64,256]{2,1,0:T(8,128)(2,1)S(1)}, u32[]{:S(2)}, u32[]{:S(2)}) collective-permute-start(bf16[4,64,256]{2,1,0:T(8,128)(2,1)} %get-tuple-element.43), channel_id=1, source_target_pairs={{0,16},{1,17},{2,18},{3,19},{4,20},{5,21},{6,22},{7,23},{8,24},{9,... | collective-permute-start | bytes 393224 | tf_op jit(solution)/shard_map/ppermute | solution.py:692
  9.8 2.3 %collective-permute-start.1 = (bf16[4,64,256]{2,1,0:T(8,128)(2,1)}, bf16[4,64,256]{2,1,0:T(8,128)(2,1)S(1)}, u32[]{:S(2)}, u32[]{:S(2)}) collective-permute-start(bf16[4,64,256]{2,1,0:T(8,128)(2,1)} %get-tuple-element.44), channel_id=1, source_target_pairs={{0,112},{1,113},{2,114},{3,115},{4,116},{5,117},{6,118},{7,119},{8... | collective-permute-start | bytes 393224 | tf_op jit(solution)/shard_map/ppermute | solution.py:692
  12.1 1.0 collective-permute-start.2
  13.1 1.2 %collective-permute-start.3 = (bf16[4,64,256]{2,1,0:T(8,128)(2,1)}, bf16[4,64,256]{2,1,0:T(8,128)(2,1)S(1)}, u32[]{:S(2)}, u32[]{:S(2)}) collective-permute-start(bf16[4,64,256]{2,1,0:T(8,128)(2,1)} %get-tuple-element.46), channel_id=1, source_target_pairs={{0,15},{1,2},{2,1},{3,4},{4,3},{5,6},{6,5},{7,8},{8,7},{9,10},{10,... | collective-permute-start | bytes 393224 | tf_op jit(solution)/shard_map/ppermute | solution.py:692
  14.3 20.6 %inner.2 = (bf16[4,64,64,256]{3,2,1,0:T(8,128)(2,1)}, f32[256,256]{1,0:T(8,128)}, f32[2,10,8,128]{3,2,1,0:T(8,128)}) custom-call(bf16[4,64,64,256]{3,2,1,0:T(8,128)(2,1)} %refs_0_.3, bf16[4,64,64,256]{3,2,1,0:T(8,128)(2,1)} %refs_1_.3, bf16[256,256]{1,0:T(8,128)(2,1)} %refs_2_.3, f32[9,256]{1,0:T(8,128)} %refs_9_.7, f32[1,256]{1,0:T(1,128)} %bitcast.4), custom_call_target="tpu_custom_call" | custom-call | flops 20000000000 | bytes 12582912 | tf_op jit(solution)/shard_map/inner/pallas_call | solution.py:215
  35.7 7.7 %ring.1 = (bf16[4,4,64,256]{3,2,1,0:T(8,128)(2,1)}, bf16[4,64,256]{2,1,0:T(8,128)(2,1)}, bf16[4,64,256]{2,1,0:T(8,128)(2,1)}, bf16[4,64,256]{2,1,0:T(8,128)(2,1)...) custom-call(s32[17]{0:T(128)} %get-tuple-element.41.table.refs_5_.refs_0_, ...), custom_call_target="tpu_custom_call" | custom-call | flops 3000000000 | bytes 12582912 | tf_op jit(solution)/shard_map/ring/pallas_call | solution.py:449
  43.4 2.0 %collective-permute-start.4 = (bf16[4,64,256]{2,1,0:T(8,128)(2,1)}, bf16[4,64,256]{2,1,0:T(8,128)(2,1)S(1)}, u32[]{:S(2)}, u32[]{:S(2)}) collective-permute-start(bf16[4,64,256]{2,1,0:T(8,128)(2,1)} %get-tuple-element.53), channel_id=1, source_target_pairs={{0,16},{1,17},{2,18},{3,19},{4,20},{5,21},{6,22},{7,23},{8,24},{9,... | collective-permute-start | bytes 393224 | tf_op jit(solution)/shard_map/ppermute | solution.py:692
  45.4 1.4 %collective-permute-start.5 = (bf16[4,64,256]{2,1,0:T(8,128)(2,1)}, bf16[4,64,256]{2,1,0:T(8,128)(2,1)S(1)}, u32[]{:S(2)}, u32[]{:S(2)}) collective-permute-start(bf16[4,64,256]{2,1,0:T(8,128)(2,1)} %get-tuple-element.54), channel_id=1, source_target_pairs={{0,112},{1,113},{2,114},{3,115},{4,116},{5,117},{6,118},{7,119},{8... | collective-permute-start | bytes 393224 | tf_op jit(solution)/shard_map/ppermute | solution.py:692
  46.7 3.4 %collective-permute-start.6 = (bf16[4,64,256]{2,1,0:T(8,128)(2,1)}, bf16[4,64,256]{2,1,0:T(8,128)(2,1)S(1)}, u32[]{:S(2)}, u32[]{:S(2)}) collective-permute-start(bf16[4,64,256]{2,1,0:T(8,128)(2,1)} %get-tuple-element.55), channel_id=1, source_target_pairs={{0,1},{1,0},{2,3},{3,2},{4,5},{5,4},{6,7},{7,6},{8,9},{9,8},{10,11... | collective-permute-start | bytes 393224 | tf_op jit(solution)/shard_map/ppermute | solution.py:692
  50.2 20.8 %inner.3 = (bf16[4,64,64,256]{3,2,1,0:T(8,128)(2,1)}, f32[136,256]{1,0:T(8,128)}, f32[136,256]{1,0:T(8,128)}) custom-call(bf16[4,64,64,256]{3,2,1,0:T(8,128)(2,1)} %refs_0_.3, bf16[4,64,64,256]{3,2,1,0:T(8,128)(2,1)} %refs_1_.3, bf16[256,256]{1,0:T(8,128)(2,1)} %refs_2_.3, f32[9,256]{1,0:T(8,128)} %refs_9_.7, ...), custom_call_target="tpu_custom_call", output_to_operand_aliasing={{0}: (6, {})} | custom-call | flops 20000000000 | bytes 12582912 | tf_op jit(solution)/shard_map/inner/pallas_call | solution.py:215
  70.9 0.9 collective-permute-start.8
  71.9 0.6 copy-done
  72.6 3.7 %spread.8 = (bf16[4,64,64,256]{3,2,1,0:T(8,128)(2,1)}, f32[8,128]{1,0:T(8,128)}) custom-call(s32[17]{0:T(128)} %get-tuple-element.41.table.refs_5_.refs_0_, bf16[4,64,64,256]{3,2,1,0:T(8,128)(2,1)} %get-tuple-element.51.refs_1_.refs_2_.refs_3_, bf16[4,64,64,256]{3,2,1,0:T(8,128)(2,1)} %get-tuple-element.51.refs_1_.refs_2_.refs_3_, ...), custom_call_target="tpu_custom_call" | custom-call | flops 1500000000 | bytes 2097152 | tf_op jit(solution)/shard_map/spread/pallas_call | solution.py:628
  76.3 1.1 collective-permute-start.9
  77.4 3.6 %spread.9 = (bf16[4,64,64,256]{3,2,1,0:T(8,128)(2,1)}, f32[8,128]{1,0:T(8,128)}) custom-call(s32[17]{0:T(128)} %get-tuple-element.41.table.refs_5_.refs_0_, bf16[4,64,64,256]{3,2,1,0:T(8,128)(2,1)} %get-tuple-element.51.refs_1_.refs_2_.refs_3_, bf16[4,64,64,256]{3,2,1,0:T(8,128)(2,1)} %get-tuple-element.51.refs_1_.refs_2_.refs_3_, ...), custom_call_target="tpu_custom_call", output_to_operand_aliasing={{0}: (10, {})} | custom-call | flops 1500000000 | bytes 2097152 | tf_op jit(solution)/shard_map/spread/pallas_call | solution.py:628
  81.1 0.6 collective-permute-done.9
  81.7 1.4 %collective-permute-start.10 = (f32[136,256]{1,0:T(8,128)S(1)}, f32[136,256]{1,0:T(8,128)S(1)}, u32[]{:S(2)}, u32[]{:S(2)}) collective-permute-start(f32[136,256]{1,0:T(8,128)S(1)} %add.22), channel_id=1, source_target_pairs={{0,6},{1,7},{2,4},{3,5},{4,2},{5,3},{6,0},{7,1},{8,14},{9,15},{10,... | collective-permute-start | bytes 417800 | tf_op jit(solution)/shard_map/ppermute | solution.py:698
  83.2 3.7 %spread.10 = (bf16[4,64,64,256]{3,2,1,0:T(8,128)(2,1)}, f32[8,128]{1,0:T(8,128)}) custom-call(s32[17]{0:T(128)} %get-tuple-element.41.table.refs_5_.refs_0_, bf16[4,64,64,256]{3,2,1,0:T(8,128)(2,1)} %get-tuple-element.51.refs_1_.refs_2_.refs_3_, bf16[4,64,64,256]{3,2,1,0:T(8,128)(2,1)} %get-tuple-element.51.refs_1_.refs_2_.refs_3_, ...), custom_call_target="tpu_custom_call", output_to_operand_aliasing={{0}: (10, {})} | custom-call | flops 1500000000 | bytes 2097152 | tf_op jit(solution)/shard_map/spread/pallas_call | solution.py:628
  86.8 0.8 collective-permute-done.10
  88.1 3.6 %spread.11 = (bf16[4,64,64,256]{3,2,1,0:T(8,128)(2,1)}, f32[8,128]{1,0:T(8,128)}) custom-call(s32[17]{0:T(128)} %get-tuple-element.41.table.refs_5_.refs_0_, bf16[4,64,64,256]{3,2,1,0:T(8,128)(2,1)} %get-tuple-element.51.refs_1_.refs_2_.refs_3_, bf16[4,64,64,256]{3,2,1,0:T(8,128)(2,1)} %get-tuple-element.51.refs_1_.refs_2_.refs_3_, ...), custom_call_target="tpu_custom_call", output_to_operand_aliasing={{0}: (10, {})} | custom-call | flops 1500000000 | bytes 2097152 | tf_op jit(solution)/shard_map/spread/pallas_call | solution.py:628
  91.8 2.6 %collective-permute-start.12 = (f32[136,256]{1,0:T(8,128)S(1)}, f32[136,256]{1,0:T(8,128)S(1)}, u32[]{:S(2)}, u32[]{:S(2)}) collective-permute-start(f32[136,256]{1,0:T(8,128)S(1)} %add.24), channel_id=1, source_target_pairs={{0,24},{1,25},{2,26},{3,27},{4,28},{5,29},{6,30},{7,31},{8,16},{9,... | collective-permute-start | bytes 417800 | tf_op jit(solution)/shard_map/ppermute | solution.py:698
  94.4 3.7 %spread.12 = (bf16[4,64,64,256]{3,2,1,0:T(8,128)(2,1)}, f32[8,128]{1,0:T(8,128)}) custom-call(s32[17]{0:T(128)} %get-tuple-element.41.table.refs_5_.refs_0_, bf16[4,64,64,256]{3,2,1,0:T(8,128)(2,1)} %get-tuple-element.51.refs_1_.refs_2_.refs_3_, bf16[4,64,64,256]{3,2,1,0:T(8,128)(2,1)} %get-tuple-element.51.refs_1_.refs_2_.refs_3_, ...), custom_call_target="tpu_custom_call", output_to_operand_aliasing={{0}: (10, {})} | custom-call | flops 1500000000 | bytes 2097152 | tf_op jit(solution)/shard_map/spread/pallas_call | solution.py:628
  98.1 1.0 collective-permute-start.13
  99.1 3.6 %spread.13 = (bf16[4,64,64,256]{3,2,1,0:T(8,128)(2,1)}, f32[8,128]{1,0:T(8,128)}) custom-call(s32[17]{0:T(128)} %get-tuple-element.41.table.refs_5_.refs_0_, bf16[4,64,64,256]{3,2,1,0:T(8,128)(2,1)} %get-tuple-element.51.refs_1_.refs_2_.refs_3_, bf16[4,64,64,256]{3,2,1,0:T(8,128)(2,1)} %get-tuple-element.51.refs_1_.refs_2_.refs_3_, ...), custom_call_target="tpu_custom_call", output_to_operand_aliasing={{0}: (10, {})} | custom-call | flops 1500000000 | bytes 2097152 | tf_op jit(solution)/shard_map/spread/pallas_call | solution.py:628
  102.8 0.9 collective-permute-start.14
  103.7 3.7 %spread.14 = (bf16[4,64,64,256]{3,2,1,0:T(8,128)(2,1)}, f32[8,128]{1,0:T(8,128)}) custom-call(s32[17]{0:T(128)} %get-tuple-element.41.table.refs_5_.refs_0_, bf16[4,64,64,256]{3,2,1,0:T(8,128)(2,1)} %get-tuple-element.51.refs_1_.refs_2_.refs_3_, bf16[4,64,64,256]{3,2,1,0:T(8,128)(2,1)} %get-tuple-element.51.refs_1_.refs_2_.refs_3_, ...), custom_call_target="tpu_custom_call", output_to_operand_aliasing={{0}: (10, {})} | custom-call | flops 1500000000 | bytes 2097152 | tf_op jit(solution)/shard_map/spread/pallas_call | solution.py:628
  107.4 0.6 collective-permute-done.14
  108.0 4.4 %collective-permute-start.15 = (f32[136,256]{1,0:T(8,128)S(1)}, f32[136,256]{1,0:T(8,128)S(1)}, u32[]{:S(2)}, u32[]{:S(2)}) collective-permute-start(f32[136,256]{1,0:T(8,128)S(1)} %add.27.mine_ref), channel_id=1, source_target_pairs={{0,1},{1,0},{2,3},{3,2},{4,5},{5,4},{6,7},{7,6},{8,9},{9,8},{10,11... | collective-permute-start | bytes 417800 | tf_op jit(solution)/shard_map/ppermute | solution.py:698
  112.5 3.7 %spread.15 = (bf16[4,64,64,256]{3,2,1,0:T(8,128)(2,1)}, f32[8,128]{1,0:T(8,128)}) custom-call(s32[17]{0:T(128)} %get-tuple-element.41.table.refs_5_.refs_0_, bf16[4,64,64,256]{3,2,1,0:T(8,128)(2,1)} %get-tuple-element.51.refs_1_.refs_2_.refs_3_, bf16[4,64,64,256]{3,2,1,0:T(8,128)(2,1)} %get-tuple-element.51.refs_1_.refs_2_.refs_3_, ...), custom_call_target="tpu_custom_call", output_to_operand_aliasing={{0}: (10, {})} | custom-call | flops 1500000000 | bytes 2097152 | tf_op jit(solution)/shard_map/spread/pallas_call | solution.py:628
  116.1 0.6 copy-done.6
  116.8 1.7 %finish.1 = (f32[9,256]{1,0:T(8,128)}, f32[1,256]{1,0:T(1,128)}, f32[256,256]{1,0:T(8,128)}) custom-call(s32[17]{0:T(128)} %get-tuple-element.41.table.refs_5_.refs_0_, f32[136,256]{1,0:T(8,128)} %copy-done.4, f32[136,256]{1,0:T(8,128)} %copy-done.6), custom_call_target="tpu_custom_call" | custom-call | tf_op jit(solution)/shard_map/finish/pallas_call | solution.py:668
  (43 shorter events, 2.2 us)
Async XLA Ops:
  5.3 29.6 %collective-permute-start = (bf16[4,64,256]{2,1,0:T(8,128)(2,1)}, bf16[4,64,256]{2,1,0:T(8,128)(2,1)S(1)}, u32[]{:S(2)}, u32[]{:S(2)}) collective-permute-start(bf16[4,64,256]{2,1,0:T(8,128)(2,1)} %get-tuple-element.43), channel_id=1, source_target_pairs={{0,16},{1,17},{2,18},{3,19},{4,20},{5,21},{6,22},{7,23},{8,24},{9,... | collective-permute-start | bytes 393224 | tf_op jit(solution)/shard_map/ppermute | solution.py:692
  9.8 25.1 %collective-permute-start.1 = (bf16[4,64,256]{2,1,0:T(8,128)(2,1)}, bf16[4,64,256]{2,1,0:T(8,128)(2,1)S(1)}, u32[]{:S(2)}, u32[]{:S(2)}) collective-permute-start(bf16[4,64,256]{2,1,0:T(8,128)(2,1)} %get-tuple-element.44), channel_id=1, source_target_pairs={{0,112},{1,113},{2,114},{3,115},{4,116},{5,117},{6,118},{7,119},{8... | collective-permute-start | bytes 393224 | tf_op jit(solution)/shard_map/ppermute | solution.py:692
  12.1 22.8 %collective-permute-start.2 = (bf16[4,64,256]{2,1,0:T(8,128)(2,1)}, bf16[4,64,256]{2,1,0:T(8,128)(2,1)S(1)}, u32[]{:S(2)}, u32[]{:S(2)}) collective-permute-start(bf16[4,64,256]{2,1,0:T(8,128)(2,1)} %get-tuple-element.45), channel_id=1, source_target_pairs={{0,1},{1,0},{2,3},{3,2},{4,5},{5,4},{6,7},{7,6},{8,9},{9,8},{10,11... | collective-permute-start | bytes 393224 | tf_op jit(solution)/shard_map/ppermute | solution.py:692
  13.1 21.9 %collective-permute-start.3 = (bf16[4,64,256]{2,1,0:T(8,128)(2,1)}, bf16[4,64,256]{2,1,0:T(8,128)(2,1)S(1)}, u32[]{:S(2)}, u32[]{:S(2)}) collective-permute-start(bf16[4,64,256]{2,1,0:T(8,128)(2,1)} %get-tuple-element.46), channel_id=1, source_target_pairs={{0,15},{1,2},{2,1},{3,4},{4,3},{5,6},{6,5},{7,8},{8,7},{9,10},{10,... | collective-permute-start | bytes 393224 | tf_op jit(solution)/shard_map/ppermute | solution.py:692
  34.9 0.6 copy-start.7
  34.9 0.7 copy-start.8
  34.9 0.7 copy-start.9
  35.0 0.8 copy-start.10
  43.4 28.4 %collective-permute-start.4 = (bf16[4,64,256]{2,1,0:T(8,128)(2,1)}, bf16[4,64,256]{2,1,0:T(8,128)(2,1)S(1)}, u32[]{:S(2)}, u32[]{:S(2)}) collective-permute-start(bf16[4,64,256]{2,1,0:T(8,128)(2,1)} %get-tuple-element.53), channel_id=1, source_target_pairs={{0,16},{1,17},{2,18},{3,19},{4,20},{5,21},{6,22},{7,23},{8,24},{9,... | collective-permute-start | bytes 393224 | tf_op jit(solution)/shard_map/ppermute | solution.py:692
  45.4 26.5 %collective-permute-start.5 = (bf16[4,64,256]{2,1,0:T(8,128)(2,1)}, bf16[4,64,256]{2,1,0:T(8,128)(2,1)S(1)}, u32[]{:S(2)}, u32[]{:S(2)}) collective-permute-start(bf16[4,64,256]{2,1,0:T(8,128)(2,1)} %get-tuple-element.54), channel_id=1, source_target_pairs={{0,112},{1,113},{2,114},{3,115},{4,116},{5,117},{6,118},{7,119},{8... | collective-permute-start | bytes 393224 | tf_op jit(solution)/shard_map/ppermute | solution.py:692
  46.7 25.1 %collective-permute-start.6 = (bf16[4,64,256]{2,1,0:T(8,128)(2,1)}, bf16[4,64,256]{2,1,0:T(8,128)(2,1)S(1)}, u32[]{:S(2)}, u32[]{:S(2)}) collective-permute-start(bf16[4,64,256]{2,1,0:T(8,128)(2,1)} %get-tuple-element.55), channel_id=1, source_target_pairs={{0,1},{1,0},{2,3},{3,2},{4,5},{5,4},{6,7},{7,6},{8,9},{9,8},{10,11... | collective-permute-start | bytes 393224 | tf_op jit(solution)/shard_map/ppermute | solution.py:692
  50.2 21.7 %collective-permute-start.7 = (bf16[4,64,256]{2,1,0:T(8,128)(2,1)}, bf16[4,64,256]{2,1,0:T(8,128)(2,1)S(1)}, u32[]{:S(2)}, u32[]{:S(2)}) collective-permute-start(bf16[4,64,256]{2,1,0:T(8,128)(2,1)} %get-tuple-element.56), channel_id=1, source_target_pairs={{0,15},{1,2},{2,1},{3,4},{4,3},{5,6},{6,5},{7,8},{8,7},{9,10},{10,... | collective-permute-start | bytes 393224 | tf_op jit(solution)/shard_map/ppermute | solution.py:692
  70.9 5.4 %collective-permute-start.8 = (f32[136,256]{1,0:T(8,128)}, f32[136,256]{1,0:T(8,128)S(1)}, u32[]{:S(2)}, u32[]{:S(2)}) collective-permute-start(f32[136,256]{1,0:T(8,128)} %get-tuple-element.58), channel_id=1, source_target_pairs={{0,1},{1,0},{2,3},{3,2},{4,5},{5,4},{6,7},{7,6},{8,9},{9,8},{10,11... | collective-permute-start | bytes 417800 | tf_op jit(solution)/shard_map/ppermute | solution.py:698
  71.8 0.7 copy-start
  71.8 0.7 copy-start.1
  71.9 0.7 copy-start.2
  71.9 0.7 copy-start.3
  72.6 3.7 %copy-start.5 = (f32[136,256]{1,0:T(8,128)S(1)}, f32[136,256]{1,0:T(8,128)}, u32[]{:S(2)}) copy-start(f32[136,256]{1,0:T(8,128)} %get-tuple-element.57) | copy-start | bytes 417796
  76.3 5.4 %collective-permute-start.9 = (f32[136,256]{1,0:T(8,128)S(1)}, f32[136,256]{1,0:T(8,128)S(1)}, u32[]{:S(2)}, u32[]{:S(2)}) collective-permute-start(f32[136,256]{1,0:T(8,128)S(1)} %add.21), channel_id=1, source_target_pairs={{0,2},{1,3},{2,0},{3,1},{4,6},{5,7},{6,4},{7,5},{8,10},{9,11},{10,... | collective-permute-start | bytes 417800 | tf_op jit(solution)/shard_map/ppermute | solution.py:698
  81.7 5.9 %collective-permute-start.10 = (f32[136,256]{1,0:T(8,128)S(1)}, f32[136,256]{1,0:T(8,128)S(1)}, u32[]{:S(2)}, u32[]{:S(2)}) collective-permute-start(f32[136,256]{1,0:T(8,128)S(1)} %add.22), channel_id=1, source_target_pairs={{0,6},{1,7},{2,4},{3,5},{4,2},{5,3},{6,0},{7,1},{8,14},{9,15},{10,... | collective-permute-start | bytes 417800 | tf_op jit(solution)/shard_map/ppermute | solution.py:698
  87.6 4.2 %collective-permute-start.11 = (f32[136,256]{1,0:T(8,128)S(1)}, f32[136,256]{1,0:T(8,128)S(1)}, u32[]{:S(2)}, u32[]{:S(2)}) collective-permute-start(f32[136,256]{1,0:T(8,128)S(1)} %add.23), channel_id=1, source_target_pairs={{0,8},{1,9},{2,10},{3,11},{4,12},{5,13},{6,14},{7,15},{8,0},{9,1},... | collective-permute-start | bytes 417800 | tf_op jit(solution)/shard_map/ppermute | solution.py:698
  91.8 6.3 %collective-permute-start.12 = (f32[136,256]{1,0:T(8,128)S(1)}, f32[136,256]{1,0:T(8,128)S(1)}, u32[]{:S(2)}, u32[]{:S(2)}) collective-permute-start(f32[136,256]{1,0:T(8,128)S(1)} %add.24), channel_id=1, source_target_pairs={{0,24},{1,25},{2,26},{3,27},{4,28},{5,29},{6,30},{7,31},{8,16},{9,... | collective-permute-start | bytes 417800 | tf_op jit(solution)/shard_map/ppermute | solution.py:698
  98.1 4.6 %collective-permute-start.13 = (f32[136,256]{1,0:T(8,128)S(1)}, f32[136,256]{1,0:T(8,128)S(1)}, u32[]{:S(2)}, u32[]{:S(2)}) collective-permute-start(f32[136,256]{1,0:T(8,128)S(1)} %add.25), channel_id=1, source_target_pairs={{0,32},{1,33},{2,34},{3,35},{4,36},{5,37},{6,38},{7,39},{8,40},{9,... | collective-permute-start | bytes 417800 | tf_op jit(solution)/shard_map/ppermute | solution.py:698
  102.8 5.2 %collective-permute-start.14 = (f32[136,256]{1,0:T(8,128)S(1)}, f32[136,256]{1,0:T(8,128)S(1)}, u32[]{:S(2)}, u32[]{:S(2)}) collective-permute-start(f32[136,256]{1,0:T(8,128)S(1)} %add.26), channel_id=1, source_target_pairs={{0,96},{1,97},{2,98},{3,99},{4,100},{5,101},{6,102},{7,103},{8,104... | collective-permute-start | bytes 417800 | tf_op jit(solution)/shard_map/ppermute | solution.py:698
  108.0 8.1 %copy-start.4 = (f32[136,256]{1,0:T(8,128)}, f32[136,256]{1,0:T(8,128)S(1)}, u32[]{:S(2)}) copy-start(f32[136,256]{1,0:T(8,128)S(1)} %add.27.mine_ref) | copy-start | bytes 417796
  108.0 8.1 %collective-permute-start.15 = (f32[136,256]{1,0:T(8,128)S(1)}, f32[136,256]{1,0:T(8,128)S(1)}, u32[]{:S(2)}, u32[]{:S(2)}) collective-permute-start(f32[136,256]{1,0:T(8,128)S(1)} %add.27.mine_ref), channel_id=1, source_target_pairs={{0,1},{1,0},{2,3},{3,2},{4,5},{5,4},{6,7},{7,6},{8,9},{9,8},{10,11... | collective-permute-start | bytes 417800 | tf_op jit(solution)/shard_map/ppermute | solution.py:698
  116.1 0.7 copy-start.6

commit v6 on v5

--- a/solution.py
+++ b/solution.py
@@ -40,7 +40,7 @@
     return jnp.broadcast_to(ref[k : k + 1, hf * LANES : hf * LANES + LANES], (SUB, LANES))
 
 
-def inner_body(pairs, carried, x_ref, cot_ref, w_ref, tap_ref, bias_ref, gh_ref, outs, u, hide, acc, half_w, pg_ref, *bufs):
+def inner_body(pairs, x_ref, cot_ref, w_ref, tap_ref, bias_ref, gh_ref, pg_out, dg_out, u, hide, acc, half_w, pg_ref, *bufs):
     step = pl.program_id(0)
     side = x_ref.shape[1]
     cols = x_ref.shape[2]
@@ -163,34 +163,18 @@
     @pl.when(step == pl.num_programs(0) - 1)
     def _():
         point = pg_ref[...] * (0.5 / ALPHA)
-        if carried is None:
-            pg_out, dg_out = outs
-            pg_out[...] = point
-            for hf in range(2):
-                for k, line in enumerate(tap_sums(hf)):
-                    dg_out[hf, k] = line
-            return
-        table, _, pg_in, dg_in = carried
-        mine, sent = outs
-        rows = mine.shape[0]
-        lines = []
+        pg_out[...] = point
         for hf in range(2):
-            own = [jnp.sum(v + dg_in[hf, k], axis=0, keepdims=True) for k, v in enumerate(tap_sums(hf))]
-            lines.append(jnp.concatenate(own + [jnp.zeros((6, LANES), F32)], axis=0))
-        point = point + pg_in[...]
-        low = point[:rows]
-        high = jnp.concatenate([point[rows:], jnp.concatenate(lines, axis=1)], axis=0)
-        first = table[CORE] == 0
-        mine[...] = jnp.where(first, low, high)
-        sent[...] = jnp.where(first, high, low)
+            for k, line in enumerate(tap_sums(hf)):
+                dg_out[hf, k] = line
 
 
 PAIRS = 4
 
 
-def inner_call(first, count, state, cotangent, weight, taps, bias, carried=None):
+def inner_call(state, cotangent, weight, taps, bias):
     batch, side, cols, channels = state.shape
-    tile = pl.BlockSpec((1, side, cols, channels), lambda b: (b + first, 0, 0, 0))
+    tile = pl.BlockSpec((1, side, cols, channels), lambda b: (b, 0, 0, 0))
     whole = lambda *shape: pl.BlockSpec(shape, lambda b: (0,) * len(shape))
     buf = [
         pltpu.VMEM((2, PAIRS, 4, cols + 2 * PAD, LANES), F32),
@@ -198,24 +182,12 @@
         pltpu.VMEM((2 * PAIRS * cols, channels), BF16),
         pltpu.VMEM((2 * PAIRS * cols, channels), BF16),
     ]
-    square, lines, half = (channels, channels), (2, 10, SUB, LANES), ((channels + 16) // 2, channels)
-    in_specs = [tile, tile, whole(*square), whole(9, channels), whole(1, channels)]
-    operands = [state, cotangent, weight, taps, bias]
-    shapes, aliases = (square, lines), {}
-    if carried is not None:
-        in_specs += [pl.BlockSpec(memory_space=pltpu.SMEM), pl.BlockSpec(memory_space=pl.ANY), whole(*square), whole(*lines)]
-        operands += carried
-        shapes, aliases = (half, half), {6: 0}
-    given = len(operands)
-
-    def body(*refs):
-        extra = None if carried is None else refs[5:given]
-        inner_body(PAIRS, extra, *refs[:5], refs[given], refs[given + 1 : given + 3], *refs[given + 3 :])
-
+    square, lines = (channels, channels), (2, 10, SUB, LANES)
+    shapes = (square, lines)
     return pl.pallas_call(
-        body,
-        grid=(count,),
-        in_specs=in_specs,
+        functools.partial(inner_body, PAIRS),
+        grid=(batch,),
+        in_specs=[tile, tile, whole(*square), whole(9, channels), whole(1, channels)],
         out_specs=[tile, *(whole(*shape) for shape in shapes)],
         out_shape=[
             jax.ShapeDtypeStruct(state.shape, BF16),
@@ -230,23 +202,22 @@
             *buf,
             *buf,
         ],
-        input_output_aliases=aliases,
         compiler_params=pltpu.CompilerParams(vmem_limit_bytes=57 << 20),
         cost_estimate=pl.CostEstimate(
-            flops=10_000_000_000 * count, bytes_accessed=state.size * 6 * count // batch, transcendentals=state.size
+            flops=40_000_000_000, bytes_accessed=state.size * 6, transcendentals=state.size
         ),
         name="inner",
-    )(*operands)
+    )(state, cotangent, weight, taps, bias)
 
 
 DIR_OF_SIDE, SIDE_OF_DIR, FLIPS, MASKS, CORE = 0, 4, 8, 12, 16
 
 
-def from_dir(table, got, s):
+def from_dir(table, got, s, b=0):
     d = table[DIR_OF_SIDE + s]
-    rows = got[3][0]
+    rows = got[3][b]
     for k in range(3):
-        rows = jnp.where(d == k, got[k][0], rows)
+        rows = jnp.where(d == k, got[k][b], rows)
     return rows
 
 
@@ -259,7 +230,17 @@
     return jnp.dot(pick, rows, preferred_element_type=F32).astype(BF16)
 
 
-def edges_body(sizes, where, links, flips, masks, top_ref, low_ref, left_ref, right_ref, to0, to1, to2, to3, table, turned):
+def columns(tile, buf, which):
+    rows = tile.shape[0]
+    flat = tile.astype(F32).reshape(rows * SUB, 2 * LANES)
+    for hf in range(2):
+        buf[hf] = flat[:, hf * LANES : hf * LANES + LANES]
+    return [
+        jnp.concatenate([buf[hf, pl.ds(c, rows, stride=SUB), :] for hf in range(2)], axis=1) for c in which
+    ]
+
+
+def edges_body(sizes, where, links, flips, masks, top_ref, low_ref, left_ref, right_ref, to0, to1, to2, to3, table, turned, wide):
     faces, tiles = sizes
 
     @pl.when(pl.program_id(0) == 0)
@@ -282,23 +263,28 @@
         table[CORE] = lax.rem(tile, 2)
 
     last = right_ref.shape[2] - 1
-    turned[0] = turn(table, 0, top_ref[0, 0])
-    turned[1] = turn(table, 1, right_ref[0].astype(F32)[:, last].astype(BF16))
-    turned[2] = turn(table, 2, low_ref[0, 0])
-    turned[3] = turn(table, 3, left_ref[0].astype(F32)[:, 0].astype(BF16))
-    for d, to in enumerate((to0, to1, to2, to3)):
-        to[0] = turned[table[SIDE_OF_DIR + d]]
+    for b in range(top_ref.shape[0]):
+        turned[b, 0] = turn(table, 0, top_ref[b, 0])
+        turned[b, 1] = turn(table, 1, columns(right_ref[b], wide.at[0], (last,))[0].astype(BF16))
+        turned[b, 2] = turn(table, 2, low_ref[b, 0])
+        turned[b, 3] = turn(table, 3, columns(left_ref[b], wide.at[1], (0,))[0].astype(BF16))
+    for b in range(top_ref.shape[0]):
+        for d, to in enumerate((to0, to1, to2, to3)):
+            to[b] = turned[b, table[SIDE_OF_DIR + d]]
+
+
+EDGE_SAMPLES, RING_SAMPLES = 2, 2
 
 
 def edges_call(where, links, flips, masks, state):
     batch, side, cols, channels = state.shape
-    wide = 8
-    one = lambda at: pl.BlockSpec((1, 1, cols, channels), lambda b: (b, at, 0, 0))
-    column = lambda at: pl.BlockSpec((1, side, wide, channels), lambda b: (b, 0, at, 0))
-    facing = pl.BlockSpec((1, side, channels), lambda b: (b, 0, 0))
+    wide, held = 8, EDGE_SAMPLES
+    one = lambda at: pl.BlockSpec((held, 1, cols, channels), lambda b: (b, at, 0, 0))
+    column = lambda at: pl.BlockSpec((held, side, wide, channels), lambda b: (b, 0, at, 0))
+    facing = pl.BlockSpec((held, side, channels), lambda b: (b, 0, 0))
     return pl.pallas_call(
         functools.partial(edges_body, (lax.axis_size("face"), lax.axis_size("tile"))),
-        grid=(batch,),
+        grid=(batch // held,),
         in_specs=[
             *[pl.BlockSpec(memory_space=pltpu.SMEM)] * 4,
             one(0),
@@ -311,7 +297,10 @@
             *[jax.ShapeDtypeStruct((batch, side, channels), BF16)] * 4,
             jax.ShapeDtypeStruct((CORE + 1,), jnp.int32),
         ],
-        scratch_shapes=[pltpu.VMEM((4, side, channels), BF16)],
+        scratch_shapes=[
+            pltpu.VMEM((held, 4, side, channels), BF16),
+            pltpu.VMEM((2, 2, side * SUB, LANES), F32),
+        ],
         compiler_params=pltpu.CompilerParams(vmem_limit_bytes=57 << 20),
         name="edges",
     )(where, links, flips, masks, state, state, state, state)
@@ -324,7 +313,7 @@
 def ring_body(
     table, top_ref, low_ref, left_ref, right_ref, ctop_ref, clow_ref, cleft_ref, cright_ref,
     got0, got1, got2, got3, w_ref, tap_ref, bias_ref, pg_ref, dg_ref,
-    gr_ref, to0, to1, to2, to3, point_ref, line_ref, strip, ext, acts, acc, turned,
+    gr_ref, to0, to1, to2, to3, mine, sent, strip, ext, acts, acc, turned, wide, point_ref,
 ):
     step = pl.program_id(0)
     side = got0.shape[1]
@@ -337,118 +326,131 @@
         point_ref[...] = pg_ref[...]
         ext[...] = jnp.zeros_like(ext)
 
-    rims = [from_dir(table, got, s).astype(F32) for s in range(4)]
-    top = top_ref[0].astype(F32)
-    low = low_ref[0].astype(F32)
-    left = left_ref[0].astype(F32)
-    right = right_ref[0].astype(F32)
-    last = left.shape[1] - 1
-    end = side - 1
-
-    def corner(k, first, second):
-        return (masks[k] * 0.5 * (first + second)).astype(BF16).astype(F32)
-
-    def at(s, i):
-        return rims[s][i : i + 1]
-
-    nw = corner(0, at(0, 0), at(3, 0))
-    ne = corner(1, at(0, end), at(1, 0))
-    se = corner(2, at(1, end), at(2, end))
-    sw = corner(3, at(2, 0), at(3, end))
-    lines = (
-        ((rims[0], nw, ne), (top[0], at(3, 0), at(1, 0)), (top[1], at(3, 1), at(1, 1))),
-        (
-            (right[:, last - 1], at(0, end - 1), at(2, end - 1)),
-            (right[:, last], at(0, end), at(2, end)),
-            (rims[1], ne, se),
-        ),
-        (
-            (low[0], at(3, end - 1), at(1, end - 1)),
-            (low[1], at(3, end), at(1, end)),
-            (rims[2], sw, se),
-        ),
-        ((rims[3], nw, sw), (left[:, 0], at(0, 0), at(2, 0)), (left[:, 1], at(0, 1), at(2, 1))),
-    )
-    for s in range(4):
-        for a in range(3):
-            line, before, after = lines[s][a]
+    def sample(n):
+        rims = [from_dir(table, got, s, n).astype(F32) for s in range(4)]
+        top = top_ref[n].astype(F32)
+        low = low_ref[n].astype(F32)
+        last = SUB - 1
+        left = columns(left_ref[n], wide.at[0], (0, 1))
+        right = columns(right_ref[n], wide.at[1], (last - 1, last))
+        end = side - 1
+
+        def corner(k, first, second):
+            return (masks[k] * 0.5 * (first + second)).astype(BF16).astype(F32)
+
+        def at(s, i):
+            return rims[s][i : i + 1]
+
+        nw = corner(0, at(0, 0), at(3, 0))
+        ne = corner(1, at(0, end), at(1, 0))
+        se = corner(2, at(1, end), at(2, end))
+        sw = corner(3, at(2, 0), at(3, end))
+        lines = (
+            ((rims[0], nw, ne), (top[0], at(3, 0), at(1, 0)), (top[1], at(3, 1), at(1, 1))),
+            (
+                (right[0], at(0, end - 1), at(2, end - 1)),
+                (right[1], at(0, end), at(2, end)),
+                (rims[1], ne, se),
+            ),
+            (
+                (low[0], at(3, end - 1), at(1, end - 1)),
+                (low[1], at(3, end), at(1, end)),
+                (rims[2], sw, se),
+            ),
+            ((rims[3], nw, sw), (left[0], at(0, 0), at(2, 0)), (left[1], at(0, 1), at(2, 1))),
+        )
+        for s in range(4):
+            for a in range(3):
+                line, before, after = lines[s][a]
+                for hf in range(2):
+                    lanes = slice(hf * LANES, hf * LANES + LANES)
+                    strip[n, s, hf, a, PAD : PAD + side, :] = line[:, lanes]
+                    strip[n, s, hf, a, PAD - 1 : PAD, :] = before[:, lanes]
+                    strip[n, s, hf, a, PAD + side : PAD + side + 1, :] = after[:, lanes]
+        cots = jnp.concatenate(
+            [
+                ctop_ref[n, 0].astype(F32),
+                columns(cright_ref[n], wide.at[2], (last,))[0],
+                clow_ref[n, 0].astype(F32),
+                columns(cleft_ref[n], wide.at[3], (0,))[0],
+            ],
+            axis=0,
+        ).astype(BF16)
+        ga = lax.dot_general(cots, w_ref[...], (((1,), (1,)), ((), ())), preferred_element_type=F32)
+        row = lax.broadcasted_iota(jnp.int32, (side, LANES), 0)
+        middle = jnp.logical_and(row > 0, row < end)
+        for s in range(4):
+            upright = s % 2 == 0
+            rim_line = 0 if s in (0, 3) else 2
             for hf in range(2):
                 lanes = slice(hf * LANES, hf * LANES + LANES)
-                strip[s, hf, a, PAD : PAD + side, :] = line[:, lanes]
-                strip[s, hf, a, PAD - 1 : PAD, :] = before[:, lanes]
-                strip[s, hf, a, PAD + side : PAD + side + 1, :] = after[:, lanes]
-    cots = jnp.concatenate(
-        [
-            ctop_ref[0, 0].astype(F32),
-            cright_ref[0].astype(F32)[:, last],
-            clow_ref[0, 0].astype(F32),
-            cleft_ref[0].astype(F32)[:, 0],
-        ],
-        axis=0,
-    ).astype(BF16)
-    ga = lax.dot_general(cots, w_ref[...], (((1,), (1,)), ((), ())), preferred_element_type=F32)
-    row = lax.broadcasted_iota(jnp.int32, (side, LANES), 0)
-    middle = jnp.logical_and(row > 0, row < end)
-    for s in range(4):
-        upright = s % 2 == 0
-        rim_line = 0 if s in (0, 3) else 2
+
+                def tap(a, b):
+                    k = 3 * a + b if upright else 3 * b + a
+                    return k, tap_ref[k : k + 1, lanes]
+
+                h = jnp.zeros((side, LANES), F32) + bias_ref[0:1, lanes]
+                for a in range(3):
+                    for b in range(3):
+                        h = h + tap(a, b)[1] * strip[n, s, hf, a, PAD - 1 + b : PAD - 1 + b + side, :]
+                act, slope = gelu_pair(h)
+                g = (ga[s * side : s * side + side, lanes] * slope).astype(BF16)
+                gr_ref[s, n, :, lanes] = g
+                g = g.astype(F32)
+                counted = g
+                if not upright:
+                    counted = jnp.where(middle, g, 0.0)
+                    act = jnp.where(middle, act, 0.0)
+                acts[n, s * side : s * side + side, lanes] = act.astype(BF16)
+                for a in range(3):
+                    for b in range(3):
+                        k = tap(a, b)[0]
+                        term = counted * strip[n, s, hf, a, PAD - 1 + b : PAD - 1 + b + side, :]
+                        acc[hf, k] += jnp.sum(term.reshape(side // SUB, SUB, LANES), axis=0)
+                acc[hf, 9] += jnp.sum(counted.reshape(side // SUB, SUB, LANES), axis=0)
+                ext[n, PAD : PAD + side, :] = g
+                first, mid, final = (tap(rim_line, b)[1] for b in range(3))
+                back = (
+                    first * ext[n, PAD + 1 : PAD + 1 + side, :]
+                    + mid * g
+                    + final * ext[n, PAD - 1 : PAD - 1 + side, :]
+                )
+                back = back + jnp.where(row == 0, (0.5 * masks[LOW[s]]) * first * g, 0.0)
+                back = back + jnp.where(row == end, (0.5 * masks[HIGH[s]]) * final * g, 0.0)
+                turned[n, s, :, lanes] = turn(table, s, back.astype(BF16))
+        for d, to in enumerate((to0, to1, to2, to3)):
+            to[n] = turned[n, table[SIDE_OF_DIR + d]]
+        point_ref[...] += lax.dot_general(acts[n], cots, (((0,), (0,)), ((), ())), preferred_element_type=F32)
+
+    for n in range(got0.shape[0]):
+        sample(n)
+
+    @pl.when(step == pl.num_programs(0) - 1)
+    def _():
+        rows = mine.shape[0]
+        lines = []
         for hf in range(2):
-            lanes = slice(hf * LANES, hf * LANES + LANES)
-
-            def tap(a, b):
-                k = 3 * a + b if upright else 3 * b + a
-                return k, tap_ref[k : k + 1, lanes]
-
-            h = jnp.zeros((side, LANES), F32) + bias_ref[0:1, lanes]
-            for a in range(3):
-                for b in range(3):
-                    h = h + tap(a, b)[1] * strip[s, hf, a, PAD - 1 + b : PAD - 1 + b + side, :]
-            act, slope = gelu_pair(h)
-            g = (ga[s * side : s * side + side, lanes] * slope).astype(BF16)
-            gr_ref[s, 0, :, lanes] = g
-            g = g.astype(F32)
-            counted = g
-            if not upright:
-                counted = jnp.where(middle, g, 0.0)
-                act = jnp.where(middle, act, 0.0)
-            acts[s * side : s * side + side, lanes] = act.astype(BF16)
-            for a in range(3):
-                for b in range(3):
-                    k = tap(a, b)[0]
-                    term = counted * strip[s, hf, a, PAD - 1 + b : PAD - 1 + b + side, :]
-                    acc[hf, k] += jnp.sum(term.reshape(side // SUB, SUB, LANES), axis=0)
-            acc[hf, 9] += jnp.sum(counted.reshape(side // SUB, SUB, LANES), axis=0)
-            ext[PAD : PAD + side, :] = g
-            first, mid, final = (tap(rim_line, b)[1] for b in range(3))
-            back = (
-                first * ext[PAD + 1 : PAD + 1 + side, :]
-                + mid * g
-                + final * ext[PAD - 1 : PAD - 1 + side, :]
-            )
-            back = back + jnp.where(row == 0, (0.5 * masks[LOW[s]]) * first * g, 0.0)
-            back = back + jnp.where(row == end, (0.5 * masks[HIGH[s]]) * final * g, 0.0)
-            turned[s, :, lanes] = turn(table, s, back.astype(BF16))
-    for d, to in enumerate((to0, to1, to2, to3)):
-        to[0] = turned[table[SIDE_OF_DIR + d]]
-    point_ref[...] += lax.dot_general(acts[...], cots, (((0,), (0,)), ((), ())), preferred_element_type=F32)
-
-    @pl.when(step == pl.num_programs(0) - 1)
-    def _():
-        line_ref[...] = acc[...]
+            own = [jnp.sum(acc[hf, k], axis=0, keepdims=True) for k in range(10)]
+            lines.append(jnp.concatenate(own + [jnp.zeros((6, LANES), F32)], axis=0))
+        low = point_ref[0:rows]
+        high = jnp.concatenate([point_ref[rows:], jnp.concatenate(lines, axis=1)], axis=0)
+        first = table[CORE] == 0
+        mine[...] = jnp.where(first, low, high)
+        sent[...] = jnp.where(first, high, low)
 
 
 def ring_call(table, state, cotangent, got, weight, taps, bias, point_inner, depth_inner):
     batch, side, cols, channels = state.shape
-    wide = 8
-    two = lambda at: pl.BlockSpec((1, 2, cols, channels), lambda b: (b, at, 0, 0))
-    one = lambda at: pl.BlockSpec((1, 1, cols, channels), lambda b: (b, at, 0, 0))
-    column = lambda at: pl.BlockSpec((1, side, wide, channels), lambda b: (b, 0, at, 0))
-    strips = pl.BlockSpec((4, 1, side, channels), lambda b: (0, b, 0, 0))
-    facing = pl.BlockSpec((1, side, channels), lambda b: (b, 0, 0))
+    wide, held, half = 8, RING_SAMPLES, (channels + 16) // 2
+    two = lambda at: pl.BlockSpec((held, 2, cols, channels), lambda b: (b, at, 0, 0))
+    one = lambda at: pl.BlockSpec((held, 1, cols, channels), lambda b: (b, at, 0, 0))
+    column = lambda at: pl.BlockSpec((held, side, wide, channels), lambda b: (b, 0, at, 0))
+    strips = pl.BlockSpec((4, held, side, channels), lambda b: (0, b, 0, 0))
+    facing = pl.BlockSpec((held, side, channels), lambda b: (b, 0, 0))
     far = cols // wide - 1
     return pl.pallas_call(
         ring_body,
-        grid=(batch,),
+        grid=(batch // held,),
         in_specs=[
             pl.BlockSpec(memory_space=pltpu.SMEM),
             two(0),
@@ -469,21 +471,21 @@
         out_specs=[
             strips,
             *[facing] * 4,
-            pl.BlockSpec((channels, channels), lambda b: (0, 0)),
-            pl.BlockSpec((2, 10, SUB, LANES), lambda b: (0, 0, 0, 0)),
+            *[pl.BlockSpec((half, channels), lambda b: (0, 0))] * 2,
         ],
         out_shape=[
             jax.ShapeDtypeStruct((4, batch, side, channels), BF16),
             *[jax.ShapeDtypeStruct((batch, side, channels), BF16)] * 4,
-            jax.ShapeDtypeStruct((channels, channels), F32),
-            jax.ShapeDtypeStruct((2, 10, SUB, LANES), F32),
+            *[jax.ShapeDtypeStruct((half, channels), F32)] * 2,
         ],
         scratch_shapes=[
-            pltpu.VMEM((4, 2, 3, cols + 2 * PAD, LANES), F32),
-            pltpu.VMEM((cols + 2 * PAD, LANES), F32),
-            pltpu.VMEM((4 * side, channels), BF16),
+            pltpu.VMEM((held, 4, 2, 3, cols + 2 * PAD, LANES), F32),
+            pltpu.VMEM((held, cols + 2 * PAD, LANES), F32),
+            pltpu.VMEM((held, 4 * side, channels), BF16),
             pltpu.VMEM((2, 10, SUB, LANES), F32),
-            pltpu.VMEM((4, side, channels), BF16),
+            pltpu.VMEM((held, 4, side, channels), BF16),
+            pltpu.VMEM((4, 2, side * SUB, LANES), F32),
+            pltpu.VMEM((channels, channels), F32),
         ],
         compiler_params=pltpu.CompilerParams(vmem_limit_bytes=57 << 20),
         cost_estimate=pl.CostEstimate(
@@ -715,21 +717,17 @@
     *edges, table = edges_call(where, tile_links, link_flips, corner_masks, state)
     got = exchange(edges)
     layer = (point_weight, depth_weight, bias)
-    early = batch // 2
-    grad, point_sum, depth_sum = inner_call(0, early, state, cotangent, *layer)
-    ring, *facing, point_sum, depth_sum = ring_call(table, state, cotangent, got, *layer, point_sum, depth_sum)
+    grad, point_sum, depth_sum = inner_call(state, cotangent, *layer)
+    ring, *facing, mine, sent = ring_call(table, state, cotangent, got, *layer, point_sum, depth_sum)
     incoming = exchange(facing)
-    grad, mine, sent = inner_call(
-        early, batch - early, state, cotangent, *layer, (table, grad, point_sum, depth_sum)
-    )
 
     first, field_grad = 0, None
     for stage, (mask_bits, steps) in enumerate(
-        ((1, 2), (2, 2), (6, 2), (8, 2), (24, 2), (32, 2), (96, 2), (1, 2))
+        ((1, 0), (2, 2), (6, 2), (8, 2), (24, 3), (32, 2), (96, 3), (1, 2))
     ):
         got = swap(sent if stage == 0 else mine, mask_bits)
         if steps:
-            held = after(depth_weight, mine if stage else sent)
+            held = after(depth_weight, mine)
             field_grad, token = spread_call(first, steps, table, grad, ring, incoming, held, field_grad)
             got = after(got, token)
             first += steps

time: 119 us -> 115 us (0.966)
  Pallas kernels: 84.2 us -> 77.3 us
  waiting for transfers between devices: 2.07 us -> 7.5 us
  starting transfers between devices: 28.5 us -> 25.3 us
    ppermute x8, waiting for transfers between devices: 0.02 us -> 5.84 us  [exchange(): got.append(lax.ppermute(rows, ('face', 'tile'), pairs))]
    pallas_call x3 -> x2, Pallas kernels: 49.1 us -> 44.7 us  [the longest x1 37.5 us: inner_call(): pl.pallas_call(functools.partial(inner_body, PAIRS), grid=(batch,), in_sp...]
    ppermute x8, starting transfers between devices: 15.7 us -> 12.8 us  [exchange(): got.append(lax.ppermute(rows, ('face', 'tile'), pairs))]
    pallas_call x1, Pallas kernels: 4.11 us -> 2.84 us  [edges_call(): pl.pallas_call(functools.partial(edges_body, (lax.axis_size('face'), lax....]
    pallas_call x8 -> x7, Pallas kernels: 29.3 us -> 28 us  [spread_call(): pl.pallas_call(body, grid=(steps,), in_specs=in_specs, out_specs=[rows, p...]
  transfers between devices with their start and end apart: 16 -> 16, of which waited for: 3 -> 4; matrix products, arithmetic and copies ran while one was open for 0% -> 1% of each run, Pallas kernels for 60% -> 57%
where the time goes in v6:
time: 115 us
  Pallas kernels  77.3 us (67%)
  starting transfers between devices  25.3 us (22%)
  waiting for transfers between devices  7.5 us (7%)
  local copies, waits for them, and re-layouts  2.14 us (2%)
  other arithmetic  1.65 us (1%)
    pallas_call x1, Pallas kernels, inner_call(): pl.pallas_call(functools.partial(inner_body, PAIRS), grid=(batch,), in_sp...  37.5 us
    pallas_call x7, Pallas kernels, spread_call(): pl.pallas_call(body, grid=(steps,), in_specs=in_specs, out_specs=[rows, p...  28 us
    ppermute x8, starting transfers between devices, exchange(): got.append(lax.ppermute(rows, ('face', 'tile'), pairs))  12.8 us
    ppermute x8, starting transfers between devices, swap(): lax.ppermute(value, ('face', 'tile'), [(i, i ^ mask) for i in range(devic...  12.4 us
    pallas_call x1, Pallas kernels, ring_call(): pl.pallas_call(ring_body, grid=(batch // held,), in_specs=[pl.BlockSpec(m...  7.11 us
    ppermute x8, waiting for transfers between devices, exchange(): got.append(lax.ppermute(rows, ('face', 'tile'), pairs))  5.84 us
    pallas_call x1, Pallas kernels, edges_call(): pl.pallas_call(functools.partial(edges_body, (lax.axis_size('face'), lax....  2.84 us
  transfers between devices with their start and end apart: 16, of which 4 were waited for; matrix products, arithmetic and copies ran while one was open for 1% of the time, Pallas kernels for 57%

profile of v6, /device:TPU:1, one launch (start us, length us, event | category | flops | bytes accessed | tf_op | source)
XLA Modules:
  0.0 114.6 jit_solution(18205877985762474214)
XLA Ops:
  0.6 0.6 pad_add_fusion.where
  1.2 2.8 %edges.1 = (bf16[4,64,256]{2,1,0:T(8,128)(2,1)}, bf16[4,64,256]{2,1,0:T(8,128)(2,1)}, bf16[4,64,256]{2,1,0:T(8,128)(2,1)}, bf16[4,64,256]{2,1,0:T(8,128)(2,1)}, s32[17]{0:T(128)}) custom-call(s32[2]{0:T(128)} %pad_add_fusion.where, s32[1,4]{1,0:T(1,128)} %links.1, s32[1,4]{1,0:T(1,128)} %flips.1, s32[1,4]{1,0:T(1,128)} %masks.1, ...), custom_call_target="tpu_custom_call" | custom-call | tf_op jit(solution)/shard_map/edges/pallas_call | solution.py:285
  4.1 4.5 %collective-permute-start = (bf16[4,64,256]{2,1,0:T(8,128)(2,1)}, bf16[4,64,256]{2,1,0:T(8,128)(2,1)S(1)}, u32[]{:S(2)}, u32[]{:S(2)}) collective-permute-start(bf16[4,64,256]{2,1,0:T(8,128)(2,1)} %get-tuple-element.38), channel_id=1, source_target_pairs={{0,16},{1,17},{2,18},{3,19},{4,20},{5,21},{6,22},{7,23},{8,24},{9,... | collective-permute-start | bytes 393224 | tf_op jit(solution)/shard_map/ppermute | solution.py:694
  8.6 2.3 %collective-permute-start.1 = (bf16[4,64,256]{2,1,0:T(8,128)(2,1)}, bf16[4,64,256]{2,1,0:T(8,128)(2,1)S(1)}, u32[]{:S(2)}, u32[]{:S(2)}) collective-permute-start(bf16[4,64,256]{2,1,0:T(8,128)(2,1)} %get-tuple-element.39), channel_id=1, source_target_pairs={{0,112},{1,113},{2,114},{3,115},{4,116},{5,117},{6,118},{7,119},{8... | collective-permute-start | bytes 393224 | tf_op jit(solution)/shard_map/ppermute | solution.py:694
  10.9 1.0 collective-permute-start.2
  11.8 1.2 %collective-permute-start.3 = (bf16[4,64,256]{2,1,0:T(8,128)(2,1)}, bf16[4,64,256]{2,1,0:T(8,128)(2,1)S(1)}, u32[]{:S(2)}, u32[]{:S(2)}) collective-permute-start(bf16[4,64,256]{2,1,0:T(8,128)(2,1)} %get-tuple-element.41), channel_id=1, source_target_pairs={{0,15},{1,2},{2,1},{3,4},{4,3},{5,6},{6,5},{7,8},{8,7},{9,10},{10,... | collective-permute-start | bytes 393224 | tf_op jit(solution)/shard_map/ppermute | solution.py:694
  13.0 37.5 %inner.1 = (bf16[4,64,64,256]{3,2,1,0:T(8,128)(2,1)}, f32[256,256]{1,0:T(8,128)}, f32[2,10,8,128]{3,2,1,0:T(8,128)}) custom-call(bf16[4,64,64,256]{3,2,1,0:T(8,128)(2,1)} %right_ref.3, bf16[4,64,64,256]{3,2,1,0:T(8,128)(2,1)} %cright_ref.1, bf16[256,256]{1,0:T(8,128)(2,1)} %w_ref.3, f32[9,256]{1,0:T(8,128)} %refs_9_.6, f32[1,256]{1,0:T(1,128)} %bitcast.4), custom_call_target="tpu_custom_call" | custom-call | flops 40000000000 | bytes 25165824 | tf_op jit(solution)/shard_map/inner/pallas_call | solution.py:187
  50.6 0.6 copy-done.6
  51.4 7.1 %ring.1 = (bf16[4,4,64,256]{3,2,1,0:T(8,128)(2,1)}, bf16[4,64,256]{2,1,0:T(8,128)(2,1)}, bf16[4,64,256]{2,1,0:T(8,128)(2,1)}, bf16[4,64,256]{2,1,0:T(8,128)(2,1)...) custom-call(s32[17]{0:T(128)} %get-tuple-element.36.table.refs_0_, ...), custom_call_target="tpu_custom_call" | custom-call | flops 3000000000 | bytes 12582912 | tf_op jit(solution)/shard_map/ring/pallas_call | solution.py:451
  58.5 2.9 %collective-permute-start.8 = (f32[136,256]{1,0:T(8,128)}, f32[136,256]{1,0:T(8,128)S(1)}, u32[]{:S(2)}, u32[]{:S(2)}) collective-permute-start(f32[136,256]{1,0:T(8,128)} %get-tuple-element.50), channel_id=1, source_target_pairs={{0,1},{1,0},{2,3},{3,2},{4,5},{5,4},{6,7},{7,6},{8,9},{9,8},{10,11... | collective-permute-start | bytes 417800 | tf_op jit(solution)/shard_map/ppermute | solution.py:700
  61.4 2.1 %collective-permute-start.4 = (bf16[4,64,256]{2,1,0:T(8,128)(2,1)}, bf16[4,64,256]{2,1,0:T(8,128)(2,1)S(1)}, u32[]{:S(2)}, u32[]{:S(2)}) collective-permute-start(bf16[4,64,256]{2,1,0:T(8,128)(2,1)} %get-tuple-element.45), channel_id=1, source_target_pairs={{0,16},{1,17},{2,18},{3,19},{4,20},{5,21},{6,22},{7,23},{8,24},{9,... | collective-permute-start | bytes 393224 | tf_op jit(solution)/shard_map/ppermute | solution.py:694
  63.5 1.2 %collective-permute-start.5 = (bf16[4,64,256]{2,1,0:T(8,128)(2,1)}, bf16[4,64,256]{2,1,0:T(8,128)(2,1)S(1)}, u32[]{:S(2)}, u32[]{:S(2)}) collective-permute-start(bf16[4,64,256]{2,1,0:T(8,128)(2,1)} %get-tuple-element.46), channel_id=1, source_target_pairs={{0,112},{1,113},{2,114},{3,115},{4,116},{5,117},{6,118},{7,119},{8... | collective-permute-start | bytes 393224 | tf_op jit(solution)/shard_map/ppermute | solution.py:694
  64.7 0.6 collective-permute-start.6
  65.3 0.9 add.21
  66.3 4.4 %collective-permute-done.4.refs_5_ = bf16[4,64,256]{2,1,0:T(8,128)(2,1)S(1)} collective-permute-done((bf16[4,64,256]{2,1,0:T(8,128)(2,1)}, bf16[4,64,256]{2,1,0:T(8,128)(2,1)S(1)}, u32[]{:S(2)}, u32[]{:S(2)}) %collective-permute-start.4) | collective-permute-done | bytes 131104 | tf_op jit(solution)/shard_map/ppermute | solution.py:694
  70.7 1.5 %collective-permute-done.5.refs_6_ = bf16[4,64,256]{2,1,0:T(8,128)(2,1)S(1)} collective-permute-done((bf16[4,64,256]{2,1,0:T(8,128)(2,1)}, bf16[4,64,256]{2,1,0:T(8,128)(2,1)S(1)}, u32[]{:S(2)}, u32[]{:S(2)}) %collective-permute-start.5) | collective-permute-done | bytes 131104 | tf_op jit(solution)/shard_map/ppermute | solution.py:694
  72.2 0.6 copy-done.1
  72.9 3.7 %spread.7 = (bf16[4,64,64,256]{3,2,1,0:T(8,128)(2,1)}, f32[8,128]{1,0:T(8,128)}) custom-call(s32[17]{0:T(128)} %get-tuple-element.36.table.refs_0_, bf16[4,64,64,256]{3,2,1,0:T(8,128)(2,1)} %get-tuple-element.37.refs_1_.refs_2_.refs_3_, bf16[4,64,64,256]{3,2,1,0:T(8,128)(2,1)} %get-tuple-element.37.refs_1_.refs_2_.refs_3_, ...), custom_call_target="tpu_custom_call" | custom-call | flops 1500000000 | bytes 2097152 | tf_op jit(solution)/shard_map/spread/pallas_call | solution.py:630
  76.7 3.7 %spread.8 = (bf16[4,64,64,256]{3,2,1,0:T(8,128)(2,1)}, f32[8,128]{1,0:T(8,128)}) custom-call(s32[17]{0:T(128)} %get-tuple-element.36.table.refs_0_, bf16[4,64,64,256]{3,2,1,0:T(8,128)(2,1)} %get-tuple-element.37.refs_1_.refs_2_.refs_3_, bf16[4,64,64,256]{3,2,1,0:T(8,128)(2,1)} %get-tuple-element.37.refs_1_.refs_2_.refs_3_, ...), custom_call_target="tpu_custom_call", output_to_operand_aliasing={{0}: (10, {})} | custom-call | flops 1500000000 | bytes 2097152 | tf_op jit(solution)/shard_map/spread/pallas_call | solution.py:630
  80.4 1.4 %collective-permute-done.10 = f32[136,256]{1,0:T(8,128)S(1)} collective-permute-done((f32[136,256]{1,0:T(8,128)S(1)}, f32[136,256]{1,0:T(8,128)S(1)}, u32[]{:S(2)}, u32[]{:S(2)}) %collective-permute-start.10) | collective-permute-done | bytes 139296 | tf_op jit(solution)/shard_map/ppermute | solution.py:700
  81.9 3.7 %spread.9 = (bf16[4,64,64,256]{3,2,1,0:T(8,128)(2,1)}, f32[8,128]{1,0:T(8,128)}) custom-call(s32[17]{0:T(128)} %get-tuple-element.36.table.refs_0_, bf16[4,64,64,256]{3,2,1,0:T(8,128)(2,1)} %get-tuple-element.37.refs_1_.refs_2_.refs_3_, bf16[4,64,64,256]{3,2,1,0:T(8,128)(2,1)} %get-tuple-element.37.refs_1_.refs_2_.refs_3_, ...), custom_call_target="tpu_custom_call", output_to_operand_aliasing={{0}: (10, {})} | custom-call | flops 1500000000 | bytes 2097152 | tf_op jit(solution)/shard_map/spread/pallas_call | solution.py:630
  85.6 0.2 collective-permute-done.11
  85.9 3.0 %collective-permute-start.12 = (f32[136,256]{1,0:T(8,128)S(1)}, f32[136,256]{1,0:T(8,128)S(1)}, u32[]{:S(2)}, u32[]{:S(2)}) collective-permute-start(f32[136,256]{1,0:T(8,128)S(1)} %add.24), channel_id=1, source_target_pairs={{0,24},{1,25},{2,26},{3,27},{4,28},{5,29},{6,30},{7,31},{8,16},{9,... | collective-permute-start | bytes 417800 | tf_op jit(solution)/shard_map/ppermute | solution.py:700
  88.9 4.9 %spread.10 = (bf16[4,64,64,256]{3,2,1,0:T(8,128)(2,1)}, f32[8,128]{1,0:T(8,128)}) custom-call(s32[17]{0:T(128)} %get-tuple-element.36.table.refs_0_, bf16[4,64,64,256]{3,2,1,0:T(8,128)(2,1)} %get-tuple-element.37.refs_1_.refs_2_.refs_3_, bf16[4,64,64,256]{3,2,1,0:T(8,128)(2,1)} %get-tuple-element.37.refs_1_.refs_2_.refs_3_, ...), custom_call_target="tpu_custom_call", output_to_operand_aliasing={{0}: (10, {})} | custom-call | flops 2249999872 | bytes 3145728 | tf_op jit(solution)/shard_map/spread/pallas_call | solution.py:630
  93.8 1.3 %collective-permute-start.13 = (f32[136,256]{1,0:T(8,128)S(1)}, f32[136,256]{1,0:T(8,128)S(1)}, u32[]{:S(2)}, u32[]{:S(2)}) collective-permute-start(f32[136,256]{1,0:T(8,128)S(1)} %add.25), channel_id=1, source_target_pairs={{0,32},{1,33},{2,34},{3,35},{4,36},{5,37},{6,38},{7,39},{8,40},{9,... | collective-permute-start | bytes 417800 | tf_op jit(solution)/shard_map/ppermute | solution.py:700
  95.1 3.6 %spread.11 = (bf16[4,64,64,256]{3,2,1,0:T(8,128)(2,1)}, f32[8,128]{1,0:T(8,128)}) custom-call(s32[17]{0:T(128)} %get-tuple-element.36.table.refs_0_, bf16[4,64,64,256]{3,2,1,0:T(8,128)(2,1)} %get-tuple-element.37.refs_1_.refs_2_.refs_3_, bf16[4,64,64,256]{3,2,1,0:T(8,128)(2,1)} %get-tuple-element.37.refs_1_.refs_2_.refs_3_, ...), custom_call_target="tpu_custom_call", output_to_operand_aliasing={{0}: (10, {})} | custom-call | flops 1500000000 | bytes 2097152 | tf_op jit(solution)/shard_map/spread/pallas_call | solution.py:630
  98.8 1.6 %collective-permute-start.14 = (f32[136,256]{1,0:T(8,128)S(1)}, f32[136,256]{1,0:T(8,128)S(1)}, u32[]{:S(2)}, u32[]{:S(2)}) collective-permute-start(f32[136,256]{1,0:T(8,128)S(1)} %add.26), channel_id=1, source_target_pairs={{0,96},{1,97},{2,98},{3,99},{4,100},{5,101},{6,102},{7,103},{8,104... | collective-permute-start | bytes 417800 | tf_op jit(solution)/shard_map/ppermute | solution.py:700
  100.4 4.8 %spread.12 = (bf16[4,64,64,256]{3,2,1,0:T(8,128)(2,1)}, f32[8,128]{1,0:T(8,128)}) custom-call(s32[17]{0:T(128)} %get-tuple-element.36.table.refs_0_, bf16[4,64,64,256]{3,2,1,0:T(8,128)(2,1)} %get-tuple-element.37.refs_1_.refs_2_.refs_3_, bf16[4,64,64,256]{3,2,1,0:T(8,128)(2,1)} %get-tuple-element.37.refs_1_.refs_2_.refs_3_, ...), custom_call_target="tpu_custom_call", output_to_operand_aliasing={{0}: (10, {})} | custom-call | flops 2249999872 | bytes 3145728 | tf_op jit(solution)/shard_map/spread/pallas_call | solution.py:630
  105.3 3.3 %collective-permute-start.15 = (f32[136,256]{1,0:T(8,128)S(1)}, f32[136,256]{1,0:T(8,128)S(1)}, u32[]{:S(2)}, u32[]{:S(2)}) collective-permute-start(f32[136,256]{1,0:T(8,128)S(1)} %add.27.mine_ref), channel_id=1, source_target_pairs={{0,1},{1,0},{2,3},{3,2},{4,5},{5,4},{6,7},{7,6},{8,9},{9,8},{10,11... | collective-permute-start | bytes 417800 | tf_op jit(solution)/shard_map/ppermute | solution.py:700
  108.6 3.6 %spread.13 = (bf16[4,64,64,256]{3,2,1,0:T(8,128)(2,1)}, f32[8,128]{1,0:T(8,128)}) custom-call(s32[17]{0:T(128)} %get-tuple-element.36.table.refs_0_, bf16[4,64,64,256]{3,2,1,0:T(8,128)(2,1)} %get-tuple-element.37.refs_1_.refs_2_.refs_3_, bf16[4,64,64,256]{3,2,1,0:T(8,128)(2,1)} %get-tuple-element.37.refs_1_.refs_2_.refs_3_, ...), custom_call_target="tpu_custom_call", output_to_operand_aliasing={{0}: (10, {})} | custom-call | flops 1500000000 | bytes 2097152 | tf_op jit(solution)/shard_map/spread/pallas_call | solution.py:630
  112.3 0.6 copy-done.5
  112.9 1.7 %finish.1 = (f32[9,256]{1,0:T(8,128)}, f32[1,256]{1,0:T(1,128)}, f32[256,256]{1,0:T(8,128)}) custom-call(s32[17]{0:T(128)} %get-tuple-element.36.table.refs_0_, f32[136,256]{1,0:T(8,128)} %copy-done.4, f32[136,256]{1,0:T(8,128)} %copy-done.5), custom_call_target="tpu_custom_call" | custom-call | tf_op jit(solution)/shard_map/finish/pallas_call | solution.py:670
  (39 shorter events, 0.7 us)
Async XLA Ops:
  4.1 46.5 %collective-permute-start = (bf16[4,64,256]{2,1,0:T(8,128)(2,1)}, bf16[4,64,256]{2,1,0:T(8,128)(2,1)S(1)}, u32[]{:S(2)}, u32[]{:S(2)}) collective-permute-start(bf16[4,64,256]{2,1,0:T(8,128)(2,1)} %get-tuple-element.38), channel_id=1, source_target_pairs={{0,16},{1,17},{2,18},{3,19},{4,20},{5,21},{6,22},{7,23},{8,24},{9,... | collective-permute-start | bytes 393224 | tf_op jit(solution)/shard_map/ppermute | solution.py:694
  8.6 42.0 %collective-permute-start.1 = (bf16[4,64,256]{2,1,0:T(8,128)(2,1)}, bf16[4,64,256]{2,1,0:T(8,128)(2,1)S(1)}, u32[]{:S(2)}, u32[]{:S(2)}) collective-permute-start(bf16[4,64,256]{2,1,0:T(8,128)(2,1)} %get-tuple-element.39), channel_id=1, source_target_pairs={{0,112},{1,113},{2,114},{3,115},{4,116},{5,117},{6,118},{7,119},{8... | collective-permute-start | bytes 393224 | tf_op jit(solution)/shard_map/ppermute | solution.py:694
  10.9 39.7 %collective-permute-start.2 = (bf16[4,64,256]{2,1,0:T(8,128)(2,1)}, bf16[4,64,256]{2,1,0:T(8,128)(2,1)S(1)}, u32[]{:S(2)}, u32[]{:S(2)}) collective-permute-start(bf16[4,64,256]{2,1,0:T(8,128)(2,1)} %get-tuple-element.40), channel_id=1, source_target_pairs={{0,1},{1,0},{2,3},{3,2},{4,5},{5,4},{6,7},{7,6},{8,9},{9,8},{10,11... | collective-permute-start | bytes 393224 | tf_op jit(solution)/shard_map/ppermute | solution.py:694
  11.8 38.8 %collective-permute-start.3 = (bf16[4,64,256]{2,1,0:T(8,128)(2,1)}, bf16[4,64,256]{2,1,0:T(8,128)(2,1)S(1)}, u32[]{:S(2)}, u32[]{:S(2)}) collective-permute-start(bf16[4,64,256]{2,1,0:T(8,128)(2,1)} %get-tuple-element.41), channel_id=1, source_target_pairs={{0,15},{1,2},{2,1},{3,4},{4,3},{5,6},{6,5},{7,8},{8,7},{9,10},{10,... | collective-permute-start | bytes 393224 | tf_op jit(solution)/shard_map/ppermute | solution.py:694
  50.5 0.7 copy-start.6
  50.6 0.7 copy-start.7
  50.6 0.7 copy-start.8
  50.6 0.8 copy-start.9
  58.5 6.8 %collective-permute-start.8 = (f32[136,256]{1,0:T(8,128)}, f32[136,256]{1,0:T(8,128)S(1)}, u32[]{:S(2)}, u32[]{:S(2)}) collective-permute-start(f32[136,256]{1,0:T(8,128)} %get-tuple-element.50), channel_id=1, source_target_pairs={{0,1},{1,0},{2,3},{3,2},{4,5},{5,4},{6,7},{7,6},{8,9},{9,8},{10,11... | collective-permute-start | bytes 417800 | tf_op jit(solution)/shard_map/ppermute | solution.py:700
  61.4 9.3 %collective-permute-start.4 = (bf16[4,64,256]{2,1,0:T(8,128)(2,1)}, bf16[4,64,256]{2,1,0:T(8,128)(2,1)S(1)}, u32[]{:S(2)}, u32[]{:S(2)}) collective-permute-start(bf16[4,64,256]{2,1,0:T(8,128)(2,1)} %get-tuple-element.45), channel_id=1, source_target_pairs={{0,16},{1,17},{2,18},{3,19},{4,20},{5,21},{6,22},{7,23},{8,24},{9,... | collective-permute-start | bytes 393224 | tf_op jit(solution)/shard_map/ppermute | solution.py:694
  63.5 8.7 %collective-permute-start.5 = (bf16[4,64,256]{2,1,0:T(8,128)(2,1)}, bf16[4,64,256]{2,1,0:T(8,128)(2,1)S(1)}, u32[]{:S(2)}, u32[]{:S(2)}) collective-permute-start(bf16[4,64,256]{2,1,0:T(8,128)(2,1)} %get-tuple-element.46), channel_id=1, source_target_pairs={{0,112},{1,113},{2,114},{3,115},{4,116},{5,117},{6,118},{7,119},{8... | collective-permute-start | bytes 393224 | tf_op jit(solution)/shard_map/ppermute | solution.py:694
  64.7 7.5 %collective-permute-start.6 = (bf16[4,64,256]{2,1,0:T(8,128)(2,1)}, bf16[4,64,256]{2,1,0:T(8,128)(2,1)S(1)}, u32[]{:S(2)}, u32[]{:S(2)}) collective-permute-start(bf16[4,64,256]{2,1,0:T(8,128)(2,1)} %get-tuple-element.47), channel_id=1, source_target_pairs={{0,1},{1,0},{2,3},{3,2},{4,5},{5,4},{6,7},{7,6},{8,9},{9,8},{10,11... | collective-permute-start | bytes 393224 | tf_op jit(solution)/shard_map/ppermute | solution.py:694
  65.3 6.9 %collective-permute-start.7 = (bf16[4,64,256]{2,1,0:T(8,128)(2,1)}, bf16[4,64,256]{2,1,0:T(8,128)(2,1)S(1)}, u32[]{:S(2)}, u32[]{:S(2)}) collective-permute-start(bf16[4,64,256]{2,1,0:T(8,128)(2,1)} %get-tuple-element.48), channel_id=1, source_target_pairs={{0,15},{1,2},{2,1},{3,4},{4,3},{5,6},{6,5},{7,8},{8,7},{9,10},{10,... | collective-permute-start | bytes 393224 | tf_op jit(solution)/shard_map/ppermute | solution.py:694
  66.3 10.3 %collective-permute-start.9 = (f32[136,256]{1,0:T(8,128)S(1)}, f32[136,256]{1,0:T(8,128)S(1)}, u32[]{:S(2)}, u32[]{:S(2)}) collective-permute-start(f32[136,256]{1,0:T(8,128)S(1)} %add.21), channel_id=1, source_target_pairs={{0,2},{1,3},{2,0},{3,1},{4,6},{5,7},{6,4},{7,5},{8,10},{9,11},{10,... | collective-permute-start | bytes 417800 | tf_op jit(solution)/shard_map/ppermute | solution.py:700
  70.7 1.5 %copy-start = (bf16[4,64,256]{2,1,0:T(8,128)(2,1)}, bf16[4,64,256]{2,1,0:T(8,128)(2,1)S(1)}, u32[]{:S(2)}) copy-start(bf16[4,64,256]{2,1,0:T(8,128)(2,1)S(1)} %collective-permute-done.4.refs_5_) | copy-start | bytes 393220
  72.2 0.6 copy-start.1
  72.2 0.7 copy-start.2
  72.2 0.7 copy-start.3
  76.6 5.2 %collective-permute-start.10 = (f32[136,256]{1,0:T(8,128)S(1)}, f32[136,256]{1,0:T(8,128)S(1)}, u32[]{:S(2)}, u32[]{:S(2)}) collective-permute-start(f32[136,256]{1,0:T(8,128)S(1)} %add.22), channel_id=1, source_target_pairs={{0,6},{1,7},{2,4},{3,5},{4,2},{5,3},{6,0},{7,1},{8,14},{9,15},{10,... | collective-permute-start | bytes 417800 | tf_op jit(solution)/shard_map/ppermute | solution.py:700
  81.8 4.0 %collective-permute-start.11 = (f32[136,256]{1,0:T(8,128)S(1)}, f32[136,256]{1,0:T(8,128)S(1)}, u32[]{:S(2)}, u32[]{:S(2)}) collective-permute-start(f32[136,256]{1,0:T(8,128)S(1)} %add.23), channel_id=1, source_target_pairs={{0,8},{1,9},{2,10},{3,11},{4,12},{5,13},{6,14},{7,15},{8,0},{9,1},... | collective-permute-start | bytes 417800 | tf_op jit(solution)/shard_map/ppermute | solution.py:700
  85.9 8.0 %collective-permute-start.12 = (f32[136,256]{1,0:T(8,128)S(1)}, f32[136,256]{1,0:T(8,128)S(1)}, u32[]{:S(2)}, u32[]{:S(2)}) collective-permute-start(f32[136,256]{1,0:T(8,128)S(1)} %add.24), channel_id=1, source_target_pairs={{0,24},{1,25},{2,26},{3,27},{4,28},{5,29},{6,30},{7,31},{8,16},{9,... | collective-permute-start | bytes 417800 | tf_op jit(solution)/shard_map/ppermute | solution.py:700
  93.8 4.9 %collective-permute-start.13 = (f32[136,256]{1,0:T(8,128)S(1)}, f32[136,256]{1,0:T(8,128)S(1)}, u32[]{:S(2)}, u32[]{:S(2)}) collective-permute-start(f32[136,256]{1,0:T(8,128)S(1)} %add.25), channel_id=1, source_target_pairs={{0,32},{1,33},{2,34},{3,35},{4,36},{5,37},{6,38},{7,39},{8,40},{9,... | collective-permute-start | bytes 417800 | tf_op jit(solution)/shard_map/ppermute | solution.py:700
  98.8 6.4 %collective-permute-start.14 = (f32[136,256]{1,0:T(8,128)S(1)}, f32[136,256]{1,0:T(8,128)S(1)}, u32[]{:S(2)}, u32[]{:S(2)}) collective-permute-start(f32[136,256]{1,0:T(8,128)S(1)} %add.26), channel_id=1, source_target_pairs={{0,96},{1,97},{2,98},{3,99},{4,100},{5,101},{6,102},{7,103},{8,104... | collective-permute-start | bytes 417800 | tf_op jit(solution)/shard_map/ppermute | solution.py:700
  105.3 7.0 %copy-start.4 = (f32[136,256]{1,0:T(8,128)}, f32[136,256]{1,0:T(8,128)S(1)}, u32[]{:S(2)}) copy-start(f32[136,256]{1,0:T(8,128)S(1)} %add.27.mine_ref) | copy-start | bytes 417796
  105.3 7.0 %collective-permute-start.15 = (f32[136,256]{1,0:T(8,128)S(1)}, f32[136,256]{1,0:T(8,128)S(1)}, u32[]{:S(2)}, u32[]{:S(2)}) collective-permute-start(f32[136,256]{1,0:T(8,128)S(1)} %add.27.mine_ref), channel_id=1, source_target_pairs={{0,1},{1,0},{2,3},{3,2},{4,5},{5,4},{6,7},{7,6},{8,9},{9,8},{10,11... | collective-permute-start | bytes 417800 | tf_op jit(solution)/shard_map/ppermute | solution.py:700
  112.3 0.7 copy-start.5

commit v7 on v6

--- a/solution.py
+++ b/solution.py
@@ -649,37 +649,6 @@
     )(*operands)
 
 
-def finish_body(scale, table, mine_ref, other_ref, dg_ref, bg_ref, pg_ref):
-    rows = mine_ref.shape[0]
-    channels = pg_ref.shape[0]
-    own = mine_ref[...] * scale
-    far = other_ref[...] * scale
-    first = table[CORE] == 0
-    low = jnp.where(first, own, far)
-    high = jnp.where(first, far, own)
-    pg_ref[0:rows, :] = low
-    pg_ref[rows:channels, :] = high[: channels - rows]
-    tail = high[channels - rows :]
-    dg_ref[...] = tail[0:9]
-    bg_ref[...] = tail[9:10]
-
-
-def finish_call(scale, bit, mine, other):
-    channels = mine.shape[1]
-    vmem = pl.BlockSpec(memory_space=pltpu.VMEM)
-    return pl.pallas_call(
-        functools.partial(finish_body, scale),
-        in_specs=[pl.BlockSpec(memory_space=pltpu.SMEM), vmem, vmem],
-        out_specs=[vmem, vmem, vmem],
-        out_shape=[
-            jax.ShapeDtypeStruct((9, channels), F32),
-            jax.ShapeDtypeStruct((1, channels), F32),
-            jax.ShapeDtypeStruct((channels, channels), F32),
-        ],
-        name="finish",
-    )(bit, mine, other)
-
-
 def exchange(facing):
     faces, tiles = lax.axis_size("face"), lax.axis_size("tile")
     got = []
@@ -722,20 +691,23 @@
     incoming = exchange(facing)
 
     first, field_grad = 0, None
-    for stage, (mask_bits, steps) in enumerate(
-        ((1, 0), (2, 2), (6, 2), (8, 2), (24, 3), (32, 2), (96, 3), (1, 2))
-    ):
-        got = swap(sent if stage == 0 else mine, mask_bits)
+    for stage, (mask_bits, steps) in enumerate(((1, 0), (2, 2), (6, 3), (8, 2), (24, 3), (32, 3), (96, 3))):
+        last = mask_bits == 96
+        got = [swap(sent if stage == 0 else mine, bits) for bits in ((96, 1, 97) if last else (mask_bits,))]
         if steps:
             held = after(depth_weight, mine)
             field_grad, token = spread_call(first, steps, table, grad, ring, incoming, held, field_grad)
-            got = after(got, token)
+            got = lax.optimization_barrier((*got, token))[:-1]
             first += steps
-        if stage < 7:
-            mine = mine + got
+        mine = mine + got[0]
+    other = got[1] + got[2]
     scale = float(batch * side * cols * face_count * tile_count) ** -0.5
-    depth_grad, bias_grad, point_grad = finish_call(scale, table, mine, got)
-    return field_grad, depth_grad, bias_grad.reshape(channels), point_grad
+    core = tile_pos % 2
+    rows = channels - mine.shape[0]
+    low = jnp.where(core == 0, mine, other) * scale
+    high = jnp.where(core == 0, other, mine) * scale
+    point_grad = jnp.concatenate([low, high[:rows]], axis=0)
+    return field_grad, high[rows : rows + 9], high[rows + 9], point_grad
 
 
 def solution(mesh):

time: 115 us -> 114 us (level)
  Pallas kernels: 77.3 us -> 74.3 us
    pallas_call x1 -> x0, Pallas kernels: 1.72 us -> none  [finish_call(): pl.pallas_call(functools.partial(finish_body, scale), in_specs=[pl.BlockS...]
    pallas_call x7 -> x6, Pallas kernels: 28 us -> 26.8 us  [spread_call(): pl.pallas_call(body, grid=(steps,), in_specs=in_specs, out_specs=[rows, p...]
    slice x0 -> x3, local copies, waits for them, and re-layouts: none -> 1.18 us  [the longest x2 1.17 us: shards(): return (field_grad, high[rows:rows + 9], high[rows + 9], point_grad)]
    ppermute x8 -> x9, starting transfers between devices: 12.4 us -> 13.3 us  [swap(): lax.ppermute(value, ('face', 'tile'), [(i, i ^ mask) for i in range(devic...]
  transfers between devices with their start and end apart: 16 -> 17, of which waited for: 4 -> 4; matrix products, arithmetic and copies ran while one was open for 1% -> 1% of each run, Pallas kernels for 57% -> 57%
where the time goes in v7:
time: 114 us; the launch traced here: 113 us
  Pallas kernels  74.3 us (65%)
  starting transfers between devices  26.1 us (23%)
  waiting for transfers between devices  6.88 us (6%)
  local copies, waits for them, and re-layouts  2.67 us (2%)
  other arithmetic  2.41 us (2%)
    pallas_call x1, Pallas kernels, inner_call(): pl.pallas_call(functools.partial(inner_body, PAIRS), grid=(batch,), in_sp...  37.5 us
    pallas_call x6, Pallas kernels, spread_call(): pl.pallas_call(body, grid=(steps,), in_specs=in_specs, out_specs=[rows, p...  26.8 us
    ppermute x9, starting transfers between devices, swap(): lax.ppermute(value, ('face', 'tile'), [(i, i ^ mask) for i in range(devic...  13.3 us
    ppermute x8, starting transfers between devices, exchange(): got.append(lax.ppermute(rows, ('face', 'tile'), pairs))  12.8 us
    pallas_call x1, Pallas kernels, ring_call(): pl.pallas_call(ring_body, grid=(batch // held,), in_specs=[pl.BlockSpec(m...  7.12 us
    ppermute x8, waiting for transfers between devices, exchange(): got.append(lax.ppermute(rows, ('face', 'tile'), pairs))  5.82 us
    pallas_call x1, Pallas kernels, edges_call(): pl.pallas_call(functools.partial(edges_body, (lax.axis_size('face'), lax....  2.84 us
  transfers between devices with their start and end apart: 17, of which 4 were waited for; matrix products, arithmetic and copies ran while one was open for 1% of the time, Pallas kernels for 57%

profile of v7, /device:TPU:1, one launch (start us, length us, event | category | flops | bytes accessed | tf_op | source)
XLA Modules:
  0.0 113.2 jit_solution(6955176337031380075)
XLA Ops:
  0.6 0.6 pad_add_fusion.where
  1.2 2.8 %edges.1 = (bf16[4,64,256]{2,1,0:T(8,128)(2,1)}, bf16[4,64,256]{2,1,0:T(8,128)(2,1)}, bf16[4,64,256]{2,1,0:T(8,128)(2,1)}, bf16[4,64,256]{2,1,0:T(8,128)(2,1)}, s32[17]{0:T(128)}) custom-call(s32[2]{0:T(128)} %pad_add_fusion.where, s32[1,4]{1,0:T(1,128)} %links.1, s32[1,4]{1,0:T(1,128)} %flips.1, s32[1,4]{1,0:T(1,128)} %masks.1, ...), custom_call_target="tpu_custom_call" | custom-call | tf_op jit(solution)/shard_map/edges/pallas_call | solution.py:285
  4.1 4.5 %collective-permute-start = (bf16[4,64,256]{2,1,0:T(8,128)(2,1)}, bf16[4,64,256]{2,1,0:T(8,128)(2,1)S(1)}, u32[]{:S(2)}, u32[]{:S(2)}) collective-permute-start(bf16[4,64,256]{2,1,0:T(8,128)(2,1)} %get-tuple-element.36), channel_id=1, source_target_pairs={{0,16},{1,17},{2,18},{3,19},{4,20},{5,21},{6,22},{7,23},{8,24},{9,... | collective-permute-start | bytes 393224 | tf_op jit(solution)/shard_map/ppermute | solution.py:663
  8.6 2.3 %collective-permute-start.1 = (bf16[4,64,256]{2,1,0:T(8,128)(2,1)}, bf16[4,64,256]{2,1,0:T(8,128)(2,1)S(1)}, u32[]{:S(2)}, u32[]{:S(2)}) collective-permute-start(bf16[4,64,256]{2,1,0:T(8,128)(2,1)} %get-tuple-element.37), channel_id=1, source_target_pairs={{0,112},{1,113},{2,114},{3,115},{4,116},{5,117},{6,118},{7,119},{8... | collective-permute-start | bytes 393224 | tf_op jit(solution)/shard_map/ppermute | solution.py:663
  10.9 1.0 collective-permute-start.2
  11.8 1.2 %collective-permute-start.3 = (bf16[4,64,256]{2,1,0:T(8,128)(2,1)}, bf16[4,64,256]{2,1,0:T(8,128)(2,1)S(1)}, u32[]{:S(2)}, u32[]{:S(2)}) collective-permute-start(bf16[4,64,256]{2,1,0:T(8,128)(2,1)} %get-tuple-element.39), channel_id=1, source_target_pairs={{0,15},{1,2},{2,1},{3,4},{4,3},{5,6},{6,5},{7,8},{8,7},{9,10},{10,... | collective-permute-start | bytes 393224 | tf_op jit(solution)/shard_map/ppermute | solution.py:663
  13.0 37.5 %inner.1 = (bf16[4,64,64,256]{3,2,1,0:T(8,128)(2,1)}, f32[256,256]{1,0:T(8,128)}, f32[2,10,8,128]{3,2,1,0:T(8,128)}) custom-call(bf16[4,64,64,256]{3,2,1,0:T(8,128)(2,1)} %right_ref.3, bf16[4,64,64,256]{3,2,1,0:T(8,128)(2,1)} %cright_ref.1, bf16[256,256]{1,0:T(8,128)(2,1)} %w_ref.3, f32[9,256]{1,0:T(8,128)} %refs_9_.5, f32[1,256]{1,0:T(1,128)} %bitcast.4), custom_call_target="tpu_custom_call" | custom-call | flops 40000000000 | bytes 25165824 | tf_op jit(solution)/shard_map/inner/pallas_call | solution.py:187
  50.6 0.6 copy-done.4
  51.4 7.1 %ring.1 = (bf16[4,4,64,256]{3,2,1,0:T(8,128)(2,1)}, bf16[4,64,256]{2,1,0:T(8,128)(2,1)}, bf16[4,64,256]{2,1,0:T(8,128)(2,1)}, bf16[4,64,256]{2,1,0:T(8,128)(2,1)...) custom-call(s32[17]{0:T(128)} %get-tuple-element.34.table.refs_0_, ...), custom_call_target="tpu_custom_call" | custom-call | flops 3000000000 | bytes 12582912 | tf_op jit(solution)/shard_map/ring/pallas_call | solution.py:451
  58.5 2.9 %collective-permute-start.8 = (f32[136,256]{1,0:T(8,128)}, f32[136,256]{1,0:T(8,128)S(1)}, u32[]{:S(2)}, u32[]{:S(2)}) collective-permute-start(f32[136,256]{1,0:T(8,128)} %get-tuple-element.48), channel_id=1, source_target_pairs={{0,1},{1,0},{2,3},{3,2},{4,5},{5,4},{6,7},{7,6},{8,9},{9,8},{10,11... | collective-permute-start | bytes 417800 | tf_op jit(solution)/shard_map/ppermute | solution.py:669
  61.5 2.0 %collective-permute-start.4 = (bf16[4,64,256]{2,1,0:T(8,128)(2,1)}, bf16[4,64,256]{2,1,0:T(8,128)(2,1)S(1)}, u32[]{:S(2)}, u32[]{:S(2)}) collective-permute-start(bf16[4,64,256]{2,1,0:T(8,128)(2,1)} %get-tuple-element.43), channel_id=1, source_target_pairs={{0,16},{1,17},{2,18},{3,19},{4,20},{5,21},{6,22},{7,23},{8,24},{9,... | collective-permute-start | bytes 393224 | tf_op jit(solution)/shard_map/ppermute | solution.py:663
  63.5 1.2 %collective-permute-start.5 = (bf16[4,64,256]{2,1,0:T(8,128)(2,1)}, bf16[4,64,256]{2,1,0:T(8,128)(2,1)S(1)}, u32[]{:S(2)}, u32[]{:S(2)}) collective-permute-start(bf16[4,64,256]{2,1,0:T(8,128)(2,1)} %get-tuple-element.44), channel_id=1, source_target_pairs={{0,112},{1,113},{2,114},{3,115},{4,116},{5,117},{6,118},{7,119},{8... | collective-permute-start | bytes 393224 | tf_op jit(solution)/shard_map/ppermute | solution.py:663
  64.7 0.6 collective-permute-start.6
  65.4 0.9 add.28
  66.4 4.4 %collective-permute-done.4.refs_5_ = bf16[4,64,256]{2,1,0:T(8,128)(2,1)S(1)} collective-permute-done((bf16[4,64,256]{2,1,0:T(8,128)(2,1)}, bf16[4,64,256]{2,1,0:T(8,128)(2,1)S(1)}, u32[]{:S(2)}, u32[]{:S(2)}) %collective-permute-start.4) | collective-permute-done | bytes 131104 | tf_op jit(solution)/shard_map/ppermute | solution.py:663
  70.7 1.5 %collective-permute-done.5.refs_6_ = bf16[4,64,256]{2,1,0:T(8,128)(2,1)S(1)} collective-permute-done((bf16[4,64,256]{2,1,0:T(8,128)(2,1)}, bf16[4,64,256]{2,1,0:T(8,128)(2,1)S(1)}, u32[]{:S(2)}, u32[]{:S(2)}) %collective-permute-start.5) | collective-permute-done | bytes 131104 | tf_op jit(solution)/shard_map/ppermute | solution.py:663
  72.2 0.6 copy-done.1
  72.9 3.7 %spread.6 = (bf16[4,64,64,256]{3,2,1,0:T(8,128)(2,1)}, f32[8,128]{1,0:T(8,128)}) custom-call(s32[17]{0:T(128)} %get-tuple-element.34.table.refs_0_, bf16[4,64,64,256]{3,2,1,0:T(8,128)(2,1)} %get-tuple-element.35.refs_1_.refs_2_.refs_3_, bf16[4,64,64,256]{3,2,1,0:T(8,128)(2,1)} %get-tuple-element.35.refs_1_.refs_2_.refs_3_, ...), custom_call_target="tpu_custom_call" | custom-call | flops 1500000000 | bytes 2097152 | tf_op jit(solution)/shard_map/spread/pallas_call | solution.py:630
  76.7 4.9 %spread.7 = (bf16[4,64,64,256]{3,2,1,0:T(8,128)(2,1)}, f32[8,128]{1,0:T(8,128)}) custom-call(s32[17]{0:T(128)} %get-tuple-element.34.table.refs_0_, bf16[4,64,64,256]{3,2,1,0:T(8,128)(2,1)} %get-tuple-element.35.refs_1_.refs_2_.refs_3_, bf16[4,64,64,256]{3,2,1,0:T(8,128)(2,1)} %get-tuple-element.35.refs_1_.refs_2_.refs_3_, ...), custom_call_target="tpu_custom_call", output_to_operand_aliasing={{0}: (10, {})} | custom-call | flops 2249999872 | bytes 3145728 | tf_op jit(solution)/shard_map/spread/pallas_call | solution.py:630
  81.8 0.6 collective-permute-start.11
  82.4 3.6 %spread.8 = (bf16[4,64,64,256]{3,2,1,0:T(8,128)(2,1)}, f32[8,128]{1,0:T(8,128)}) custom-call(s32[17]{0:T(128)} %get-tuple-element.34.table.refs_0_, bf16[4,64,64,256]{3,2,1,0:T(8,128)(2,1)} %get-tuple-element.35.refs_1_.refs_2_.refs_3_, bf16[4,64,64,256]{3,2,1,0:T(8,128)(2,1)} %get-tuple-element.35.refs_1_.refs_2_.refs_3_, ...), custom_call_target="tpu_custom_call", output_to_operand_aliasing={{0}: (10, {})} | custom-call | flops 1500000000 | bytes 2097152 | tf_op jit(solution)/shard_map/spread/pallas_call | solution.py:630
  86.1 2.8 %collective-permute-start.12 = (f32[136,256]{1,0:T(8,128)S(1)}, f32[136,256]{1,0:T(8,128)S(1)}, u32[]{:S(2)}, u32[]{:S(2)}) collective-permute-start(f32[136,256]{1,0:T(8,128)S(1)} %add.31), channel_id=1, source_target_pairs={{0,24},{1,25},{2,26},{3,27},{4,28},{5,29},{6,30},{7,31},{8,16},{9,... | collective-permute-start | bytes 417800 | tf_op jit(solution)/shard_map/ppermute | solution.py:669
  88.9 4.8 %spread.9 = (bf16[4,64,64,256]{3,2,1,0:T(8,128)(2,1)}, f32[8,128]{1,0:T(8,128)}) custom-call(s32[17]{0:T(128)} %get-tuple-element.34.table.refs_0_, bf16[4,64,64,256]{3,2,1,0:T(8,128)(2,1)} %get-tuple-element.35.refs_1_.refs_2_.refs_3_, bf16[4,64,64,256]{3,2,1,0:T(8,128)(2,1)} %get-tuple-element.35.refs_1_.refs_2_.refs_3_, ...), custom_call_target="tpu_custom_call", output_to_operand_aliasing={{0}: (10, {})} | custom-call | flops 2249999872 | bytes 3145728 | tf_op jit(solution)/shard_map/spread/pallas_call | solution.py:630
  93.7 1.3 %collective-permute-start.13 = (f32[136,256]{1,0:T(8,128)S(1)}, f32[136,256]{1,0:T(8,128)S(1)}, u32[]{:S(2)}, u32[]{:S(2)}) collective-permute-start(f32[136,256]{1,0:T(8,128)S(1)} %add.32), channel_id=1, source_target_pairs={{0,32},{1,33},{2,34},{3,35},{4,36},{5,37},{6,38},{7,39},{8,40},{9,... | collective-permute-start | bytes 417800 | tf_op jit(solution)/shard_map/ppermute | solution.py:669
  95.0 4.9 %spread.10 = (bf16[4,64,64,256]{3,2,1,0:T(8,128)(2,1)}, f32[8,128]{1,0:T(8,128)}) custom-call(s32[17]{0:T(128)} %get-tuple-element.34.table.refs_0_, bf16[4,64,64,256]{3,2,1,0:T(8,128)(2,1)} %get-tuple-element.35.refs_1_.refs_2_.refs_3_, bf16[4,64,64,256]{3,2,1,0:T(8,128)(2,1)} %get-tuple-element.35.refs_1_.refs_2_.refs_3_, ...), custom_call_target="tpu_custom_call", output_to_operand_aliasing={{0}: (10, {})} | custom-call | flops 2249999872 | bytes 3145728 | tf_op jit(solution)/shard_map/spread/pallas_call | solution.py:630
  100.0 1.6 %collective-permute-start.14 = (f32[136,256]{1,0:T(8,128)S(1)}, f32[136,256]{1,0:T(8,128)S(1)}, u32[]{:S(2)}, u32[]{:S(2)}) collective-permute-start(f32[136,256]{1,0:T(8,128)S(1)} %add.33), channel_id=1, source_target_pairs={{0,96},{1,97},{2,98},{3,99},{4,100},{5,101},{6,102},{7,103},{8,104... | collective-permute-start | bytes 417800 | tf_op jit(solution)/shard_map/ppermute | solution.py:669
  101.6 2.9 %collective-permute-start.15 = (f32[136,256]{1,0:T(8,128)S(1)}, f32[136,256]{1,0:T(8,128)S(1)}, u32[]{:S(2)}, u32[]{:S(2)}) collective-permute-start(f32[136,256]{1,0:T(8,128)S(1)} %add.33), channel_id=1, source_target_pairs={{0,1},{1,0},{2,3},{3,2},{4,5},{5,4},{6,7},{7,6},{8,9},{9,8},{10,11... | collective-permute-start | bytes 417800 | tf_op jit(solution)/shard_map/ppermute | solution.py:669
  104.5 1.0 collective-permute-start.16
  105.5 4.8 %spread.11 = (bf16[4,64,64,256]{3,2,1,0:T(8,128)(2,1)}, f32[8,128]{1,0:T(8,128)}) custom-call(s32[17]{0:T(128)} %get-tuple-element.34.table.refs_0_, bf16[4,64,64,256]{3,2,1,0:T(8,128)(2,1)} %get-tuple-element.35.refs_1_.refs_2_.refs_3_, bf16[4,64,64,256]{3,2,1,0:T(8,128)(2,1)} %get-tuple-element.35.refs_1_.refs_2_.refs_3_, ...), custom_call_target="tpu_custom_call", output_to_operand_aliasing={{0}: (10, {})} | custom-call | flops 2249999872 | bytes 3145728 | tf_op jit(solution)/shard_map/spread/pallas_call | solution.py:630
  110.4 0.9 collective-permute-done.16
  111.3 0.6 slice.12
  112.5 0.7 pad_maximum_fusion
  (39 shorter events, 1.4 us)
Async XLA Ops:
  4.1 46.5 %collective-permute-start = (bf16[4,64,256]{2,1,0:T(8,128)(2,1)}, bf16[4,64,256]{2,1,0:T(8,128)(2,1)S(1)}, u32[]{:S(2)}, u32[]{:S(2)}) collective-permute-start(bf16[4,64,256]{2,1,0:T(8,128)(2,1)} %get-tuple-element.36), channel_id=1, source_target_pairs={{0,16},{1,17},{2,18},{3,19},{4,20},{5,21},{6,22},{7,23},{8,24},{9,... | collective-permute-start | bytes 393224 | tf_op jit(solution)/shard_map/ppermute | solution.py:663
  8.6 42.0 %collective-permute-start.1 = (bf16[4,64,256]{2,1,0:T(8,128)(2,1)}, bf16[4,64,256]{2,1,0:T(8,128)(2,1)S(1)}, u32[]{:S(2)}, u32[]{:S(2)}) collective-permute-start(bf16[4,64,256]{2,1,0:T(8,128)(2,1)} %get-tuple-element.37), channel_id=1, source_target_pairs={{0,112},{1,113},{2,114},{3,115},{4,116},{5,117},{6,118},{7,119},{8... | collective-permute-start | bytes 393224 | tf_op jit(solution)/shard_map/ppermute | solution.py:663
  10.9 39.7 %collective-permute-start.2 = (bf16[4,64,256]{2,1,0:T(8,128)(2,1)}, bf16[4,64,256]{2,1,0:T(8,128)(2,1)S(1)}, u32[]{:S(2)}, u32[]{:S(2)}) collective-permute-start(bf16[4,64,256]{2,1,0:T(8,128)(2,1)} %get-tuple-element.38), channel_id=1, source_target_pairs={{0,1},{1,0},{2,3},{3,2},{4,5},{5,4},{6,7},{7,6},{8,9},{9,8},{10,11... | collective-permute-start | bytes 393224 | tf_op jit(solution)/shard_map/ppermute | solution.py:663
  11.8 38.8 %collective-permute-start.3 = (bf16[4,64,256]{2,1,0:T(8,128)(2,1)}, bf16[4,64,256]{2,1,0:T(8,128)(2,1)S(1)}, u32[]{:S(2)}, u32[]{:S(2)}) collective-permute-start(bf16[4,64,256]{2,1,0:T(8,128)(2,1)} %get-tuple-element.39), channel_id=1, source_target_pairs={{0,15},{1,2},{2,1},{3,4},{4,3},{5,6},{6,5},{7,8},{8,7},{9,10},{10,... | collective-permute-start | bytes 393224 | tf_op jit(solution)/shard_map/ppermute | solution.py:663
  50.5 0.6 copy-start.4
  50.6 0.7 copy-start.5
  50.6 0.7 copy-start.6
  50.6 0.8 copy-start.7
  58.5 6.8 %collective-permute-start.8 = (f32[136,256]{1,0:T(8,128)}, f32[136,256]{1,0:T(8,128)S(1)}, u32[]{:S(2)}, u32[]{:S(2)}) collective-permute-start(f32[136,256]{1,0:T(8,128)} %get-tuple-element.48), channel_id=1, source_target_pairs={{0,1},{1,0},{2,3},{3,2},{4,5},{5,4},{6,7},{7,6},{8,9},{9,8},{10,11... | collective-permute-start | bytes 417800 | tf_op jit(solution)/shard_map/ppermute | solution.py:669
  61.5 9.3 %collective-permute-start.4 = (bf16[4,64,256]{2,1,0:T(8,128)(2,1)}, bf16[4,64,256]{2,1,0:T(8,128)(2,1)S(1)}, u32[]{:S(2)}, u32[]{:S(2)}) collective-permute-start(bf16[4,64,256]{2,1,0:T(8,128)(2,1)} %get-tuple-element.43), channel_id=1, source_target_pairs={{0,16},{1,17},{2,18},{3,19},{4,20},{5,21},{6,22},{7,23},{8,24},{9,... | collective-permute-start | bytes 393224 | tf_op jit(solution)/shard_map/ppermute | solution.py:663
  63.5 8.7 %collective-permute-start.5 = (bf16[4,64,256]{2,1,0:T(8,128)(2,1)}, bf16[4,64,256]{2,1,0:T(8,128)(2,1)S(1)}, u32[]{:S(2)}, u32[]{:S(2)}) collective-permute-start(bf16[4,64,256]{2,1,0:T(8,128)(2,1)} %get-tuple-element.44), channel_id=1, source_target_pairs={{0,112},{1,113},{2,114},{3,115},{4,116},{5,117},{6,118},{7,119},{8... | collective-permute-start | bytes 393224 | tf_op jit(solution)/shard_map/ppermute | solution.py:663
  64.7 7.5 %collective-permute-start.6 = (bf16[4,64,256]{2,1,0:T(8,128)(2,1)}, bf16[4,64,256]{2,1,0:T(8,128)(2,1)S(1)}, u32[]{:S(2)}, u32[]{:S(2)}) collective-permute-start(bf16[4,64,256]{2,1,0:T(8,128)(2,1)} %get-tuple-element.45), channel_id=1, source_target_pairs={{0,1},{1,0},{2,3},{3,2},{4,5},{5,4},{6,7},{7,6},{8,9},{9,8},{10,11... | collective-permute-start | bytes 393224 | tf_op jit(solution)/shard_map/ppermute | solution.py:663
  65.3 6.8 %collective-permute-start.7 = (bf16[4,64,256]{2,1,0:T(8,128)(2,1)}, bf16[4,64,256]{2,1,0:T(8,128)(2,1)S(1)}, u32[]{:S(2)}, u32[]{:S(2)}) collective-permute-start(bf16[4,64,256]{2,1,0:T(8,128)(2,1)} %get-tuple-element.46), channel_id=1, source_target_pairs={{0,15},{1,2},{2,1},{3,4},{4,3},{5,6},{6,5},{7,8},{8,7},{9,10},{10,... | collective-permute-start | bytes 393224 | tf_op jit(solution)/shard_map/ppermute | solution.py:663
  66.3 10.3 %collective-permute-start.9 = (f32[136,256]{1,0:T(8,128)S(1)}, f32[136,256]{1,0:T(8,128)S(1)}, u32[]{:S(2)}, u32[]{:S(2)}) collective-permute-start(f32[136,256]{1,0:T(8,128)S(1)} %add.28), channel_id=1, source_target_pairs={{0,2},{1,3},{2,0},{3,1},{4,6},{5,7},{6,4},{7,5},{8,10},{9,11},{10,... | collective-permute-start | bytes 417800 | tf_op jit(solution)/shard_map/ppermute | solution.py:669
  70.7 1.5 %copy-start = (bf16[4,64,256]{2,1,0:T(8,128)(2,1)}, bf16[4,64,256]{2,1,0:T(8,128)(2,1)S(1)}, u32[]{:S(2)}) copy-start(bf16[4,64,256]{2,1,0:T(8,128)(2,1)S(1)} %collective-permute-done.4.refs_5_) | copy-start | bytes 393220
  72.2 0.7 copy-start.1
  72.2 0.7 copy-start.2
  72.2 0.7 copy-start.3
  76.6 5.2 %collective-permute-start.10 = (f32[136,256]{1,0:T(8,128)S(1)}, f32[136,256]{1,0:T(8,128)S(1)}, u32[]{:S(2)}, u32[]{:S(2)}) collective-permute-start(f32[136,256]{1,0:T(8,128)S(1)} %add.29), channel_id=1, source_target_pairs={{0,6},{1,7},{2,4},{3,5},{4,2},{5,3},{6,0},{7,1},{8,14},{9,15},{10,... | collective-permute-start | bytes 417800 | tf_op jit(solution)/shard_map/ppermute | solution.py:669
  81.8 4.2 %collective-permute-start.11 = (f32[136,256]{1,0:T(8,128)S(1)}, f32[136,256]{1,0:T(8,128)S(1)}, u32[]{:S(2)}, u32[]{:S(2)}) collective-permute-start(f32[136,256]{1,0:T(8,128)S(1)} %add.30), channel_id=1, source_target_pairs={{0,8},{1,9},{2,10},{3,11},{4,12},{5,13},{6,14},{7,15},{8,0},{9,1},... | collective-permute-start | bytes 417800 | tf_op jit(solution)/shard_map/ppermute | solution.py:669
  86.1 7.6 %collective-permute-start.12 = (f32[136,256]{1,0:T(8,128)S(1)}, f32[136,256]{1,0:T(8,128)S(1)}, u32[]{:S(2)}, u32[]{:S(2)}) collective-permute-start(f32[136,256]{1,0:T(8,128)S(1)} %add.31), channel_id=1, source_target_pairs={{0,24},{1,25},{2,26},{3,27},{4,28},{5,29},{6,30},{7,31},{8,16},{9,... | collective-permute-start | bytes 417800 | tf_op jit(solution)/shard_map/ppermute | solution.py:669
  93.7 6.2 %collective-permute-start.13 = (f32[136,256]{1,0:T(8,128)S(1)}, f32[136,256]{1,0:T(8,128)S(1)}, u32[]{:S(2)}, u32[]{:S(2)}) collective-permute-start(f32[136,256]{1,0:T(8,128)S(1)} %add.32), channel_id=1, source_target_pairs={{0,32},{1,33},{2,34},{3,35},{4,36},{5,37},{6,38},{7,39},{8,40},{9,... | collective-permute-start | bytes 417800 | tf_op jit(solution)/shard_map/ppermute | solution.py:669
  100.0 10.4 %collective-permute-start.14 = (f32[136,256]{1,0:T(8,128)S(1)}, f32[136,256]{1,0:T(8,128)S(1)}, u32[]{:S(2)}, u32[]{:S(2)}) collective-permute-start(f32[136,256]{1,0:T(8,128)S(1)} %add.33), channel_id=1, source_target_pairs={{0,96},{1,97},{2,98},{3,99},{4,100},{5,101},{6,102},{7,103},{8,104... | collective-permute-start | bytes 417800 | tf_op jit(solution)/shard_map/ppermute | solution.py:669
  101.6 8.8 %collective-permute-start.15 = (f32[136,256]{1,0:T(8,128)S(1)}, f32[136,256]{1,0:T(8,128)S(1)}, u32[]{:S(2)}, u32[]{:S(2)}) collective-permute-start(f32[136,256]{1,0:T(8,128)S(1)} %add.33), channel_id=1, source_target_pairs={{0,1},{1,0},{2,3},{3,2},{4,5},{5,4},{6,7},{7,6},{8,9},{9,8},{10,11... | collective-permute-start | bytes 417800 | tf_op jit(solution)/shard_map/ppermute | solution.py:669
  104.5 6.8 %collective-permute-start.16 = (f32[136,256]{1,0:T(8,128)S(1)}, f32[136,256]{1,0:T(8,128)S(1)}, u32[]{:S(2)}, u32[]{:S(2)}) collective-permute-start(f32[136,256]{1,0:T(8,128)S(1)} %add.33), channel_id=1, source_target_pairs={{0,97},{1,96},{2,99},{3,98},{4,101},{5,100},{6,103},{7,102},{8,105... | collective-permute-start | bytes 417800 | tf_op jit(solution)/shard_map/ppermute | solution.py:669

commit v8 on v7

--- a/solution.py
+++ b/solution.py
@@ -691,7 +691,7 @@
     incoming = exchange(facing)
 
     first, field_grad = 0, None
-    for stage, (mask_bits, steps) in enumerate(((1, 0), (2, 2), (6, 3), (8, 2), (24, 3), (32, 3), (96, 3))):
+    for stage, (mask_bits, steps) in enumerate(((1, 0), (2, 2), (6, 3), (8, 2), (24, 3), (32, 2), (96, 4))):
         last = mask_bits == 96
         got = [swap(sent if stage == 0 else mine, bits) for bits in ((96, 1, 97) if last else (mask_bits,))]
         if steps:

time: 114 us -> 113 us (level)
  transfers between devices with their start and end apart: 17 -> 17, of which waited for: 4 -> 3; matrix products, arithmetic and copies ran while one was open for 1% -> 1% of each run, Pallas kernels for 57% -> 57%
where the time goes in v8:
time: 113 us
  Pallas kernels  74 us (65%)
  starting transfers between devices  26.9 us (24%)
  waiting for transfers between devices  6.02 us (5%)
  local copies, waits for them, and re-layouts  2.67 us (2%)
  other arithmetic  2.41 us (2%)
    pallas_call x1, Pallas kernels, inner_call(): pl.pallas_call(functools.partial(inner_body, PAIRS), grid=(batch,), in_sp...  37.5 us
    pallas_call x6, Pallas kernels, spread_call(): pl.pallas_call(body, grid=(steps,), in_specs=in_specs, out_specs=[rows, p...  26.5 us
    ppermute x9, starting transfers between devices, swap(): lax.ppermute(value, ('face', 'tile'), [(i, i ^ mask) for i in range(devic...  14.1 us
    ppermute x8, starting transfers between devices, exchange(): got.append(lax.ppermute(rows, ('face', 'tile'), pairs))  12.8 us
    pallas_call x1, Pallas kernels, ring_call(): pl.pallas_call(ring_body, grid=(batch // held,), in_specs=[pl.BlockSpec(m...  7.12 us
    ppermute x8, waiting for transfers between devices, exchange(): got.append(lax.ppermute(rows, ('face', 'tile'), pairs))  5.83 us
    pallas_call x1, Pallas kernels, edges_call(): pl.pallas_call(functools.partial(edges_body, (lax.axis_size('face'), lax....  2.84 us
  transfers between devices with their start and end apart: 17, of which 3 were waited for; matrix products, arithmetic and copies ran while one was open for 1% of the time, Pallas kernels for 57%

profile of v8, /device:TPU:1, one launch (start us, length us, event | category | flops | bytes accessed | tf_op | source)
XLA Modules:
  0.0 112.9 jit_solution(17690574208078873902)
XLA Ops:
  0.6 0.6 pad_add_fusion.where
  1.2 2.8 %edges.1 = (bf16[4,64,256]{2,1,0:T(8,128)(2,1)}, bf16[4,64,256]{2,1,0:T(8,128)(2,1)}, bf16[4,64,256]{2,1,0:T(8,128)(2,1)}, bf16[4,64,256]{2,1,0:T(8,128)(2,1)}, s32[17]{0:T(128)}) custom-call(s32[2]{0:T(128)} %pad_add_fusion.where, s32[1,4]{1,0:T(1,128)} %links.1, s32[1,4]{1,0:T(1,128)} %flips.1, s32[1,4]{1,0:T(1,128)} %masks.1, ...), custom_call_target="tpu_custom_call" | custom-call | tf_op jit(solution)/shard_map/edges/pallas_call | solution.py:285
  4.1 4.5 %collective-permute-start = (bf16[4,64,256]{2,1,0:T(8,128)(2,1)}, bf16[4,64,256]{2,1,0:T(8,128)(2,1)S(1)}, u32[]{:S(2)}, u32[]{:S(2)}) collective-permute-start(bf16[4,64,256]{2,1,0:T(8,128)(2,1)} %get-tuple-element.36), channel_id=1, source_target_pairs={{0,16},{1,17},{2,18},{3,19},{4,20},{5,21},{6,22},{7,23},{8,24},{9,... | collective-permute-start | bytes 393224 | tf_op jit(solution)/shard_map/ppermute | solution.py:663
  8.6 2.3 %collective-permute-start.1 = (bf16[4,64,256]{2,1,0:T(8,128)(2,1)}, bf16[4,64,256]{2,1,0:T(8,128)(2,1)S(1)}, u32[]{:S(2)}, u32[]{:S(2)}) collective-permute-start(bf16[4,64,256]{2,1,0:T(8,128)(2,1)} %get-tuple-element.37), channel_id=1, source_target_pairs={{0,112},{1,113},{2,114},{3,115},{4,116},{5,117},{6,118},{7,119},{8... | collective-permute-start | bytes 393224 | tf_op jit(solution)/shard_map/ppermute | solution.py:663
  10.9 1.0 collective-permute-start.2
  11.8 1.2 %collective-permute-start.3 = (bf16[4,64,256]{2,1,0:T(8,128)(2,1)}, bf16[4,64,256]{2,1,0:T(8,128)(2,1)S(1)}, u32[]{:S(2)}, u32[]{:S(2)}) collective-permute-start(bf16[4,64,256]{2,1,0:T(8,128)(2,1)} %get-tuple-element.39), channel_id=1, source_target_pairs={{0,15},{1,2},{2,1},{3,4},{4,3},{5,6},{6,5},{7,8},{8,7},{9,10},{10,... | collective-permute-start | bytes 393224 | tf_op jit(solution)/shard_map/ppermute | solution.py:663
  13.0 37.5 %inner.1 = (bf16[4,64,64,256]{3,2,1,0:T(8,128)(2,1)}, f32[256,256]{1,0:T(8,128)}, f32[2,10,8,128]{3,2,1,0:T(8,128)}) custom-call(bf16[4,64,64,256]{3,2,1,0:T(8,128)(2,1)} %right_ref.3, bf16[4,64,64,256]{3,2,1,0:T(8,128)(2,1)} %cright_ref.1, bf16[256,256]{1,0:T(8,128)(2,1)} %w_ref.3, f32[9,256]{1,0:T(8,128)} %refs_9_.5, f32[1,256]{1,0:T(1,128)} %bitcast.4), custom_call_target="tpu_custom_call" | custom-call | flops 40000000000 | bytes 25165824 | tf_op jit(solution)/shard_map/inner/pallas_call | solution.py:187
  50.6 0.6 copy-done.4
  51.4 7.1 %ring.1 = (bf16[4,4,64,256]{3,2,1,0:T(8,128)(2,1)}, bf16[4,64,256]{2,1,0:T(8,128)(2,1)}, bf16[4,64,256]{2,1,0:T(8,128)(2,1)}, bf16[4,64,256]{2,1,0:T(8,128)(2,1)...) custom-call(s32[17]{0:T(128)} %get-tuple-element.34.table.refs_0_, ...), custom_call_target="tpu_custom_call" | custom-call | flops 3000000000 | bytes 12582912 | tf_op jit(solution)/shard_map/ring/pallas_call | solution.py:451
  58.5 2.9 %collective-permute-start.8 = (f32[136,256]{1,0:T(8,128)}, f32[136,256]{1,0:T(8,128)S(1)}, u32[]{:S(2)}, u32[]{:S(2)}) collective-permute-start(f32[136,256]{1,0:T(8,128)} %get-tuple-element.48), channel_id=1, source_target_pairs={{0,1},{1,0},{2,3},{3,2},{4,5},{5,4},{6,7},{7,6},{8,9},{9,8},{10,11... | collective-permute-start | bytes 417800 | tf_op jit(solution)/shard_map/ppermute | solution.py:669
  61.5 2.0 %collective-permute-start.4 = (bf16[4,64,256]{2,1,0:T(8,128)(2,1)}, bf16[4,64,256]{2,1,0:T(8,128)(2,1)S(1)}, u32[]{:S(2)}, u32[]{:S(2)}) collective-permute-start(bf16[4,64,256]{2,1,0:T(8,128)(2,1)} %get-tuple-element.43), channel_id=1, source_target_pairs={{0,16},{1,17},{2,18},{3,19},{4,20},{5,21},{6,22},{7,23},{8,24},{9,... | collective-permute-start | bytes 393224 | tf_op jit(solution)/shard_map/ppermute | solution.py:663
  63.5 1.2 %collective-permute-start.5 = (bf16[4,64,256]{2,1,0:T(8,128)(2,1)}, bf16[4,64,256]{2,1,0:T(8,128)(2,1)S(1)}, u32[]{:S(2)}, u32[]{:S(2)}) collective-permute-start(bf16[4,64,256]{2,1,0:T(8,128)(2,1)} %get-tuple-element.44), channel_id=1, source_target_pairs={{0,112},{1,113},{2,114},{3,115},{4,116},{5,117},{6,118},{7,119},{8... | collective-permute-start | bytes 393224 | tf_op jit(solution)/shard_map/ppermute | solution.py:663
  64.7 0.6 collective-permute-start.6
  65.3 0.9 add.28
  66.4 4.4 %collective-permute-done.4.refs_5_ = bf16[4,64,256]{2,1,0:T(8,128)(2,1)S(1)} collective-permute-done((bf16[4,64,256]{2,1,0:T(8,128)(2,1)}, bf16[4,64,256]{2,1,0:T(8,128)(2,1)S(1)}, u32[]{:S(2)}, u32[]{:S(2)}) %collective-permute-start.4) | collective-permute-done | bytes 131104 | tf_op jit(solution)/shard_map/ppermute | solution.py:663
  70.7 1.5 %collective-permute-done.5.refs_6_ = bf16[4,64,256]{2,1,0:T(8,128)(2,1)S(1)} collective-permute-done((bf16[4,64,256]{2,1,0:T(8,128)(2,1)}, bf16[4,64,256]{2,1,0:T(8,128)(2,1)S(1)}, u32[]{:S(2)}, u32[]{:S(2)}) %collective-permute-start.5) | collective-permute-done | bytes 131104 | tf_op jit(solution)/shard_map/ppermute | solution.py:663
  72.2 0.6 copy-done.1
  72.9 3.7 %spread.6 = (bf16[4,64,64,256]{3,2,1,0:T(8,128)(2,1)}, f32[8,128]{1,0:T(8,128)}) custom-call(s32[17]{0:T(128)} %get-tuple-element.34.table.refs_0_, bf16[4,64,64,256]{3,2,1,0:T(8,128)(2,1)} %get-tuple-element.35.refs_1_.refs_2_.refs_3_, bf16[4,64,64,256]{3,2,1,0:T(8,128)(2,1)} %get-tuple-element.35.refs_1_.refs_2_.refs_3_, ...), custom_call_target="tpu_custom_call" | custom-call | flops 1500000000 | bytes 2097152 | tf_op jit(solution)/shard_map/spread/pallas_call | solution.py:630
  76.7 4.9 %spread.7 = (bf16[4,64,64,256]{3,2,1,0:T(8,128)(2,1)}, f32[8,128]{1,0:T(8,128)}) custom-call(s32[17]{0:T(128)} %get-tuple-element.34.table.refs_0_, bf16[4,64,64,256]{3,2,1,0:T(8,128)(2,1)} %get-tuple-element.35.refs_1_.refs_2_.refs_3_, bf16[4,64,64,256]{3,2,1,0:T(8,128)(2,1)} %get-tuple-element.35.refs_1_.refs_2_.refs_3_, ...), custom_call_target="tpu_custom_call", output_to_operand_aliasing={{0}: (10, {})} | custom-call | flops 2249999872 | bytes 3145728 | tf_op jit(solution)/shard_map/spread/pallas_call | solution.py:630
  81.8 0.6 collective-permute-start.11
  82.4 3.6 %spread.8 = (bf16[4,64,64,256]{3,2,1,0:T(8,128)(2,1)}, f32[8,128]{1,0:T(8,128)}) custom-call(s32[17]{0:T(128)} %get-tuple-element.34.table.refs_0_, bf16[4,64,64,256]{3,2,1,0:T(8,128)(2,1)} %get-tuple-element.35.refs_1_.refs_2_.refs_3_, bf16[4,64,64,256]{3,2,1,0:T(8,128)(2,1)} %get-tuple-element.35.refs_1_.refs_2_.refs_3_, ...), custom_call_target="tpu_custom_call", output_to_operand_aliasing={{0}: (10, {})} | custom-call | flops 1500000000 | bytes 2097152 | tf_op jit(solution)/shard_map/spread/pallas_call | solution.py:630
  86.1 2.8 %collective-permute-start.12 = (f32[136,256]{1,0:T(8,128)S(1)}, f32[136,256]{1,0:T(8,128)S(1)}, u32[]{:S(2)}, u32[]{:S(2)}) collective-permute-start(f32[136,256]{1,0:T(8,128)S(1)} %add.31), channel_id=1, source_target_pairs={{0,24},{1,25},{2,26},{3,27},{4,28},{5,29},{6,30},{7,31},{8,16},{9,... | collective-permute-start | bytes 417800 | tf_op jit(solution)/shard_map/ppermute | solution.py:669
  88.9 4.8 %spread.9 = (bf16[4,64,64,256]{3,2,1,0:T(8,128)(2,1)}, f32[8,128]{1,0:T(8,128)}) custom-call(s32[17]{0:T(128)} %get-tuple-element.34.table.refs_0_, bf16[4,64,64,256]{3,2,1,0:T(8,128)(2,1)} %get-tuple-element.35.refs_1_.refs_2_.refs_3_, bf16[4,64,64,256]{3,2,1,0:T(8,128)(2,1)} %get-tuple-element.35.refs_1_.refs_2_.refs_3_, ...), custom_call_target="tpu_custom_call", output_to_operand_aliasing={{0}: (10, {})} | custom-call | flops 2249999872 | bytes 3145728 | tf_op jit(solution)/shard_map/spread/pallas_call | solution.py:630
  93.7 1.3 %collective-permute-start.13 = (f32[136,256]{1,0:T(8,128)S(1)}, f32[136,256]{1,0:T(8,128)S(1)}, u32[]{:S(2)}, u32[]{:S(2)}) collective-permute-start(f32[136,256]{1,0:T(8,128)S(1)} %add.32), channel_id=1, source_target_pairs={{0,32},{1,33},{2,34},{3,35},{4,36},{5,37},{6,38},{7,39},{8,40},{9,... | collective-permute-start | bytes 417800 | tf_op jit(solution)/shard_map/ppermute | solution.py:669
  95.0 3.6 %spread.10 = (bf16[4,64,64,256]{3,2,1,0:T(8,128)(2,1)}, f32[8,128]{1,0:T(8,128)}) custom-call(s32[17]{0:T(128)} %get-tuple-element.34.table.refs_0_, bf16[4,64,64,256]{3,2,1,0:T(8,128)(2,1)} %get-tuple-element.35.refs_1_.refs_2_.refs_3_, bf16[4,64,64,256]{3,2,1,0:T(8,128)(2,1)} %get-tuple-element.35.refs_1_.refs_2_.refs_3_, ...), custom_call_target="tpu_custom_call", output_to_operand_aliasing={{0}: (10, {})} | custom-call | flops 1500000000 | bytes 2097152 | tf_op jit(solution)/shard_map/spread/pallas_call | solution.py:630
  98.7 1.6 %collective-permute-start.14 = (f32[136,256]{1,0:T(8,128)S(1)}, f32[136,256]{1,0:T(8,128)S(1)}, u32[]{:S(2)}, u32[]{:S(2)}) collective-permute-start(f32[136,256]{1,0:T(8,128)S(1)} %add.33), channel_id=1, source_target_pairs={{0,96},{1,97},{2,98},{3,99},{4,100},{5,101},{6,102},{7,103},{8,104... | collective-permute-start | bytes 417800 | tf_op jit(solution)/shard_map/ppermute | solution.py:669
  100.3 2.9 %collective-permute-start.15 = (f32[136,256]{1,0:T(8,128)S(1)}, f32[136,256]{1,0:T(8,128)S(1)}, u32[]{:S(2)}, u32[]{:S(2)}) collective-permute-start(f32[136,256]{1,0:T(8,128)S(1)} %add.33), channel_id=1, source_target_pairs={{0,1},{1,0},{2,3},{3,2},{4,5},{5,4},{6,7},{7,6},{8,9},{9,8},{10,11... | collective-permute-start | bytes 417800 | tf_op jit(solution)/shard_map/ppermute | solution.py:669
  103.2 1.9 %collective-permute-start.16 = (f32[136,256]{1,0:T(8,128)S(1)}, f32[136,256]{1,0:T(8,128)S(1)}, u32[]{:S(2)}, u32[]{:S(2)}) collective-permute-start(f32[136,256]{1,0:T(8,128)S(1)} %add.33), channel_id=1, source_target_pairs={{0,97},{1,96},{2,99},{3,98},{4,101},{5,100},{6,103},{7,102},{8,105... | collective-permute-start | bytes 417800 | tf_op jit(solution)/shard_map/ppermute | solution.py:669
  105.1 5.8 %spread.11 = (bf16[4,64,64,256]{3,2,1,0:T(8,128)(2,1)}, f32[8,128]{1,0:T(8,128)}) custom-call(s32[17]{0:T(128)} %get-tuple-element.34.table.refs_0_, bf16[4,64,64,256]{3,2,1,0:T(8,128)(2,1)} %get-tuple-element.35.refs_1_.refs_2_.refs_3_, bf16[4,64,64,256]{3,2,1,0:T(8,128)(2,1)} %get-tuple-element.35.refs_1_.refs_2_.refs_3_, ...), custom_call_target="tpu_custom_call", output_to_operand_aliasing={{0}: (10, {})} | custom-call | flops 3000000000 | bytes 4194304 | tf_op jit(solution)/shard_map/spread/pallas_call | solution.py:630
  110.9 0.6 slice.12
  111.6 0.6 slice.13
  112.1 0.7 pad_maximum_fusion
  (39 shorter events, 0.9 us)
Async XLA Ops:
  4.1 46.5 %collective-permute-start = (bf16[4,64,256]{2,1,0:T(8,128)(2,1)}, bf16[4,64,256]{2,1,0:T(8,128)(2,1)S(1)}, u32[]{:S(2)}, u32[]{:S(2)}) collective-permute-start(bf16[4,64,256]{2,1,0:T(8,128)(2,1)} %get-tuple-element.36), channel_id=1, source_target_pairs={{0,16},{1,17},{2,18},{3,19},{4,20},{5,21},{6,22},{7,23},{8,24},{9,... | collective-permute-start | bytes 393224 | tf_op jit(solution)/shard_map/ppermute | solution.py:663
  8.6 42.0 %collective-permute-start.1 = (bf16[4,64,256]{2,1,0:T(8,128)(2,1)}, bf16[4,64,256]{2,1,0:T(8,128)(2,1)S(1)}, u32[]{:S(2)}, u32[]{:S(2)}) collective-permute-start(bf16[4,64,256]{2,1,0:T(8,128)(2,1)} %get-tuple-element.37), channel_id=1, source_target_pairs={{0,112},{1,113},{2,114},{3,115},{4,116},{5,117},{6,118},{7,119},{8... | collective-permute-start | bytes 393224 | tf_op jit(solution)/shard_map/ppermute | solution.py:663
  10.9 39.7 %collective-permute-start.2 = (bf16[4,64,256]{2,1,0:T(8,128)(2,1)}, bf16[4,64,256]{2,1,0:T(8,128)(2,1)S(1)}, u32[]{:S(2)}, u32[]{:S(2)}) collective-permute-start(bf16[4,64,256]{2,1,0:T(8,128)(2,1)} %get-tuple-element.38), channel_id=1, source_target_pairs={{0,1},{1,0},{2,3},{3,2},{4,5},{5,4},{6,7},{7,6},{8,9},{9,8},{10,11... | collective-permute-start | bytes 393224 | tf_op jit(solution)/shard_map/ppermute | solution.py:663
  11.8 38.8 %collective-permute-start.3 = (bf16[4,64,256]{2,1,0:T(8,128)(2,1)}, bf16[4,64,256]{2,1,0:T(8,128)(2,1)S(1)}, u32[]{:S(2)}, u32[]{:S(2)}) collective-permute-start(bf16[4,64,256]{2,1,0:T(8,128)(2,1)} %get-tuple-element.39), channel_id=1, source_target_pairs={{0,15},{1,2},{2,1},{3,4},{4,3},{5,6},{6,5},{7,8},{8,7},{9,10},{10,... | collective-permute-start | bytes 393224 | tf_op jit(solution)/shard_map/ppermute | solution.py:663
  50.5 0.6 copy-start.4
  50.6 0.7 copy-start.5
  50.6 0.7 copy-start.6
  50.6 0.8 copy-start.7
  58.5 6.8 %collective-permute-start.8 = (f32[136,256]{1,0:T(8,128)}, f32[136,256]{1,0:T(8,128)S(1)}, u32[]{:S(2)}, u32[]{:S(2)}) collective-permute-start(f32[136,256]{1,0:T(8,128)} %get-tuple-element.48), channel_id=1, source_target_pairs={{0,1},{1,0},{2,3},{3,2},{4,5},{5,4},{6,7},{7,6},{8,9},{9,8},{10,11... | collective-permute-start | bytes 417800 | tf_op jit(solution)/shard_map/ppermute | solution.py:669
  61.5 9.3 %collective-permute-start.4 = (bf16[4,64,256]{2,1,0:T(8,128)(2,1)}, bf16[4,64,256]{2,1,0:T(8,128)(2,1)S(1)}, u32[]{:S(2)}, u32[]{:S(2)}) collective-permute-start(bf16[4,64,256]{2,1,0:T(8,128)(2,1)} %get-tuple-element.43), channel_id=1, source_target_pairs={{0,16},{1,17},{2,18},{3,19},{4,20},{5,21},{6,22},{7,23},{8,24},{9,... | collective-permute-start | bytes 393224 | tf_op jit(solution)/shard_map/ppermute | solution.py:663
  63.5 8.7 %collective-permute-start.5 = (bf16[4,64,256]{2,1,0:T(8,128)(2,1)}, bf16[4,64,256]{2,1,0:T(8,128)(2,1)S(1)}, u32[]{:S(2)}, u32[]{:S(2)}) collective-permute-start(bf16[4,64,256]{2,1,0:T(8,128)(2,1)} %get-tuple-element.44), channel_id=1, source_target_pairs={{0,112},{1,113},{2,114},{3,115},{4,116},{5,117},{6,118},{7,119},{8... | collective-permute-start | bytes 393224 | tf_op jit(solution)/shard_map/ppermute | solution.py:663
  64.7 7.5 %collective-permute-start.6 = (bf16[4,64,256]{2,1,0:T(8,128)(2,1)}, bf16[4,64,256]{2,1,0:T(8,128)(2,1)S(1)}, u32[]{:S(2)}, u32[]{:S(2)}) collective-permute-start(bf16[4,64,256]{2,1,0:T(8,128)(2,1)} %get-tuple-element.45), channel_id=1, source_target_pairs={{0,1},{1,0},{2,3},{3,2},{4,5},{5,4},{6,7},{7,6},{8,9},{9,8},{10,11... | collective-permute-start | bytes 393224 | tf_op jit(solution)/shard_map/ppermute | solution.py:663
  65.3 6.9 %collective-permute-start.7 = (bf16[4,64,256]{2,1,0:T(8,128)(2,1)}, bf16[4,64,256]{2,1,0:T(8,128)(2,1)S(1)}, u32[]{:S(2)}, u32[]{:S(2)}) collective-permute-start(bf16[4,64,256]{2,1,0:T(8,128)(2,1)} %get-tuple-element.46), channel_id=1, source_target_pairs={{0,15},{1,2},{2,1},{3,4},{4,3},{5,6},{6,5},{7,8},{8,7},{9,10},{10,... | collective-permute-start | bytes 393224 | tf_op jit(solution)/shard_map/ppermute | solution.py:663
  66.3 10.3 %collective-permute-start.9 = (f32[136,256]{1,0:T(8,128)S(1)}, f32[136,256]{1,0:T(8,128)S(1)}, u32[]{:S(2)}, u32[]{:S(2)}) collective-permute-start(f32[136,256]{1,0:T(8,128)S(1)} %add.28), channel_id=1, source_target_pairs={{0,2},{1,3},{2,0},{3,1},{4,6},{5,7},{6,4},{7,5},{8,10},{9,11},{10,... | collective-permute-start | bytes 417800 | tf_op jit(solution)/shard_map/ppermute | solution.py:669
  70.7 1.5 %copy-start = (bf16[4,64,256]{2,1,0:T(8,128)(2,1)}, bf16[4,64,256]{2,1,0:T(8,128)(2,1)S(1)}, u32[]{:S(2)}) copy-start(bf16[4,64,256]{2,1,0:T(8,128)(2,1)S(1)} %collective-permute-done.4.refs_5_) | copy-start | bytes 393220
  72.2 0.7 copy-start.1
  72.2 0.7 copy-start.2
  72.2 0.7 copy-start.3
  76.6 5.2 %collective-permute-start.10 = (f32[136,256]{1,0:T(8,128)S(1)}, f32[136,256]{1,0:T(8,128)S(1)}, u32[]{:S(2)}, u32[]{:S(2)}) collective-permute-start(f32[136,256]{1,0:T(8,128)S(1)} %add.29), channel_id=1, source_target_pairs={{0,6},{1,7},{2,4},{3,5},{4,2},{5,3},{6,0},{7,1},{8,14},{9,15},{10,... | collective-permute-start | bytes 417800 | tf_op jit(solution)/shard_map/ppermute | solution.py:669
  81.8 4.2 %collective-permute-start.11 = (f32[136,256]{1,0:T(8,128)S(1)}, f32[136,256]{1,0:T(8,128)S(1)}, u32[]{:S(2)}, u32[]{:S(2)}) collective-permute-start(f32[136,256]{1,0:T(8,128)S(1)} %add.30), channel_id=1, source_target_pairs={{0,8},{1,9},{2,10},{3,11},{4,12},{5,13},{6,14},{7,15},{8,0},{9,1},... | collective-permute-start | bytes 417800 | tf_op jit(solution)/shard_map/ppermute | solution.py:669
  86.1 7.6 %collective-permute-start.12 = (f32[136,256]{1,0:T(8,128)S(1)}, f32[136,256]{1,0:T(8,128)S(1)}, u32[]{:S(2)}, u32[]{:S(2)}) collective-permute-start(f32[136,256]{1,0:T(8,128)S(1)} %add.31), channel_id=1, source_target_pairs={{0,24},{1,25},{2,26},{3,27},{4,28},{5,29},{6,30},{7,31},{8,16},{9,... | collective-permute-start | bytes 417800 | tf_op jit(solution)/shard_map/ppermute | solution.py:669
  93.7 4.9 %collective-permute-start.13 = (f32[136,256]{1,0:T(8,128)S(1)}, f32[136,256]{1,0:T(8,128)S(1)}, u32[]{:S(2)}, u32[]{:S(2)}) collective-permute-start(f32[136,256]{1,0:T(8,128)S(1)} %add.32), channel_id=1, source_target_pairs={{0,32},{1,33},{2,34},{3,35},{4,36},{5,37},{6,38},{7,39},{8,40},{9,... | collective-permute-start | bytes 417800 | tf_op jit(solution)/shard_map/ppermute | solution.py:669
  98.7 12.2 %collective-permute-start.14 = (f32[136,256]{1,0:T(8,128)S(1)}, f32[136,256]{1,0:T(8,128)S(1)}, u32[]{:S(2)}, u32[]{:S(2)}) collective-permute-start(f32[136,256]{1,0:T(8,128)S(1)} %add.33), channel_id=1, source_target_pairs={{0,96},{1,97},{2,98},{3,99},{4,100},{5,101},{6,102},{7,103},{8,104... | collective-permute-start | bytes 417800 | tf_op jit(solution)/shard_map/ppermute | solution.py:669
  100.3 10.5 %collective-permute-start.15 = (f32[136,256]{1,0:T(8,128)S(1)}, f32[136,256]{1,0:T(8,128)S(1)}, u32[]{:S(2)}, u32[]{:S(2)}) collective-permute-start(f32[136,256]{1,0:T(8,128)S(1)} %add.33), channel_id=1, source_target_pairs={{0,1},{1,0},{2,3},{3,2},{4,5},{5,4},{6,7},{7,6},{8,9},{9,8},{10,11... | collective-permute-start | bytes 417800 | tf_op jit(solution)/shard_map/ppermute | solution.py:669
  103.2 7.7 %collective-permute-start.16 = (f32[136,256]{1,0:T(8,128)S(1)}, f32[136,256]{1,0:T(8,128)S(1)}, u32[]{:S(2)}, u32[]{:S(2)}) collective-permute-start(f32[136,256]{1,0:T(8,128)S(1)} %add.33), channel_id=1, source_target_pairs={{0,97},{1,96},{2,99},{3,98},{4,101},{5,100},{6,103},{7,102},{8,105... | collective-permute-start | bytes 417800 | tf_op jit(solution)/shard_map/ppermute | solution.py:669
